TPU v7x, 32 devices: a whole 2x2x4 slice. The times are simulated.
32 devices in a mesh: bag: 4 (over y, x), seq: 8 (over z, core).
Axes of the slice: x: 2, y: 2, z: 4, core: 2. Of those that a mesh axis runs over, the one named last changes fastest.
Arguments:
- text_rows: bfloat16 [2048, 3072], P(('bag', 'seq')), may hold values from -6 to 6
- image_rows: bfloat16 [1024, 3072], P(('bag', 'seq')), may hold values from -6 to 6
- modulation: float32 [32, 2, 2, 3072], P('bag'), may hold values from -3 to 3
- head_weight: bfloat16 [2, 3072, 6144], P(None, None, 'seq'), may hold values from -0.109375 to 0.109375
- norm_gain: float32 [2, 2, 128], replicated, may hold values from 0.5 to 20
- store_down: bfloat16 [128, 2, 64, 3072], P('bag', None, 'seq'), may hold values from -0.109375 to 0.109375
- store_up: bfloat16 [128, 2, 64, 6144], P('bag', None, None, 'seq'), may hold values from -0.375 to 0.375
- store_row: int32 [128], replicated, may hold values from 0 to 127, as said below
- user_adapter: int32 [4, 4], replicated, may hold values from 0 to 127, as said below
- image_lengths: int32 [4, 4], P('bag'), may hold values from 1 to 64, 128 in all within a row
Outputs:
- text_out: bfloat16 [2048, 2048], P(('bag', 'seq'))
- image_out: bfloat16 [1024, 2048], P(('bag', 'seq'))
Inputs may be any that keep to these rules, and one draw needn't show every extreme that they name: A permutation: adapter a is kept at row store_row[a] of store_down and store_up, whose owner is store_row[a] // 32. `user_adapter`: the 4 users of one bag have adapters kept by 4 different owners, so every owner keeps exactly one adapter of each bag.
All inputs are finite; a program needn't handle non-finite values.
Results may differ from a plain program's by a relative error of at most 0.04.
The roundings to bfloat16 on the way count: a program that leaves them out, or rounds other values in their place, can miss the bound.
Values may be sent and summed in bfloat16 or wider, within the bound.
No kernel may reach another device: no remote copies, remote signals or barrier semaphores. Data moves between devices by JAX's collectives and lax.ppermute only.
A program may use at most 128 MiB of HBM per device.

v0:
```python
import math

import jax
import jax.numpy as jnp
from jax import lax
from jax.sharding import PartitionSpec as P

HEAD_DIM = 128
TEXT = 64


def modulate(raw_rows, shifts, scales):
    values = raw_rows.astype(jnp.float32)
    centre = values - jnp.mean(values, axis=-1, keepdims=True)
    spread = jnp.mean(centre * centre, axis=-1, keepdims=True)
    normed = centre * lax.rsqrt(spread + 1e-06)
    return ((1.0 + scales) * normed + shifts).astype(jnp.bfloat16)


def head_normed(values, gain_row):
    spread = jnp.mean(values * values, axis=-1, keepdims=True)
    return (values * lax.rsqrt(spread + 1e-06) * gain_row).astype(jnp.bfloat16)


def attend(queries, keys_all, values_all, seg_ids):
    row_total = queries.shape[0]
    block_rows = math.gcd(row_total, 1024)
    query_blocks = queries.reshape(row_total // block_rows, block_rows, queries.shape[1])
    seg_blocks = seg_ids.reshape(row_total // block_rows, block_rows)
    factor = 1.0 / math.sqrt(queries.shape[1])

    def one_block(block_pair):
        query_rows, query_segs = block_pair
        scores = jnp.dot(query_rows, keys_all.T, preferred_element_type=jnp.float32) * factor
        scores = jnp.where(query_segs[:, None] == seg_ids[None, :], scores, -1e30)
        top_score = jnp.max(scores, axis=1, keepdims=True)
        weights = jnp.exp(scores - top_score)
        prob_rows = (weights / jnp.sum(weights, axis=1, keepdims=True)).astype(jnp.bfloat16)
        return jnp.dot(prob_rows, values_all, preferred_element_type=jnp.float32).astype(
            jnp.bfloat16
        )

    return lax.map(one_block, (query_blocks, seg_blocks)).reshape(row_total, values_all.shape[1])


def user_table(user_ids, user_count):
    return user_ids[:, None] == jnp.arange(user_count, dtype=jnp.int32)[None, :]


def pick_rows(seg_pick, table_rows):
    return jnp.dot(seg_pick, table_rows, precision=lax.Precision.HIGHEST)


def part_ranks(hidden_all, down_part, user_ids, user_count):
    all_users = jnp.einsum("nd,urd->urn", hidden_all, down_part, preferred_element_type=jnp.float32)
    user_pick = user_table(user_ids, user_count).astype(jnp.float32).T
    return jnp.sum(all_users * user_pick[:, None, :], axis=0).astype(jnp.bfloat16)


def adapted(hidden_all, weight, ranks, up_users, user_ids, gain_pair):
    row_count = hidden_all.shape[0]
    user_count = up_users.shape[0]
    plain_part = jnp.dot(hidden_all, weight, preferred_element_type=jnp.float32)
    user_pick = user_table(user_ids, user_count).astype(jnp.bfloat16)
    spread_ranks = (user_pick[:, :, None] * ranks[:, None, :]).reshape(row_count, -1)
    adjust = jnp.dot(
        spread_ranks, up_users.reshape(-1, weight.shape[1]), preferred_element_type=jnp.float32
    )
    heads_here = weight.shape[1] // (3 * HEAD_DIM)
    mixed_cols = (plain_part + adjust).reshape(row_count, heads_here, 3, HEAD_DIM)
    query = head_normed(mixed_cols[:, :, 0], gain_pair[0])
    key_rows = head_normed(mixed_cols[:, :, 1], gain_pair[1])
    value_rows = mixed_cols[:, :, 2].astype(jnp.bfloat16)
    return (query, key_rows, value_rows)


def body(
    text_rows,
    image_rows,
    modulation,
    head_weight,
    norm_gain,
    store_down,
    store_up,
    store_row,
    user_adapter,
    image_lengths,
):
    seq_count = lax.axis_size("seq")
    bag_index = lax.axis_index("bag")
    seq_index = lax.axis_index("seq")
    text_dev = text_rows.shape[0]
    image_dev = image_rows.shape[0]
    text_bag = text_dev * seq_count
    image_bag = image_dev * seq_count
    user_count = image_lengths.shape[1]
    seg_count = modulation.shape[0]
    store_size = store_down.shape[0]
    seg_ends = jnp.cumsum(jnp.repeat(image_lengths[0], 2))
    text_segs = jnp.arange(text_bag, dtype=jnp.int32) // TEXT
    image_segs = jnp.sum(
        (jnp.arange(image_bag, dtype=jnp.int32)[:, None] >= seg_ends[None, :]).astype(jnp.int32),
        axis=1,
    )
    seg_range = jnp.arange(seg_count, dtype=jnp.int32)
    text_local = lax.dynamic_slice_in_dim(text_segs, seq_index * text_dev, text_dev)
    image_local = lax.dynamic_slice_in_dim(image_segs, seq_index * image_dev, image_dev)
    text_pick = (text_local[:, None] == seg_range[None, :]).astype(jnp.float32)
    image_pick = (image_local[:, None] == seg_range[None, :]).astype(jnp.float32)
    text_hidden = modulate(
        text_rows,
        pick_rows(text_pick, modulation[:, 0, 0]),
        pick_rows(text_pick, modulation[:, 0, 1]),
    )
    image_hidden = modulate(
        image_rows,
        pick_rows(image_pick, modulation[:, 1, 0]),
        pick_rows(image_pick, modulation[:, 1, 1]),
    )
    store_rows = jnp.take(store_row, user_adapter, axis=0)
    owners = store_rows // store_size
    owner_match = owners == bag_index
    sending = jnp.any(owner_match, axis=1)
    slot_index = jnp.sum(jnp.where(owner_match, store_rows % store_size, 0), axis=1)
    down_send = jnp.where(
        sending[:, None, None, None],
        jnp.take(store_down, slot_index, axis=0),
        jnp.zeros((), jnp.bfloat16),
    )
    up_send = jnp.where(
        sending[:, None, None, None],
        jnp.take(store_up, slot_index, axis=0),
        jnp.zeros((), jnp.bfloat16),
    )
    down_recv, up_recv = (
        lax.all_to_all(down_send, "bag", split_axis=0, concat_axis=0, tiled=True),
        lax.all_to_all(up_send, "bag", split_axis=0, concat_axis=0, tiled=True),
    )
    my_owners = lax.dynamic_index_in_dim(owners, bag_index, 0, keepdims=False)
    down_users = jnp.take(down_recv, my_owners, axis=0)
    up_users = jnp.take(up_recv, my_owners, axis=0)
    text_all, image_all = (
        lax.all_gather(text_hidden, "seq", axis=0, tiled=True),
        lax.all_gather(image_hidden, "seq", axis=0, tiled=True),
    )
    text_part = part_ranks(text_all, down_users[:, 0], text_segs // 2, user_count)
    image_part = part_ranks(image_all, down_users[:, 1], image_segs // 2, user_count)
    text_cols, image_cols = (
        lax.all_gather(text_part, "seq", axis=0, tiled=True),
        lax.all_gather(image_part, "seq", axis=0, tiled=True),
    )
    text_rank_all = text_cols.T
    image_rank_all = image_cols.T
    text_parts = adapted(
        text_all, head_weight[0], text_rank_all, up_users[:, 0], text_segs // 2, norm_gain[0]
    )
    image_parts = adapted(
        image_all, head_weight[1], image_rank_all, up_users[:, 1], image_segs // 2, norm_gain[1]
    )
    joined = [
        jnp.transpose(jnp.concatenate([text_parts[which], image_parts[which]], axis=0), (1, 0, 2))
        for which in range(3)
    ]
    seg_all = jnp.concatenate([text_segs, image_segs], axis=0)

    def one_head(head_rows):
        return attend(head_rows[0], head_rows[1], head_rows[2], seg_all)

    outputs = lax.map(one_head, (joined[0], joined[1], joined[2]))
    heads_here = outputs.shape[0]
    outputs = jnp.transpose(outputs, (1, 0, 2)).reshape(text_bag + image_bag, heads_here * HEAD_DIM)
    text_out, image_out = (
        lax.all_to_all(outputs[:text_bag], "seq", split_axis=0, concat_axis=1, tiled=True),
        lax.all_to_all(outputs[text_bag:], "seq", split_axis=0, concat_axis=1, tiled=True),
    )
    return (text_out, image_out)


def solution(mesh):
    in_specs = (
        P(("bag", "seq"), None),
        P(("bag", "seq"), None),
        P("bag", None, None, None),
        P(None, None, "seq"),
        P(),
        P("bag", None, "seq", None),
        P("bag", None, None, "seq"),
        P(),
        P(),
        P("bag", None),
    )
    out_specs = (P(("bag", "seq"), None), P(("bag", "seq"), None))
    return jax.shard_map(body, mesh=mesh, in_specs=in_specs, out_specs=out_specs, check_vma=False)
```

profile of v0, /device:TPU:0, one launch (start us, length us, event | category | flops | bytes accessed | tf_op | source)
XLA Modules:
  0.0 189.1 jit_solution(12241190175673804232)
XLA Ops:
  10.7 2.2 %fusion.64 = (f32[8,1,1,3072]{3,2,1,0:T(1,128)}, f32[8,1,1,3072]{3,2,1,0:T(1,128)S(1)}, f32[8,1,1,3072]{3,2,1,0:T(1,128)}, f32[8,1,1,3072]{3,2,1,0:T(1,128)}) fusion(f32[8,2,2,3072]{3,2,1,0:T(2,128)} %param.16), kind=kLoop, calls=%fused_computation.163 | loop fusion | bytes 786432 | tf_op jit(solution)/shard_map/slice | solution.py:112
  14.4 2.0 %fusion.16 = bf16[32,3072]{1,0:T(8,128)(2,1)} fusion(f32[32,3072]{1,0:T(8,128)S(1)} %fusion.15, f32[8,1,1,3072]{3,2,1,0:T(1,128)} %get-tuple-element.146, s32[32]{0:T(128)S(1)} %dynamic_slice.30), kind=kOutput, calls=%fused_computation.34 | convolution fusion | flops 9634048 | bytes 688256 | tf_op jit(solution)/shard_map/dot_general | solution.py:51
  24.4 5.2 %all-to-all-start = ((bf16[4,2,8,3072]{3,2,1,0:T(8,128)(2,1)}), bf16[4,2,8,3072]{3,2,1,0:T(8,128)(2,1)}, u32[]{:S(2)}, u32[]{:S(2)}) async-start(bf16[4,2,8,3072]{3,2,1,0:T(8,128)(2,1)} %copy.93), calls=%async_computation | async-start | bytes 786432 | tf_op jit(solution)/shard_map/all_to_all | solution.py:136
  30.1 1.5 fusion.13
  31.6 2.2 %fusion.14 = bf16[64,3072]{1,0:T(8,128)(2,1)} fusion(f32[64,3072]{1,0:T(8,128)S(1)} %fusion.13, f32[8,1,1,3072]{3,2,1,0:T(1,128)} %get-tuple-element.143, s32[64]{0:T(128)S(1)} %dynamic_slice.28), kind=kOutput, calls=%fused_computation.30 | convolution fusion | flops 19268096 | bytes 1278208 | tf_op jit(solution)/shard_map/dot_general | solution.py:51
  38.4 4.5 %gather_fusion.3 = bf16[4,2,64,768]{3,2,1,0:T(8,128)(2,1)} fusion(bf16[32,2,64,768]{3,2,1,0:T(8,128)(2,1)} %param.20, s32[1024]{0:T(1024)} %copy-done.13), kind=kCustom, calls=%fused_computation.3 | custom fusion | bytes 1572880 | tf_op jit(solution)/shard_map/jit(_take)/gather | solution.py:132
  42.9 2.2 %select_select_fusion = bf16[4,2,64,768]{3,2,1,0:T(8,128)(2,1)} fusion(bf16[4,2,64,768]{3,2,1,0:T(8,128)(2,1)} %gather_fusion.3, pred[4]{0:T(512)(128)(4,1)S(1)} %copy-done.19, pred[4]{0:T(512)(128)(4,1)} %copy-done.15), kind=kLoop, calls=%fused_computation.50 | loop fusion | flops 786432 | bytes 1572872 | tf_op jit(solution)/shard_map/jit(_where)/select_n | solution.py:130
  45.1 4.2 %all-to-all-start.1 = ((bf16[4,2,64,768]{3,2,1,0:T(8,128)(2,1)}), bf16[4,2,64,768]{3,2,1,0:T(8,128)(2,1)}, u32[]{:S(2)}, u32[]{:S(2)}) async-start(bf16[4,2,64,768]{3,2,1,0:T(8,128)(2,1)} %select_select_fusion), calls=%async_computation.1 | async-start | bytes 1572864 | tf_op jit(solution)/shard_map/all_to_all | solution.py:137
  49.3 2.3 %gather_fusion.2 = bf16[4,2,8,3072]{3,2,1,0:T(8,128)(2,1)} fusion(bf16[4,2,8,3072]{3,2,1,0:T(8,128)(2,1)} %all-to-all-done, s32[1024]{0:T(1024)S(1)} %pad_clamp_fusion), kind=kCustom, calls=%fused_computation.2 | custom fusion | bytes 786448 | tf_op jit(solution)/shard_map/jit(_take)/gather | solution.py:140
  52.7 8.0 %all-to-all-done.1 = bf16[4,2,64,768]{3,2,1,0:T(8,128)(2,1)} async-done(((bf16[4,2,64,768]{3,2,1,0:T(8,128)(2,1)}), bf16[4,2,64,768]{3,2,1,0:T(8,128)(2,1)}, u32[]{:S(2)}, u32[]{:S(2)}) %all-to-all-start.1) | async-done | bytes 786464 | tf_op jit(solution)/shard_map/all_to_all | solution.py:137
  60.7 2.8 %gather_fusion.4 = bf16[4,2,64,768]{3,2,1,0:T(8,128)(2,1)} fusion(bf16[4,2,64,768]{3,2,1,0:T(8,128)(2,1)} %all-to-all-done.1, s32[1024]{0:T(1024)} %copy-done.14), kind=kCustom, calls=%fused_computation.4 | custom fusion | bytes 1572880 | tf_op jit(solution)/shard_map/jit(_take)/gather | solution.py:141
  65.7 2.0 %fusion.30 = bf16[8,256]{1,0:T(8,128)(2,1)S(1)} fusion(bf16[256,3072]{1,0:T(8,128)(2,1)} %all-gather.5.cloned.1.call-done, bf16[4,2,8,3072]{3,2,0,1:T(8,128)(2,1)S(1)} %copy_select_fusion, f32[4,256]{1,0:T(4,128)S(1)} %fusion.49), kind=kOutput, calls=%fused_computation.44 | convolution fusion | flops 50345984 | bytes 1777664 | tf_op jit(solution)/shard_map/nd,urd->urn/dot_general | solution.py:55
  67.7 14.8 %all_gather.15 = bf16[64,256]{1,0:T(8,128)(2,1)S(1)} all-gather(bf16[8,256]{1,0:T(8,128)(2,1)S(1)} %fusion.30), channel_id=1, replica_groups=mesh['bag'=4,'seq'=8] {'seq'}, dimensions={0}, use_global_device_ids=true | all-gather | bytes 36864 | tf_op jit(solution)/shard_map/all_gather | solution.py:150
  83.2 4.2 %fusion.7 = f32[256,768]{1,0:T(8,128)S(1)} fusion(bf16[256,3072]{1,0:T(8,128)(2,1)} %all-gather.5.cloned.1.call-done, bf16[2,3072,768]{2,1,0:T(8,128)(2,1)} %param.17), kind=kOutput, calls=%fused_computation.21 | convolution fusion | flops 1207959552 | bytes 7077888 | tf_op jit(solution)/shard_map/dot_general | solution.py:63
  88.6 2.3 %copy.98 = f32[256,768]{0,1:T(8,128)} copy(f32[256,768]{1,0:T(8,128)} %convolution_add_fusion.5) | data formatting | bytes 1572864 | tf_op jit(solution)/shard_map/add | solution.py:70
  92.1 1.6 fusion.41
  93.7 1.5 multiply_convert_fusion.2
  95.2 3.1 %fusion.24 = bf16[8,512]{1,0:T(8,128)(2,1)S(1)} fusion(bf16[512,3072]{1,0:T(8,128)(2,1)} %all-gather.3.cloned.1.call-done, bf16[4,2,8,3072]{3,2,0,1:T(8,128)(2,1)S(1)} %copy_select_fusion, f32[4,512]{1,0:T(4,128)S(1)} %fusion.47), kind=kOutput, calls=%fused_computation.42 | convolution fusion | flops 100691968 | bytes 3358720 | tf_op jit(solution)/shard_map/nd,urd->urn/dot_general | solution.py:55
  98.3 14.2 %all_gather.13 = bf16[64,512]{1,0:T(8,128)(2,1)S(1)} all-gather(bf16[8,512]{1,0:T(8,128)(2,1)S(1)} %fusion.24), channel_id=1, replica_groups=mesh['bag'=4,'seq'=8] {'seq'}, dimensions={0}, use_global_device_ids=true | all-gather | bytes 73728 | tf_op jit(solution)/shard_map/all_gather | solution.py:149
  112.5 5.0 %fusion.9 = f32[512,768]{1,0:T(8,128)S(1)} fusion(bf16[512,3072]{1,0:T(8,128)(2,1)S(1)} %copy-done.3, bf16[2,3072,768]{2,1,0:T(8,128)(2,1)} %param.17), kind=kOutput, calls=%fused_computation.23 | convolution fusion | flops 2415919104 | bytes 9437184 | tf_op jit(solution)/shard_map/dot_general | solution.py:63
  117.6 1.6 convolution_add_fusion.4
  119.1 3.1 %copy.95 = f32[512,768]{0,1:T(8,128)} copy(f32[512,768]{1,0:T(8,128)} %convolution_add_fusion.4) | data formatting | bytes 3145728 | tf_op jit(solution)/shard_map/add | solution.py:70
  122.2 1.4 multiply_reduce_fusion
  128.4 26.8 %while.23 = (s32[]{:T(128)}, bf16[2,768,128]{2,1,0:T(8,128)(2,1)}, bf16[2,768,128]{1,2,0:T(8,128)(2,1)}, s32[768]{0:T(1024)S(1)}, bf16[2,768,128]{1,2,0:T(8,128)...) while((s32[]{:T(128)}, bf16[2,768,128]{2,1,0:T(8,128)(2,1)}, ...), condition=%wide.wide.region_19.20_spmd, body=%wide.wide.region_14.19_spmd.sunk | while | flops 102465024 | bytes 5647666 | solution.py:169
  132.2 8.0 %while.24 = (s32[]{:T(128)}, bf16[3,256,128]{2,1,0:T(8,128)(2,1)}, s32[3,256]{1,0:T(4,128)S(1)}, s32[768]{0:T(1024)S(1)}, bf16[3,256,128]{2,1,0:T(8,128)(2,1)}, ...) while((s32[]{:T(128)}, bf16[3,256,128]{2,1,0:T(8,128)(2,1)}, ...), condition=%wide.region_18.18_spmd, body=%wide.region_15.17_spmd.sunk | while | flops 102465024 | bytes 2894953 | solution.py:43
  140.2 1.6 bitcast_dynamic-update-slice_fusion.3
  145.6 8.0 %while.24 = (s32[]{:T(128)}, bf16[3,256,128]{2,1,0:T(8,128)(2,1)}, s32[3,256]{1,0:T(4,128)S(1)}, s32[768]{0:T(1024)S(1)}, bf16[3,256,128]{2,1,0:T(8,128)(2,1)}, ...) while((s32[]{:T(128)}, bf16[3,256,128]{2,1,0:T(8,128)(2,1)}, ...), condition=%wide.region_18.18_spmd, body=%wide.region_15.17_spmd.sunk | while | flops 102465024 | bytes 2894953 | solution.py:43
  153.6 1.6 bitcast_dynamic-update-slice_fusion.3
  157.0 4.7 %all-to-all-start.3 = ((bf16[8,32,256]{2,1,0:T(8,128)(2,1)}), bf16[8,32,256]{2,1,0:T(8,128)(2,1)S(1)}, u32[]{:S(2)}, u32[]{:S(2)}) async-start(bf16[8,32,256]{2,1,0:T(8,128)(2,1)} %all_to_all.40), calls=%async_computation.3 | async-start | bytes 262144 | tf_op jit(solution)/shard_map/all_to_all | solution.py:174
  163.9 4.6 %all-to-all-done.3 = bf16[8,32,256]{2,1,0:T(8,128)(2,1)S(1)} async-done(((bf16[8,32,256]{2,1,0:T(8,128)(2,1)}), bf16[8,32,256]{2,1,0:T(8,128)(2,1)S(1)}, u32[]{:S(2)}, u32[]{:S(2)}) %all-to-all-start.3) | async-done | bytes 131104 | tf_op jit(solution)/shard_map/all_to_all | solution.py:174
  168.5 3.4 %all-to-all-start.2 = ((bf16[8,64,256]{2,1,0:T(8,128)(2,1)}), bf16[8,64,256]{2,1,0:T(8,128)(2,1)S(1)}, u32[]{:S(2)}, u32[]{:S(2)}) async-start(bf16[8,64,256]{2,1,0:T(8,128)(2,1)} %all_to_all.36), calls=%async_computation.2 | async-start | bytes 524288 | tf_op jit(solution)/shard_map/all_to_all | solution.py:173
  172.6 9.0 %all-to-all-done.2 = bf16[8,64,256]{2,1,0:T(8,128)(2,1)S(1)} async-done(((bf16[8,64,256]{2,1,0:T(8,128)(2,1)}), bf16[8,64,256]{2,1,0:T(8,128)(2,1)S(1)}, u32[]{:S(2)}, u32[]{:S(2)}) %all-to-all-start.2) | async-done | bytes 262176 | tf_op jit(solution)/shard_map/all_to_all | solution.py:173
  (156 shorter events, 57.9 us)
Async XLA Ops:
  7.2 13.4 %copy-start = (bf16[32,2,8,3072]{3,2,1,0:T(8,128)(2,1)S(1)}, bf16[32,2,8,3072]{3,2,1,0:T(8,128)(2,1)}, u32[]{:S(2)}) copy-start(bf16[32,2,8,3072]{3,2,1,0:T(8,128)(2,1)} %param.19) | copy-start | bytes 9437188
  7.2 12.0 %copy-start.9 = (s32[4,4]{1,0:T(4,128)S(1)}, s32[4,4]{1,0:T(4,128)}, u32[]{:S(2)}) copy-start(s32[4,4]{1,0:T(4,128)} %param.22) | copy-start | bytes 196
  7.2 11.2 %copy-start.1 = (s32[128]{0:T(128)S(1)}, s32[128]{0:T(128)}, u32[]{:S(2)}) copy-start(s32[128]{0:T(128)} %param.21) | copy-start | bytes 1540
  7.2 58.5 %all-gather.5.cloned.1.call-start = ((), (), s32[]{:S(2)}) async-start(), calls=%async_computation.5 | async-start | bytes 1769472 | tf_op jit(solution)/shard_map/all_gather | solution.py:144
  10.7 2.3 %copy-start.16 = (s32[256]{0:T(256)}, s32[256]{0:T(256)S(1)}, u32[]{:S(2)}) copy-start(s32[256]{0:T(256)S(1)} %convert_reduce_fusion.2) | copy-start | bytes 3076
  14.4 15.3 %copy-start.2 = (bf16[64,3072]{1,0:T(8,128)(2,1)S(1)}, bf16[64,3072]{1,0:T(8,128)(2,1)}, u32[]{:S(2)}) copy-start(bf16[64,3072]{1,0:T(8,128)(2,1)} %param.14) | copy-start | bytes 1179652
  19.9 13.9 %copy-start.15 = (pred[4]{0:T(512)(128)(4,1)}, pred[4]{0:T(512)(128)(4,1)S(1)}, u32[]{:S(2)}) copy-start(pred[4]{0:T(512)(128)(4,1)S(1)} %get-tuple-element.130) | copy-start | bytes 16
  20.0 0.5 copy-start.22
  20.5 13.3 %copy-start.13 = (s32[1024]{0:T(1024)}, s32[1024]{0:T(1024)S(1)}, u32[]{:S(2)}) copy-start(s32[1024]{0:T(1024)S(1)} %pad_clamp_fusion.1) | copy-start | bytes 12292
  21.9 12.0 %copy-start.17 = (s32[256]{0:T(256)S(1)}, s32[256]{0:T(256)}, u32[]{:S(2)}) copy-start(s32[256]{0:T(256)} %copy-done.16) | copy-start | bytes 3076
  22.5 7.1 %copy-start.18 = (pred[4]{0:T(512)(128)(4,1)}, pred[4]{0:T(512)(128)(4,1)S(1)}, u32[]{:S(2)}) copy-start(pred[4]{0:T(512)(128)(4,1)S(1)} %compare_and_fusion) | copy-start | bytes 16
  24.4 20.7 %all-to-all-start = ((bf16[4,2,8,3072]{3,2,1,0:T(8,128)(2,1)}), bf16[4,2,8,3072]{3,2,1,0:T(8,128)(2,1)}, u32[]{:S(2)}, u32[]{:S(2)}) async-start(bf16[4,2,8,3072]{3,2,1,0:T(8,128)(2,1)} %copy.93), calls=%async_computation | async-start | bytes 786432 | tf_op jit(solution)/shard_map/all_to_all | solution.py:136
  29.6 65.6 %all-gather.3.cloned.1.call-start = ((), (), s32[]{:S(2)}) async-start(), calls=%async_computation.4 | async-start | bytes 3538944 | tf_op jit(solution)/shard_map/all_gather | solution.py:143
  31.6 11.3 %copy-start.19 = (pred[4]{0:T(512)(128)(4,1)S(1)}, pred[4]{0:T(512)(128)(4,1)}, u32[]{:S(2)}) copy-start(pred[4]{0:T(512)(128)(4,1)} %copy-done.18) | copy-start | bytes 16
  33.9 15.4 %copy-start.10 = (s32[768]{0:T(1024)}, s32[768]{0:T(1024)S(1)}, u32[]{:S(2)}) copy-start(s32[768]{0:T(1024)S(1)} %pad_add_fusion) | copy-start | bytes 9220
  34.6 14.7 %copy-start.14 = (s32[1024]{0:T(1024)}, s32[1024]{0:T(1024)S(1)}, u32[]{:S(2)}) copy-start(s32[1024]{0:T(1024)S(1)} %pad_clamp_fusion) | copy-start | bytes 12292
  45.1 15.6 %all-to-all-start.1 = ((bf16[4,2,64,768]{3,2,1,0:T(8,128)(2,1)}), bf16[4,2,64,768]{3,2,1,0:T(8,128)(2,1)}, u32[]{:S(2)}, u32[]{:S(2)}) async-start(bf16[4,2,64,768]{3,2,1,0:T(8,128)(2,1)} %select_select_fusion), calls=%async_computation.1 | async-start | bytes 1572864 | tf_op jit(solution)/shard_map/all_to_all | solution.py:137
  83.2 4.3 %copy-start.5 = (bf16[4,1,64,768]{3,2,1,0:T(8,128)(2,1)S(1)}, bf16[4,1,64,768]{3,2,1,0:T(8,128)(2,1)}, u32[]{:S(2)}) copy-start(bf16[4,1,64,768]{3,2,1,0:T(8,128)(2,1)} %get-tuple-element.142) | copy-start | bytes 1179652
  90.9 21.6 %copy-start.12 = (bf16[512,4]{0,1:T(4,128)(2,1)S(1)}, bf16[512,4]{0,1:T(4,128)(2,1)}, u32[]{:S(2)}) copy-start(bf16[512,4]{0,1:T(4,128)(2,1)} %fusion.46) | copy-start | bytes 12292
  95.2 17.3 %copy-start.3 = (bf16[512,3072]{1,0:T(8,128)(2,1)S(1)}, bf16[512,3072]{1,0:T(8,128)(2,1)}, u32[]{:S(2)}) copy-start(bf16[512,3072]{1,0:T(8,128)(2,1)} %all-gather.3.cloned.1.call-done) | copy-start | bytes 9437188
  112.5 5.0 %copy-start.4 = (bf16[4,1,64,768]{3,2,1,0:T(8,128)(2,1)S(1)}, bf16[4,1,64,768]{3,2,1,0:T(8,128)(2,1)}, u32[]{:S(2)}) copy-start(bf16[4,1,64,768]{3,2,1,0:T(8,128)(2,1)} %get-tuple-element.141) | copy-start | bytes 1179652
  119.1 5.6 %copy-start.20 = (f32[128]{0:T(128)S(1)}, f32[128]{0:T(128)}, u32[]{:S(2)}) copy-start(f32[128]{0:T(128)} %get-tuple-element.147) | copy-start | bytes 1540
  119.1 5.6 %copy-start.21 = (f32[128]{0:T(128)S(1)}, f32[128]{0:T(128)}, u32[]{:S(2)}) copy-start(f32[128]{0:T(128)} %get-tuple-element.149) | copy-start | bytes 1540
  119.1 6.9 %copy-start.8 = (bf16[256,2,128]{0,2,1:T(8,128)(2,1)S(1)}, bf16[256,2,128]{0,2,1:T(8,128)(2,1)}, u32[]{:S(2)}) copy-start(bf16[256,2,128]{0,2,1:T(8,128)(2,1)} %get-tuple-element.151) | copy-start | bytes 393220
  119.1 7.7 %copy-start.6 = (bf16[256,2,128]{0,2,1:T(8,128)(2,1)S(1)}, bf16[256,2,128]{0,2,1:T(8,128)(2,1)}, u32[]{:S(2)}) copy-start(bf16[256,2,128]{0,2,1:T(8,128)(2,1)} %fusion.41) | copy-start | bytes 393220
  122.2 5.4 %copy-start.7 = (bf16[256,2,128]{0,2,1:T(8,128)(2,1)S(1)}, bf16[256,2,128]{0,2,1:T(8,128)(2,1)}, u32[]{:S(2)}) copy-start(bf16[256,2,128]{0,2,1:T(8,128)(2,1)} %get-tuple-element.152) | copy-start | bytes 393220
  122.2 6.2 %copy-start.11 = (s32[768]{0:T(1024)S(1)}, s32[768]{0:T(1024)}, u32[]{:S(2)}) copy-start(s32[768]{0:T(1024)} %copy-done.10) | copy-start | bytes 9220
  157.0 11.5 %all-to-all-start.3 = ((bf16[8,32,256]{2,1,0:T(8,128)(2,1)}), bf16[8,32,256]{2,1,0:T(8,128)(2,1)S(1)}, u32[]{:S(2)}, u32[]{:S(2)}) async-start(bf16[8,32,256]{2,1,0:T(8,128)(2,1)} %all_to_all.40), calls=%async_computation.3 | async-start | bytes 262144 | tf_op jit(solution)/shard_map/all_to_all | solution.py:174
  168.5 13.1 %all-to-all-start.2 = ((bf16[8,64,256]{2,1,0:T(8,128)(2,1)}), bf16[8,64,256]{2,1,0:T(8,128)(2,1)S(1)}, u32[]{:S(2)}, u32[]{:S(2)}) async-start(bf16[8,64,256]{2,1,0:T(8,128)(2,1)} %all_to_all.36), calls=%async_computation.2 | async-start | bytes 524288 | tf_op jit(solution)/shard_map/all_to_all | solution.py:173
Sparse Core Ops, SparseCore 0:
  16.5 27.9 all-gather.4
  46.2 37.7 all-gather.2
where the time goes:
time: 191 us; the launch traced here: 189 us
  local copies, waits for them, and re-layouts  44.5 us (23%)
  matrix products  38.2 us (20%)
  blocking collectives  29 us (15%)
  other arithmetic  23.8 us (12%)
  waiting for transfers between devices  21.6 us (11%)
  starting transfers between devices  17.6 us (9%)
  between operations  14.4 us (8%)
    all_gather x1, blocking collectives, body(): lax.all_gather(image_part, 'seq', axis=0, tiled=True)  14.8 us
    all_gather x1, blocking collectives, body(): lax.all_gather(text_part, 'seq', axis=0, tiled=True)  14.2 us
    dot_general x2, matrix products, adapted(): plain_part = jnp.dot(hidden_all, weight, preferred_element_type=jnp.float32)  9.25 us
    all_to_all x1, waiting for transfers between devices, body(): lax.all_to_all(outputs[:text_bag], 'seq', split_axis=0, concat_axis=1, ti...  8.97 us
    all_to_all x1, waiting for transfers between devices, body(): lax.all_to_all(up_send, 'bag', split_axis=0, concat_axis=0, tiled=True)  7.96 us
    dot_general x6, matrix products, one_block(): jnp.dot(query_rows, keys_all.T, preferred_element_type=jnp.float32) * factor  7.93 us
    dynamic_slice x10, local copies, waits for them, and re-layouts, body(): outputs = lax.map(one_head, (joined[0], joined[1], joined[2]))  7.58 us
    dot_general x4, matrix products, pick_rows(): return jnp.dot(seg_pick, table_rows, precision=lax.Precision.HIGHEST)  6.94 us
  transfers between devices with their start and end apart: 6, of which 3 were waited for; matrix products, arithmetic and copies ran while one was open for 25% of the time, Pallas kernels for 0%

commit v1 on v0

v1 whole, which is shorter than its diff:
```python
import functools
import math

import jax
import jax.numpy as jnp
from jax import lax
from jax.experimental import pallas as pl
from jax.experimental.pallas import tpu as pltpu
from jax.sharding import PartitionSpec as P


HEAD_DIM = 128
TEXT = 64
CORES = 2
ROW_STEP = 16


VMEM_GRANT = 26 << 20
PARAMS = pltpu.CompilerParams(vmem_limit_bytes=VMEM_GRANT)

SMEM = functools.partial(pl.BlockSpec, memory_space=pltpu.SMEM)
VMEM = functools.partial(pl.BlockSpec, memory_space=pltpu.VMEM)
HBM = functools.partial(pl.BlockSpec, memory_space=pltpu.HBM)
NT = (((1,), (1,)), ((), ()))
TN = (((0,), (0,)), ((), ()))


def round_up(value, step):
    return -(-value // step) * step


class Plan:
    def __init__(self, seq, bags, text_dev, image_dev, users, width, rank, down_dev, store, cols):
        self.seq, self.bags, self.users, self.rank, self.store = seq, bags, users, rank, store
        self.text_dev, self.image_dev, self.width, self.cols = text_dev, image_dev, width, cols
        self.rows = text_dev + image_dev
        self.chips = seq // CORES
        self.half = self.chips // 2
        self.down_dev = down_dev
        self.down_rows = round_up(2 * down_dev, 16)
        self.parts = width // cols
        self.heads = cols // (3 * HEAD_DIM)
        self.wide = self.heads * HEAD_DIM
        self.lanes = round_up(self.rows, 128)
        self.groups = [[("own", 0)]]
        for hop in range(1, self.chips):
            if 2 * hop < self.chips:
                self.groups[0] += [("near", hop), ("far", hop)]
            else:
                self.groups.append([("both", hop)])

    def on_cores(self, pairs, cross=0):
        return [
            (CORES * a + c, CORES * b + (c ^ cross)) for a, b in pairs for c in range(CORES)
        ]


def place_of(plan, slot, half, seq_index):
    chip, core = seq_index // CORES, seq_index % CORES
    kind, hop = slot
    if kind == "own":
        source, lead = chip, core
    elif kind == "near":
        source, lead = jnp.where(core == 1, chip - hop, chip + hop), core
    elif kind == "far":
        source, lead = jnp.where(core == 1, chip + hop, chip - hop), 1 - core
    else:
        low = chip >= hop
        source, lead = jnp.where(low, chip - hop, chip + hop), jnp.where(low, 1, 0)
    valid = (source >= 0) & (source < plan.chips)
    source = jnp.clip(source, 0, plan.chips - 1)
    return source * CORES + (lead if half == 0 else 1 - lead), valid


def refs_per_half(slots):
    return CORES if slots[0][0] == "both" else 1


def is_passed(plan, slot, seq_index):
    chip, core = seq_index // CORES, seq_index % CORES
    return jnp.where(core == 1, chip >= slot[1], chip + slot[1] < plan.chips)


def image_seg_of(position, lengths_ref, users):
    seg = jnp.zeros_like(position)
    end = jnp.int32(0)
    for user in range(users):
        for _ in range(2):
            end = end + lengths_ref[0, user]
            seg = seg + (position >= end).astype(jnp.int32)
    return seg


def user_keys(plan, bag, store_row_ref, adapter_ref):
    return [
        lax.bitwise_xor(store_row_ref[adapter_ref[bag, user]] // plan.store, bag)
        for user in range(plan.users)
    ]


def hidden_kernel(plan, lengths_ref, text_ref, image_ref, mod_ref, out_ref):
    seq_index = lax.axis_index("seq")
    segs = mod_ref.shape[0]

    def normed(rows):
        values = rows.astype(jnp.float32)
        centre = values - jnp.mean(values, axis=-1, keepdims=True)
        spread = jnp.mean(centre * centre, axis=-1, keepdims=True)
        return centre * lax.rsqrt(spread + 1e-06)

    def image_step(step, _):
        rows = pl.ds(pl.multiple_of(step * ROW_STEP, ROW_STEP), ROW_STEP)
        place = seq_index * plan.image_dev + step * ROW_STEP
        position = place + lax.broadcasted_iota(jnp.int32, (ROW_STEP, 1), 0)
        seg = image_seg_of(position, lengths_ref, plan.users)
        base = normed(image_ref[rows, :])
        shift = jnp.zeros_like(base)
        scale = jnp.zeros_like(base)
        for one in range(segs):
            hit = seg == one
            shift = jnp.where(hit, mod_ref[one, 1, 0:1, :], shift)
            scale = jnp.where(hit, mod_ref[one, 1, 1:2, :], scale)
        target = pl.ds(pl.multiple_of(plan.text_dev + step * ROW_STEP, ROW_STEP), ROW_STEP)
        out_ref[target, :] = ((1.0 + scale) * base + shift).astype(jnp.bfloat16)
        return 0

    lax.fori_loop(0, plan.image_dev // ROW_STEP, image_step, 0)

    def text_step(step, _):
        rows = pl.ds(pl.multiple_of(step * ROW_STEP, ROW_STEP), ROW_STEP)
        seg = (seq_index * plan.text_dev + step * ROW_STEP) // TEXT
        shift = mod_ref[seg, 0, 0:1, :]
        scale = mod_ref[seg, 0, 1:2, :]
        out_ref[rows, :] = ((1.0 + scale) * normed(text_ref[rows, :]) + shift).astype(jnp.bfloat16)
        return 0

    lax.fori_loop(0, plan.text_dev // ROW_STEP, text_step, 0)


def hidden_rows(plan, lengths, text_rows, image_rows, modulation):
    return pl.pallas_call(
        functools.partial(hidden_kernel, plan),
        out_shape=jax.ShapeDtypeStruct((plan.rows, plan.width), jnp.bfloat16),
        in_specs=[SMEM(), VMEM(), VMEM(), VMEM()],
        out_specs=VMEM(),
        name="hidden_rows",
    )(lengths, text_rows, image_rows, modulation)


def pack_kernel(plan, store_row_ref, adapter_ref, down_hbm, up_hbm, *rest):
    outs, ups, rest = rest[: plan.bags], rest[plan.bags : 2 * plan.bags], rest[2 * plan.bags :]
    down, up, down_sem, up_sem = rest
    bag = lax.axis_index("bag")
    copies = []
    for hop in range(plan.bags):
        target = lax.bitwise_xor(bag, hop)
        place = jnp.int32(0)
        for user in range(plan.users):
            row = store_row_ref[adapter_ref[target, user]]
            place = jnp.where(row // plan.store == bag, row % plan.store, place)
        one = pltpu.make_async_copy(down_hbm.at[place], down.at[hop], down_sem.at[hop])
        two = pltpu.make_async_copy(up_hbm.at[place], up.at[hop], up_sem.at[hop])
        one.start()
        two.start()
        copies.append((one, two))
    pad = plan.down_rows - 2 * plan.down_dev
    for hop in range(plan.bags):
        copies[hop][0].wait()
        for part in range(plan.parts):
            lanes = slice(part * plan.cols, (part + 1) * plan.cols)
            rows = [down[hop, t, :, lanes].astype(jnp.float32) for t in range(2)]
            if pad:
                rows.append(jnp.zeros((pad, plan.cols), jnp.float32))
            spot = slice(part * plan.down_rows, (part + 1) * plan.down_rows)
            outs[hop][spot, :] = jnp.concatenate(rows, axis=0).astype(jnp.bfloat16)
        copies[hop][1].wait()
        for t in range(2):
            ups[hop][t * plan.rank : (t + 1) * plan.rank, :] = up[hop, t]


def packed_adapters(plan, store_row, user_adapter, store_down, store_up):
    sizes = (plan.parts * plan.down_rows, 2 * plan.rank)
    return pl.pallas_call(
        functools.partial(pack_kernel, plan),
        out_shape=[
            jax.ShapeDtypeStruct((rows, plan.cols), jnp.bfloat16)
            for rows in sizes
            for _ in range(plan.bags)
        ],
        in_specs=[SMEM(), SMEM(), HBM(), HBM()],
        out_specs=[VMEM()] * (2 * plan.bags),
        scratch_shapes=[
            pltpu.VMEM((plan.bags,) + store_down.shape[1:], jnp.bfloat16),
            pltpu.VMEM((plan.bags,) + store_up.shape[1:], jnp.bfloat16),
            pltpu.SemaphoreType.DMA((plan.bags,)),
            pltpu.SemaphoreType.DMA((plan.bags,)),
        ],
        name="packed_adapters",
    )(store_row, user_adapter, store_down, store_up)


def project_kernel(plan, slots, *refs):
    blocks, (weight_ref, text_out, image_out, texts, images) = refs[:-5], refs[-5:]
    text_dev, image_dev, each = plan.text_dev, plan.image_dev, refs_per_half(slots)

    def take(at, block):
        texts[at * text_dev : (at + 1) * text_dev, :] = block[:text_dev, :]
        images[at * image_dev : (at + 1) * image_dev, :] = block[text_dev:, :]

    if each == 1:
        for at, block in enumerate(blocks):
            take(at, block)
    else:
        passed = is_passed(plan, slots[0], lax.axis_index("seq"))
        for choice in range(2):

            @pl.when(passed if choice == 0 else jnp.logical_not(passed))
            def _():
                for at in range(CORES):
                    take(at, blocks[2 * at + choice])

    text_out[...] = jnp.dot(texts[...], weight_ref[0], preferred_element_type=jnp.float32)
    image_out[...] = jnp.dot(images[...], weight_ref[1], preferred_element_type=jnp.float32)


def project(plan, slots, blocks, head_weight):
    count = CORES * len(slots)
    sizes = (count * plan.text_dev, count * plan.image_dev)
    return pl.pallas_call(
        functools.partial(project_kernel, plan, slots),
        out_shape=tuple(jax.ShapeDtypeStruct((size, plan.cols), jnp.float32) for size in sizes),
        in_specs=[VMEM()] * (len(blocks) + 1),
        out_specs=(VMEM(), VMEM()),
        scratch_shapes=[pltpu.VMEM((size, plan.width), jnp.bfloat16) for size in sizes],
        compiler_params=PARAMS,
        cost_estimate=pl.CostEstimate(
            flops=2 * sum(sizes) * plan.width * plan.cols,
            bytes_accessed=2 * sum(sizes) * plan.width,
            transcendentals=0,
        ),
    )(*blocks, head_weight)


def lane_keys(plan, lengths_ref, keys, place):
    lane = lax.broadcasted_iota(jnp.int32, (1, plan.lanes), 1)
    is_text = lane < plan.text_dev
    text_seg = (place * plan.text_dev + lane) // TEXT
    image_at = place * plan.image_dev + lane - plan.text_dev
    seg = jnp.where(is_text, text_seg, image_seg_of(image_at, lengths_ref, plan.users))
    key = jnp.zeros_like(lane)
    for user in range(plan.users):
        key = jnp.where(seg // 2 == user, keys[user], key)
    return key, is_text


def rank_kernel(plan, slots, lengths_ref, store_row_ref, adapter_ref, *refs):
    halves = CORES * len(slots)
    downs, refs = refs[: plan.half], refs[plan.half :]
    each = refs_per_half(slots)
    blocks, refs = refs[: each * halves], refs[each * halves :]
    before, (out_ref, stacked) = refs[:-2], refs[-2:]
    for one in before:
        out_ref[...] = one[...]
    bag, seq_index = lax.axis_index("bag"), lax.axis_index("seq")
    chip = seq_index // CORES
    passed = is_passed(plan, slots[0], seq_index)
    keys = user_keys(plan, bag, store_row_ref, adapter_ref)
    tall = plan.bags * plan.down_rows
    for index, down_ref in enumerate(downs):
        for part in range(plan.parts):
            lanes = slice(part * plan.cols, (part + 1) * plan.cols)
            stacked[index * tall : (index + 1) * tall, lanes] = down_ref[part]
    for at in range(halves):
        place, valid = place_of(plan, slots[at // CORES], at % CORES, seq_index)
        block = blocks[each * at][...]
        if each > 1:
            block = jnp.where(passed, block, blocks[each * at + 1][...])
        found = lax.dot_general(block, stacked[...], NT, preferred_element_type=jnp.float32)
        found = jnp.transpose(found)
        if plan.rows < plan.lanes:
            pad = jnp.zeros((found.shape[0], plan.lanes - plan.rows), jnp.float32)
            found = jnp.concatenate([found, pad], axis=1)
        key, is_text = lane_keys(plan, lengths_ref, keys, place)
        for index in range(plan.half):
            total = jnp.zeros((plan.down_dev, plan.lanes), jnp.float32)
            for hop in range(plan.bags):
                top = index * tall + hop * plan.down_rows
                text_part = found[top : top + plan.down_dev]
                image_part = found[top + plan.down_dev : top + 2 * plan.down_dev]
                total = total + jnp.where(
                    key == hop, jnp.where(is_text, text_part, image_part), 0.0
                )
            spot = jnp.where(chip < plan.half, plan.half - 1 - index, index)

            @pl.when(valid)
            def _():
                out_ref[spot, place] = total.astype(jnp.bfloat16)


def rank_parts(plan, slots, lengths, store_row, user_adapter, downs, blocks, before):
    before = [] if before is None else [before]
    each = plan.bags * plan.down_rows
    rows = plan.rows * len(blocks)
    return pl.pallas_call(
        functools.partial(rank_kernel, plan, slots),
        out_shape=jax.ShapeDtypeStruct(
            (plan.half, plan.seq, plan.down_dev, plan.lanes), jnp.bfloat16
        ),
        in_specs=[SMEM()] * 3 + [VMEM()] * (len(downs) + len(blocks) + len(before)),
        out_specs=VMEM(),
        scratch_shapes=[pltpu.VMEM((len(downs) * each, plan.width), jnp.bfloat16)],
        compiler_params=PARAMS,
        cost_estimate=pl.CostEstimate(
            flops=4 * rows * plan.width * len(downs) * each,
            bytes_accessed=2 * rows * plan.width,
            transcendentals=0,
        ),
        name="rank_parts",
    )(lengths, store_row, user_adapter, *downs, *blocks, *before)


def head_normed(values, gain_row):
    spread = jnp.mean(values * values, axis=-1, keepdims=True)
    return (values * lax.rsqrt(spread + 1e-06) * gain_row).astype(jnp.bfloat16)


def write_heads(plan, mixed_of, gain_ref, stream, out_ref, rows):
    for head in range(plan.heads):
        for which in range(3):
            first = (3 * head + which) * HEAD_DIM
            mixed = mixed_of(slice(first, first + HEAD_DIM))
            if which < 2:
                mixed = head_normed(mixed, gain_ref[stream, which : which + 1, :])
            lanes = slice(head * HEAD_DIM, (head + 1) * HEAD_DIM)
            out_ref[which, rows, lanes] = mixed.astype(jnp.bfloat16)


def early_kernel(plan, groups, lengths_ref, store_row_ref, adapter_ref, gain_ref, *refs):
    ranks, refs = refs[: plan.half], refs[plan.half :]
    packs, refs = refs[: plan.bags], refs[plan.bags :]
    plains, refs = refs[: 2 * len(groups)], refs[2 * len(groups) :]
    text_heads, image_heads, text_last, image_last, ranks_ref, spread, ups, adjust = refs
    bag, seq_index = lax.axis_index("bag"), lax.axis_index("seq")
    chip, core = seq_index // CORES, seq_index % CORES
    upper = (chip >= plan.half).astype(jnp.int32)
    reach = jnp.where(chip < plan.half, plan.half - 1 - chip, chip - plan.half)
    for hop in range(plan.half):

        @pl.when(reach == hop)
        def _():
            ranks_ref[...] = ranks[hop][...]

    keys = user_keys(plan, bag, store_row_ref, adapter_ref)
    for place in range(plan.seq):
        key, _ = lane_keys(plan, lengths_ref, keys, place)
        lanes = slice(place * plan.lanes, (place + 1) * plan.lanes)
        for side in range(2):
            for lead in range(CORES):
                for index in range(plan.half):
                    rows = ranks_ref[
                        lax.bitwise_xor(upper, side), lax.bitwise_xor(core, lead), index, place
                    ].astype(jnp.float32)
                    first = ((side * plan.half + index) * CORES + lead) * plan.down_dev
                    for hop in range(plan.bags):
                        top = hop * plan.rank + first
                        spread[top : top + plan.down_dev, lanes] = jnp.where(key == hop, rows, 0.0)
    for stream in range(2):
        for hop in range(plan.bags):
            ups[hop * plan.rank : (hop + 1) * plan.rank, :] = packs[hop][
                stream * plan.rank : (stream + 1) * plan.rank, :
            ]
        adjust[...] = lax.dot_general(
            spread[...].astype(jnp.bfloat16), ups[...], TN, preferred_element_type=jnp.float32
        )
        size = plan.text_dev if stream == 0 else plan.image_dev
        skip = 0 if stream == 0 else plan.text_dev
        out_ref = text_heads if stream == 0 else image_heads
        last_ref = text_last if stream == 0 else image_last

        def rows_of(place):
            return pl.ds(pl.multiple_of(place * plan.lanes + skip, 32), size)

        for group_at, group in enumerate(groups):
            plain = plains[2 * group_at + stream]
            for at in range(CORES * len(group)):
                place, valid = place_of(plan, group[at // CORES], at % CORES, seq_index)

                @pl.when(valid)
                def _():
                    write_heads(
                        plan,
                        lambda lanes: plain[at * size : (at + 1) * size, lanes]
                        + adjust[rows_of(place), lanes],
                        gain_ref,
                        stream,
                        out_ref,
                        pl.ds(pl.multiple_of(place * size, size), size),
                    )

        for half in range(CORES):
            place, _ = place_of(plan, plan.groups[-1][0], half, seq_index)
            last_ref[half * size : (half + 1) * size, :] = adjust[rows_of(place), :]


def early_heads(plan, groups, lengths, store_row, user_adapter, norm_gain, ranks, packs, plains):
    total = (plan.seq * plan.text_dev, plan.seq * plan.image_dev)
    last = (CORES * plan.text_dev, CORES * plan.image_dev)
    scratch = 4 * plan.seq * plan.lanes * (plan.bags * plan.rank + plan.cols)
    return pl.pallas_call(
        functools.partial(early_kernel, plan, groups),
        out_shape=tuple(jax.ShapeDtypeStruct((3, n, plan.wide), jnp.bfloat16) for n in total)
        + tuple(jax.ShapeDtypeStruct((n, plan.cols), jnp.float32) for n in last),
        in_specs=[SMEM()] * 3 + [VMEM()] * (1 + plan.half + plan.bags + len(plains)),
        out_specs=(VMEM(),) * 4,
        scratch_shapes=[
            pltpu.VMEM(ranks[0].shape, jnp.bfloat16),
            pltpu.VMEM((plan.bags * plan.rank, plan.seq * plan.lanes), jnp.float32),
            pltpu.VMEM((plan.bags * plan.rank, plan.cols), jnp.bfloat16),
            pltpu.VMEM((plan.seq * plan.lanes, plan.cols), jnp.float32),
        ],
        compiler_params=pltpu.CompilerParams(vmem_limit_bytes=max(VMEM_GRANT, 2 * scratch)),
        cost_estimate=pl.CostEstimate(
            flops=4 * plan.seq * plan.lanes * plan.bags * plan.rank * plan.cols,
            bytes_accessed=8 * sum(total) * plan.cols,
            transcendentals=0,
        ),
        name="early_heads",
    )(lengths, store_row, user_adapter, norm_gain, *ranks, *packs, *plains)


def attend_kernel(plan, lengths_ref, gain_ref, *refs):
    text_in, image_in, text_plain, image_plain, text_adjust, image_adjust = refs[:6]
    out_ref, text_heads, image_heads = refs[6:]
    seq_index = lax.axis_index("seq")
    factor = 1.0 / math.sqrt(HEAD_DIM)
    text_heads[...] = text_in[...]
    image_heads[...] = image_in[...]
    for stream in range(2):
        plain = text_plain if stream == 0 else image_plain
        adjust = text_adjust if stream == 0 else image_adjust
        size = plan.text_dev if stream == 0 else plan.image_dev
        for half in range(CORES):
            place, valid = place_of(plan, plan.groups[-1][0], half, seq_index)
            rows = slice(half * size, (half + 1) * size)

            @pl.when(valid)
            def _():
                write_heads(
                    plan,
                    lambda lanes: plain[rows, lanes] + adjust[rows, lanes],
                    gain_ref,
                    stream,
                    text_heads if stream == 0 else image_heads,
                    pl.ds(pl.multiple_of(place * size, size), size),
                )

    text_total, image_total = plan.seq * plan.text_dev, plan.seq * plan.image_dev
    image_seg = functools.partial(image_seg_of, lengths_ref=lengths_ref, users=plan.users)
    text_cols = lax.broadcasted_iota(jnp.int32, (1, text_total), 1) // TEXT
    image_cols = image_seg(lax.broadcasted_iota(jnp.int32, (1, image_total), 1))
    image_rows = image_seg(lax.broadcasted_iota(jnp.int32, (image_total, 1), 0))
    step = TEXT

    def softmax(scores, hits):
        scores = [jnp.where(hit, one * factor, -1e30) for one, hit in zip(scores, hits)]
        tops = [jnp.max(one, axis=1, keepdims=True) for one in scores]
        top = functools.reduce(jnp.maximum, tops)
        weights = [jnp.exp(one - top) for one in scores]
        total = sum(jnp.sum(one, axis=1, keepdims=True) for one in weights)
        inverse = 1.0 / total
        return [(one * inverse).astype(jnp.bfloat16) for one in weights]

    def pair(queries, keys):
        return lax.dot_general(queries, keys, NT, preferred_element_type=jnp.float32)

    def mix(probs, values):
        found = [
            jnp.dot(one, value, preferred_element_type=jnp.float32)
            for one, value in zip(probs, values)
        ]
        return sum(found).astype(jnp.bfloat16)

    for head in range(plan.heads):
        lanes = slice(head * HEAD_DIM, (head + 1) * HEAD_DIM)
        image_keys, image_values = image_heads[1, :, lanes], image_heads[2, :, lanes]
        for seg in range(text_total // step):
            rows = slice(seg * step, (seg + 1) * step)
            queries = text_heads[0, rows, lanes]
            near = pair(queries, text_heads[1, rows, lanes]) * factor
            far = pair(queries, image_keys)
            far = jnp.where(image_cols == seg, far * factor, -1e30)
            top = jnp.maximum(
                jnp.max(near, axis=1, keepdims=True), jnp.max(far, axis=1, keepdims=True)
            )
            near, far = jnp.exp(near - top), jnp.exp(far - top)
            total = jnp.sum(near, axis=1, keepdims=True) + jnp.sum(far, axis=1, keepdims=True)
            inverse = 1.0 / total
            probs = [(one * inverse).astype(jnp.bfloat16) for one in (near, far)]
            place, inner = divmod(seg * step, plan.text_dev)
            out_ref[place, inner : inner + step, lanes] = mix(
                probs, (text_heads[2, rows, lanes], image_values)
            )
        queries = image_heads[0, :, lanes]
        probs = softmax(
            (pair(queries, image_keys), pair(queries, text_heads[1, :, lanes])),
            (image_rows == image_cols, image_rows == text_cols),
        )
        result = mix(probs, (image_values, text_heads[2, :, lanes]))
        for place in range(plan.seq):
            out_ref[place, plan.text_dev :, lanes] = result[
                place * plan.image_dev : (place + 1) * plan.image_dev, :
            ]


def attention(plan, lengths, norm_gain, arrays):
    text_total, image_total = plan.seq * plan.text_dev, plan.seq * plan.image_dev
    return pl.pallas_call(
        functools.partial(attend_kernel, plan),
        out_shape=jax.ShapeDtypeStruct((plan.seq, plan.rows, plan.wide), jnp.bfloat16),
        in_specs=[SMEM()] + [VMEM()] * (1 + len(arrays)),
        out_specs=VMEM(),
        scratch_shapes=[
            pltpu.VMEM((3, text_total, plan.wide), jnp.bfloat16),
            pltpu.VMEM((3, image_total, plan.wide), jnp.bfloat16),
        ],
        compiler_params=PARAMS,
        name="attention",
    )(lengths, norm_gain, *arrays)


def place_kernel(plan, pieces, text_out, image_out):
    for place in range(plan.seq):
        lanes = slice(place * plan.wide, (place + 1) * plan.wide)
        text_out[:, lanes] = pieces[place, : plan.text_dev, :]
        image_out[:, lanes] = pieces[place, plan.text_dev :, :]


def placed(plan, pieces):
    sizes = (plan.text_dev, plan.image_dev)
    return pl.pallas_call(
        functools.partial(place_kernel, plan),
        out_shape=tuple(
            jax.ShapeDtypeStruct((n, plan.seq * plan.wide), jnp.bfloat16) for n in sizes
        ),
        in_specs=[VMEM()],
        out_specs=(VMEM(), VMEM()),
        compiler_params=PARAMS,
        name="placed",
    )(pieces)


def steps(
    text_rows,
    image_rows,
    modulation,
    head_weight,
    norm_gain,
    store_down,
    store_up,
    store_row,
    user_adapter,
    image_lengths,
):
    seq, bags = lax.axis_size("seq"), lax.axis_size("bag")
    plan = Plan(
        seq,
        bags,
        text_rows.shape[0],
        image_rows.shape[0],
        image_lengths.shape[1],
        text_rows.shape[1],
        store_up.shape[2],
        store_down.shape[2],
        store_down.shape[0],
        head_weight.shape[2],
    )
    swap = plan.on_cores([(z, z) for z in range(plan.chips)], 1)

    hidden = hidden_rows(plan, image_lengths, text_rows, image_rows, modulation)
    blocks = {("own", 0, 0): hidden, ("own", 0, 1): lax.ppermute(hidden, "seq", swap)}
    passing = [blocks["own", 0, 0], blocks["own", 0, 1]]
    for hop in range(1, plan.chips):
        up = [(2 * z + 1, 2 * z + 3) for z in range(hop - 1, plan.chips - 1)]
        down = [(2 * z, 2 * z - 2) for z in range(1, plan.chips - hop + 1)]
        for half in range(CORES):
            passing[half] = lax.ppermute(passing[half], "seq", up + down)
            other = lax.ppermute(passing[half], "seq", swap)
            if 2 * hop < plan.chips:
                blocks["near", hop, half] = passing[half]
                blocks["far", hop, half] = other
            else:
                blocks["both", hop, half] = (passing[half], other)

    packs = packed_adapters(plan, store_row, user_adapter, store_down, store_up)
    arrived = {}
    for kind, sent in (("down", packs[:bags]), ("up", packs[bags:])):
        arrived[kind] = [sent[0]] + [
            lax.ppermute(sent[hop], "bag", [(b, b ^ hop) for b in range(bags)])
            for hop in range(1, bags)
        ]
    down_shape = (plan.parts, plan.down_rows, plan.cols)
    down_own = jnp.concatenate([one.reshape(down_shape) for one in arrived["down"]], axis=1)
    low, high = plan.half - 1, plan.half
    downs = [down_own] + [
        lax.ppermute(down_own, "seq", plan.on_cores([(low - hop, low), (high + hop, high)]))
        for hop in range(1, plan.half)
    ]

    def blocks_of(slots):
        found = [blocks[kind, hop, half] for kind, hop in slots for half in range(CORES)]
        return [one for pick in found for one in (pick if isinstance(pick, tuple) else (pick,))]

    plains = []
    for group in plan.groups:
        plains.append(project(plan, group, blocks_of(group), head_weight))
    scalars = (image_lengths, store_row, user_adapter)
    ranks = None
    for group in plan.groups[:2]:
        ranks = rank_parts(plan, group, *scalars, downs, blocks_of(group), ranks)
    ranks = jnp.stack([ranks, lax.ppermute(ranks, "seq", swap)])
    other = lax.ppermute(ranks, "seq", plan.on_cores([(low, high), (high, low)]))
    ranks = jnp.stack([ranks, other])
    ranks = [ranks] + [
        lax.ppermute(ranks, "seq", plan.on_cores([(low, low - hop), (high, high + hop)]))
        for hop in range(1, plan.half)
    ]

    arrays = early_heads(
        plan,
        plan.groups[:-1],
        *scalars,
        norm_gain,
        ranks,
        arrived["up"],
        [one for pair in plains[:-1] for one in pair],
    )
    outs = attention(
        plan, image_lengths, norm_gain, list(arrays[:2]) + list(plains[-1]) + list(arrays[2:])
    )
    pieces = lax.all_to_all(outs, "seq", split_axis=0, concat_axis=0, tiled=True)
    return placed(plan, pieces)


def solution(mesh):
    in_specs = (
        P(("bag", "seq"), None),
        P(("bag", "seq"), None),
        P("bag", None, None, None),
        P(None, None, "seq"),
        P(),
        P("bag", None, "seq", None),
        P("bag", None, None, "seq"),
        P(),
        P(),
        P("bag", None),
    )
    out_specs = (P(("bag", "seq"), None), P(("bag", "seq"), None))
    return jax.shard_map(steps, mesh=mesh, in_specs=in_specs, out_specs=out_specs, check_vma=False)
```

time: 191 us -> 113 us (0.59)
  local copies, waits for them, and re-layouts: 44.5 us -> 4.44 us
  matrix products: 38.2 us -> 0 us
  Pallas kernels: 0 us -> 31.3 us
  other arithmetic: 23.8 us -> 0.94 us
  between operations: 14.4 us -> 1 us
  blocking collectives: 29 us -> 16.3 us
  waiting for transfers between devices: 21.6 us -> 33.6 us
  starting transfers between devices: 17.6 us -> 24.6 us
    dot_general x22 -> x0, matrix products: 38.2 us -> none  [the longest x2 9.25 us: adapted(): plain_part = jnp.dot(hidden_all, weight, preferred_element_type=jnp.float32)]
    ppermute x0 -> x23, waiting for transfers between devices: none -> 33.6 us  [the longest x6 20.8 us: steps(): passing[half] = lax.ppermute(passing[half], 'seq', up + down)]
    pallas_call x0 -> x10, Pallas kernels: none -> 31.3 us  [the longest x1 7.5 us: attention(): pl.pallas_call(functools.partial(attend_kernel, plan), out_shape=jax.Shap...]
    all_gather x2 -> x0, blocking collectives: 29 us -> none  [the longest x1 14.8 us: body(): lax.all_gather(image_part, 'seq', axis=0, tiled=True)]
    ppermute x0 -> x23, starting transfers between devices: none -> 24.6 us  [the longest x6 9.05 us: steps(): lax.ppermute(sent[hop], 'bag', [(b, b ^ hop) for b in range(bags)])]
    all_to_all x4 -> x0, waiting for transfers between devices: 21.6 us -> none  [the longest x1 8.97 us: body(): lax.all_to_all(outputs[:text_bag], 'seq', split_axis=0, concat_axis=1, ti...]
    all_to_all x4 -> x0, starting transfers between devices: 17.6 us -> none  [the longest x1 5.19 us: body(): lax.all_to_all(down_send, 'bag', split_axis=0, concat_axis=0, tiled=True)]
    all_to_all x0 -> x1, blocking collectives: none -> 16.3 us  [steps(): lax.all_to_all(outs, 'seq', split_axis=0, concat_axis=0, tiled=True)]
  transfers between devices with their start and end apart: 6 -> 23, of which waited for: 3 -> 9; matrix products, arithmetic and copies ran while one was open for 25% -> 1% of each run, Pallas kernels for 0% -> 15%
where the time goes in v1:
time: 113 us; the launch traced here: 112 us
  waiting for transfers between devices  33.6 us (30%)
  Pallas kernels  31.3 us (28%)
  starting transfers between devices  24.6 us (22%)
  blocking collectives  16.3 us (14%)
  local copies, waits for them, and re-layouts  4.44 us (4%)
    ppermute x6, waiting for transfers between devices, steps(): passing[half] = lax.ppermute(passing[half], 'seq', up + down)  20.8 us
    all_to_all x1, blocking collectives, steps(): lax.all_to_all(outs, 'seq', split_axis=0, concat_axis=0, tiled=True)  16.3 us
    ppermute x6, starting transfers between devices, steps(): lax.ppermute(sent[hop], 'bag', [(b, b ^ hop) for b in range(bags)])  9.05 us
    ppermute x6, starting transfers between devices, steps(): passing[half] = lax.ppermute(passing[half], 'seq', up + down)  7.69 us
    pallas_call x1, Pallas kernels, attention(): pl.pallas_call(functools.partial(attend_kernel, plan), out_shape=jax.Shap...  7.5 us
    ppermute x1, waiting for transfers between devices, steps(): lax.ppermute(down_own, 'seq', plan.on_cores([(low - hop, low), (high + ho...  6.52 us
    pallas_call x3, Pallas kernels, project(): pl.pallas_call(functools.partial(project_kernel, plan, slots), out_shape=...  6.48 us
    pallas_call x2, Pallas kernels, rank_parts(): pl.pallas_call(functools.partial(rank_kernel, plan, slots), out_shape=jax...  6.2 us
  transfers between devices with their start and end apart: 23, of which 9 were waited for; matrix products, arithmetic and copies ran while one was open for 1% of the time, Pallas kernels for 15%

profile of v1, /device:TPU:0, one launch (start us, length us, event | category | flops | bytes accessed | tf_op | source)
XLA Modules:
  0.0 112.2 jit_solution(16961330430320937696)
XLA Ops:
  0.7 3.8 %hidden_rows.1.refs_2_.refs_0_ = bf16[96,3072]{1,0:T(8,128)(2,1)} custom-call(s32[1,4]{1,0:T(1,128)} %lengths_ref.9, bf16[64,3072]{1,0:T(8,128)(2,1)} %text_ref.1, bf16[32,3072]{1,0:T(8,128)(2,1)} %image_ref.1, f32[8,2,2,3072]{3,2,1,0:T(2,128)} %mod_ref.1), custom_call_target="tpu_custom_call" | custom-call | tf_op jit(solution)/shard_map/hidden_rows/pallas_call | solution.py:141
  4.9 1.3 %collective-permute-start.4 = (bf16[96,3072]{1,0:T(8,128)(2,1)}, bf16[96,3072]{1,0:T(8,128)(2,1)S(1)}, u32[]{:S(2)}, u32[]{:S(2)}) collective-permute-start(bf16[96,3072]{1,0:T(8,128)(2,1)} %hidden_rows.1.refs_2_.refs_0_), channel_id=1, source_target_pairs={{1,3},{3,5},{5,7},{2,0},{4,2},{6,4},{9,11},{11,13},{13,15},{10,8},... | collective-permute-start | bytes 1769480 | tf_op jit(solution)/shard_map/ppermute | solution.py:586
  6.8 1.3 %collective-permute-start.8 = (bf16[96,3072]{1,0:T(8,128)(2,1)S(1)}, bf16[96,3072]{1,0:T(8,128)(2,1)S(1)}, u32[]{:S(2)}, u32[]{:S(2)}) collective-permute-start(bf16[96,3072]{1,0:T(8,128)(2,1)S(1)} %collective-permute-done.7.refs_3_.refs_1_), channel_id=1, source_target_pairs={{1,3},{3,5},{5,7},{2,0},{4,2},{6,4},{9,11},{11,13},{13,15},{10,8},... | collective-permute-start | bytes 1769480 | tf_op jit(solution)/shard_map/ppermute | solution.py:586
  8.1 9.5 %collective-permute-done.4.refs_4_.refs_2_ = bf16[96,3072]{1,0:T(8,128)(2,1)S(1)} collective-permute-done((bf16[96,3072]{1,0:T(8,128)(2,1)}, bf16[96,3072]{1,0:T(8,128)(2,1)S(1)}, u32[]{:S(2)}, u32[]{:S(2)}) %collective-permute-start.4) | collective-permute-done | bytes 589856 | tf_op jit(solution)/shard_map/ppermute | solution.py:586
  17.6 1.3 %collective-permute-start.5 = (bf16[96,3072]{1,0:T(8,128)(2,1)S(1)}, bf16[96,3072]{1,0:T(8,128)(2,1)S(1)}, u32[]{:S(2)}, u32[]{:S(2)}) collective-permute-start(bf16[96,3072]{1,0:T(8,128)(2,1)S(1)} %collective-permute-done.4.refs_4_.refs_2_), channel_id=1, source_target_pairs={{3,5},{5,7},{2,0},{4,2},{11,13},{13,15},{10,8},{12,10},{19,21},{21... | collective-permute-start | bytes 1769480 | tf_op jit(solution)/shard_map/ppermute | solution.py:586
  18.9 5.0 %collective-permute-done.8.refs_5_.refs_3_ = bf16[96,3072]{1,0:T(8,128)(2,1)S(1)} collective-permute-done((bf16[96,3072]{1,0:T(8,128)(2,1)S(1)}, bf16[96,3072]{1,0:T(8,128)(2,1)S(1)}, u32[]{:S(2)}, u32[]{:S(2)}) %collective-permute-start.8) | collective-permute-done | bytes 589856 | tf_op jit(solution)/shard_map/ppermute | solution.py:586
  23.9 1.3 %collective-permute-start.9 = (bf16[96,3072]{1,0:T(8,128)(2,1)S(1)}, bf16[96,3072]{1,0:T(8,128)(2,1)S(1)}, u32[]{:S(2)}, u32[]{:S(2)}) collective-permute-start(bf16[96,3072]{1,0:T(8,128)(2,1)S(1)} %collective-permute-done.8.refs_5_.refs_3_), channel_id=1, source_target_pairs={{3,5},{5,7},{2,0},{4,2},{11,13},{13,15},{10,8},{12,10},{19,21},{21... | collective-permute-start | bytes 1769480 | tf_op jit(solution)/shard_map/ppermute | solution.py:586
  25.2 3.2 %packed_adapters.1 = (bf16[64,768]{1,0:T(8,128)(2,1)}, bf16[64,768]{1,0:T(8,128)(2,1)}, bf16[64,768]{1,0:T(8,128)(2,1)}, bf16[64,768]{1,0:T(8,128)(2,1)}, bf16[1...) custom-call(s32[128]{0:T(128)} %store_row_ref.7, ...), custom_call_target="tpu_custom_call" | custom-call | tf_op jit(solution)/shard_map/packed_adapters/pallas_call | solution.py:183
  28.4 2.0 %collective-permute-start = (bf16[64,768]{1,0:T(8,128)(2,1)}, bf16[64,768]{1,0:T(8,128)(2,1)S(1)}, u32[]{:S(2)}, u32[]{:S(2)}) collective-permute-start(bf16[64,768]{1,0:T(8,128)(2,1)} %get-tuple-element.21), channel_id=1, source_target_pairs={{0,8},{8,0},{16,24},{24,16},{1,9},{9,1},{17,25},{25,17},{2,10},{10... | collective-permute-start | bytes 294920 | tf_op jit(solution)/shard_map/ppermute | solution.py:598
  30.4 1.5 %collective-permute-start.1 = (bf16[64,768]{1,0:T(8,128)(2,1)}, bf16[64,768]{1,0:T(8,128)(2,1)S(1)}, u32[]{:S(2)}, u32[]{:S(2)}) collective-permute-start(bf16[64,768]{1,0:T(8,128)(2,1)} %get-tuple-element.22), channel_id=1, source_target_pairs={{0,16},{8,24},{16,0},{24,8},{1,17},{9,25},{17,1},{25,9},{2,18},{10... | collective-permute-start | bytes 294920 | tf_op jit(solution)/shard_map/ppermute | solution.py:598
  32.0 2.3 %collective-permute-done = bf16[64,768]{1,0:T(8,128)(2,1)S(1)} collective-permute-done((bf16[64,768]{1,0:T(8,128)(2,1)}, bf16[64,768]{1,0:T(8,128)(2,1)S(1)}, u32[]{:S(2)}, u32[]{:S(2)}) %collective-permute-start) | collective-permute-done | bytes 98336 | tf_op jit(solution)/shard_map/ppermute | solution.py:598
  34.3 1.2 %collective-permute-done.1 = bf16[64,768]{1,0:T(8,128)(2,1)S(1)} collective-permute-done((bf16[64,768]{1,0:T(8,128)(2,1)}, bf16[64,768]{1,0:T(8,128)(2,1)S(1)}, u32[]{:S(2)}, u32[]{:S(2)}) %collective-permute-start.1) | collective-permute-done | bytes 98336 | tf_op jit(solution)/shard_map/ppermute | solution.py:598
  35.5 2.2 %collective-permute-done.2 = bf16[64,768]{1,0:T(8,128)(2,1)S(1)} collective-permute-done((bf16[64,768]{1,0:T(8,128)(2,1)}, bf16[64,768]{1,0:T(8,128)(2,1)S(1)}, u32[]{:S(2)}, u32[]{:S(2)}) %collective-permute-start.2) | collective-permute-done | bytes 98336 | tf_op jit(solution)/shard_map/ppermute | solution.py:598
  37.7 0.9 pad_maximum_fusion.refs_0_
  38.6 4.6 %collective-permute-start.3 = (bf16[4,64,768]{2,1,0:T(8,128)(2,1)S(1)}, bf16[4,64,768]{2,1,0:T(8,128)(2,1)S(1)}, u32[]{:S(2)}, u32[]{:S(2)}) collective-permute-start(bf16[4,64,768]{2,1,0:T(8,128)(2,1)S(1)} %pad_maximum_fusion.refs_0_), channel_id=1, source_target_pairs={{0,2},{1,3},{6,4},{7,5},{8,10},{9,11},{14,12},{15,13},{16,18},{17,... | collective-permute-start | bytes 1179656 | tf_op jit(solution)/shard_map/ppermute | solution.py:605
  43.8 6.5 %collective-permute-done.3.refs_1_ = bf16[4,64,768]{2,1,0:T(8,128)(2,1)S(1)} collective-permute-done((bf16[4,64,768]{2,1,0:T(8,128)(2,1)S(1)}, bf16[4,64,768]{2,1,0:T(8,128)(2,1)S(1)}, u32[]{:S(2)}, u32[]{:S(2)}) %collective-permute-start.3) | collective-permute-done | bytes 393248 | tf_op jit(solution)/shard_map/ppermute | solution.py:605
  50.3 1.3 %collective-permute-start.19 = (bf16[96,3072]{1,0:T(8,128)(2,1)S(1)}, bf16[96,3072]{1,0:T(8,128)(2,1)S(1)}, u32[]{:S(2)}, u32[]{:S(2)}) collective-permute-start(bf16[96,3072]{1,0:T(8,128)(2,1)S(1)} %collective-permute-done.5.refs_2_.refs_0_), channel_id=1, source_target_pairs={{5,7},{2,0},{13,15},{10,8},{21,23},{18,16},{29,31},{26,24}} | collective-permute-start | bytes 1769480 | tf_op jit(solution)/shard_map/ppermute | solution.py:586
  51.6 1.3 %collective-permute-start.21 = (bf16[96,3072]{1,0:T(8,128)(2,1)S(1)}, bf16[96,3072]{1,0:T(8,128)(2,1)S(1)}, u32[]{:S(2)}, u32[]{:S(2)}) collective-permute-start(bf16[96,3072]{1,0:T(8,128)(2,1)S(1)} %collective-permute-done.9.refs_4_.refs_2_), channel_id=1, source_target_pairs={{5,7},{2,0},{13,15},{10,8},{21,23},{18,16},{29,31},{26,24}} | collective-permute-start | bytes 1769480 | tf_op jit(solution)/shard_map/ppermute | solution.py:586
  53.0 4.4 %rank_parts.2.refs_6_ = bf16[2,8,8,128]{3,2,1,0:T(8,128)(2,1)S(1)} custom-call(s32[1,4]{1,0:T(1,128)S(1)} %copy-done.5, s32[128]{0:T(128)S(1)} %copy-done.7, s32[4,4]{1,0:T(4,128)S(1)} %copy-done.4, bf16[4,64,768]{2,1,0:T(8,128)(2,1)S(1)} %pad_maximum_fusion.refs_0_, bf16[4,64,768]{2,1,0:T(8,128)(2,1)S(1)} %collective-permute-done.3.refs_1_, ...), custom_call_target="tpu_custom_call" | custom-call | flops 905969664 | bytes 3538944 | tf_op jit(solution)/shard_map/rank_parts/pallas_call | solution.py:304
  57.4 1.8 %rank_parts.3 = bf16[2,8,8,128]{3,2,1,0:T(8,128)(2,1)S(1)} custom-call(s32[1,4]{1,0:T(1,128)S(1)} %copy-done.5, s32[128]{0:T(128)S(1)} %copy-done.7, s32[4,4]{1,0:T(4,128)S(1)} %copy-done.4, bf16[4,64,768]{2,1,0:T(8,128)(2,1)S(1)} %pad_maximum_fusion.refs_0_, bf16[4,64,768]{2,1,0:T(8,128)(2,1)S(1)} %collective-permute-done.3.refs_1_, ...), custom_call_target="tpu_custom_call" | custom-call | flops 603979776 | bytes 2359296 | tf_op jit(solution)/shard_map/rank_parts/pallas_call | solution.py:304
  59.3 2.0 %collective-permute-start.16 = (bf16[128,768]{1,0:T(8,128)(2,1)S(1)}, bf16[128,768]{1,0:T(8,128)(2,1)S(1)}, u32[]{:S(2)}, u32[]{:S(2)}) collective-permute-start(bf16[128,768]{1,0:T(8,128)(2,1)S(1)} %copy-done.10), channel_id=1, source_target_pairs={{0,8},{8,0},{16,24},{24,16},{1,9},{9,1},{17,25},{25,17},{2,10},{10... | collective-permute-start | bytes 589832 | tf_op jit(solution)/shard_map/ppermute | solution.py:598
  62.3 6.2 %collective-permute-done.21.refs_2_ = bf16[96,3072]{1,0:T(8,128)(2,1)S(1)} collective-permute-done((bf16[96,3072]{1,0:T(8,128)(2,1)S(1)}, bf16[96,3072]{1,0:T(8,128)(2,1)S(1)}, u32[]{:S(2)}, u32[]{:S(2)}) %collective-permute-start.21) | collective-permute-done | bytes 589856 | tf_op jit(solution)/shard_map/ppermute | solution.py:586
  68.4 2.0 %collective-permute-start.17 = (bf16[128,768]{1,0:T(8,128)(2,1)S(1)}, bf16[128,768]{1,0:T(8,128)(2,1)S(1)}, u32[]{:S(2)}, u32[]{:S(2)}) collective-permute-start(bf16[128,768]{1,0:T(8,128)(2,1)S(1)} %copy-done.9), channel_id=1, source_target_pairs={{0,16},{8,24},{16,0},{24,8},{1,17},{9,25},{17,1},{25,9},{2,18},{10... | collective-permute-start | bytes 589832 | tf_op jit(solution)/shard_map/ppermute | solution.py:598
  70.4 1.5 %collective-permute-start.18 = (bf16[128,768]{1,0:T(8,128)(2,1)S(1)}, bf16[128,768]{1,0:T(8,128)(2,1)S(1)}, u32[]{:S(2)}, u32[]{:S(2)}) collective-permute-start(bf16[128,768]{1,0:T(8,128)(2,1)S(1)} %copy-done.8), channel_id=1, source_target_pairs={{0,24},{8,16},{16,8},{24,0},{1,25},{9,17},{17,9},{25,1},{2,26},{10... | collective-permute-start | bytes 589832 | tf_op jit(solution)/shard_map/ppermute | solution.py:598
  71.9 1.3 %collective-permute-start.15 = (bf16[2,2,2,8,8,128]{5,4,3,2,1,0:T(8,128)(2,1)S(1)}, bf16[2,2,2,8,8,128]{5,4,3,2,1,0:T(8,128)(2,1)S(1)}, u32[]{:S(2)}, u32[]{:S(2)}) collective-permute-start(bf16[2,2,2,8,8,128]{5,4,3,2,1,0:T(8,128)(2,1)S(1)} %pad_maximum_fusion.1.refs_0_), channel_id=1, source_target_pairs={{2,0},{3,1},{4,6},{5,7},{10,8},{11,9},{12,14},{13,15},{18,16},{19,... | collective-permute-start | bytes 393224 | tf_op jit(solution)/shard_map/ppermute | solution.py:624
  73.2 3.7 %copy-done = bf16[2,3072,768]{2,1,0:T(8,128)(2,1)S(1)} copy-done((bf16[2,3072,768]{2,1,0:T(8,128)(2,1)S(1)}, bf16[2,3072,768]{2,1,0:T(8,128)(2,1)}, u32[]{:S(2)}) %copy-start) | copy-done | bytes 9437208
  76.9 3.0 %shard_map.113 = (f32[384,768]{1,0:T(8,128)S(1)}, f32[192,768]{1,0:T(8,128)S(1)}) custom-call(bf16[96,3072]{1,0:T(8,128)(2,1)S(1)} %copy-done.2, bf16[96,3072]{1,0:T(8,128)(2,1)S(1)} %collective-permute-done.7.refs_3_.refs_1_, bf16[96,3072]{1,0:T(8,128)(2,1)S(1)} %collective-permute-done.4.refs_4_.refs_2_, ...), custom_call_target="tpu_custom_call" | custom-call | flops 2717908992 | bytes 3538944 | tf_op jit(solution)/shard_map/pallas_call | solution.py:229
  80.6 1.7 %shard_map.114 = (f32[128,768]{1,0:T(8,128)S(1)}, f32[64,768]{1,0:T(8,128)S(1)}) custom-call(bf16[96,3072]{1,0:T(8,128)(2,1)S(1)} %collective-permute-done.5.refs_2_.refs_0_, bf16[96,3072]{1,0:T(8,128)(2,1)S(1)} %collective-permute-done.6.refs_3_.refs_1_, bf16[96,3072]{1,0:T(8,128)(2,1)S(1)} %collective-permute-done.9.refs_4_.refs_2_, ...), custom_call_target="tpu_custom_call" | custom-call | flops 905969664 | bytes 1179648 | tf_op jit(solution)/shard_map/pallas_call | solution.py:229
  82.3 3.3 %early_heads.1 = (bf16[3,512,256]{2,1,0:T(8,128)(2,1)S(1)}, bf16[3,256,256]{2,1,0:T(8,128)(2,1)S(1)}, f32[128,768]{1,0:T(8,128)S(1)}, f32[64,768]{1,0:T(8,128)S(1)}) custom-call(s32[1,4]{1,0:T(1,128)S(1)} %copy-done.5, s32[128]{0:T(128)S(1)} %copy-done.7, s32[4,4]{1,0:T(4,128)S(1)} %copy-done.4, f32[2,2,128]{2,1,0:T(2,128)S(1)} %copy-done.6, ...), custom_call_target="tpu_custom_call" | custom-call | flops 805306368 | bytes 4718592 | tf_op jit(solution)/shard_map/early_heads/pallas_call | solution.py:409
  85.7 1.9 %shard_map.115 = (f32[128,768]{1,0:T(8,128)S(1)}, f32[64,768]{1,0:T(8,128)S(1)}) custom-call(bf16[96,3072]{1,0:T(8,128)(2,1)S(1)} %collective-permute-done.19.refs_0_, bf16[96,3072]{1,0:T(8,128)(2,1)S(1)} %collective-permute-done.20.refs_1_, bf16[96,3072]{1,0:T(8,128)(2,1)S(1)} %collective-permute-done.21.refs_2_, ...), custom_call_target="tpu_custom_call" | custom-call | flops 905969664 | bytes 1179648 | tf_op jit(solution)/shard_map/pallas_call | solution.py:229
  87.6 7.5 %attention.1 = bf16[8,96,256]{2,1,0:T(8,128)(2,1)S(1)} custom-call(s32[1,4]{1,0:T(1,128)S(1)} %copy-done.5, f32[2,2,128]{2,1,0:T(2,128)S(1)} %copy-done.6, bf16[3,512,256]{2,1,0:T(8,128)(2,1)S(1)} %get-tuple-element.32.refs_0_, bf16[3,256,256]{2,1,0:T(8,128)(2,1)S(1)} %get-tuple-element.33.refs_1_, f32[128,768]{1,0:T(8,128)S(1)} %get-tuple-element.34.refs_2_, ...), custom_call_target="tpu_custom_call" | custom-call | tf_op jit(solution)/shard_map/attention/pallas_call | solution.py:517
  95.1 16.3 %all_to_all.5.pieces = bf16[8,96,256]{2,1,0:T(8,128)(2,1)S(1)} all-to-all(bf16[8,96,256]{2,1,0:T(8,128)(2,1)S(1)} %attention.1), channel_id=1, replica_groups=mesh['bag'=4,'seq'=8] {'seq'}, dimensions={0} | all-to-all | bytes 786432 | tf_op jit(solution)/shard_map/all_to_all | solution.py:640
  (50 shorter events, 4.3 us)
Async XLA Ops:
  0.6 52.3 %copy-start.5 = (s32[1,4]{1,0:T(1,128)S(1)}, s32[1,4]{1,0:T(1,128)}, u32[]{:S(2)}) copy-start(s32[1,4]{1,0:T(1,128)} %lengths_ref.9) | copy-start | bytes 52
  0.6 52.3 %copy-start.7 = (s32[128]{0:T(128)S(1)}, s32[128]{0:T(128)}, u32[]{:S(2)}) copy-start(s32[128]{0:T(128)} %store_row_ref.7) | copy-start | bytes 1540
  0.7 52.3 %copy-start.4 = (s32[4,4]{1,0:T(4,128)S(1)}, s32[4,4]{1,0:T(4,128)}, u32[]{:S(2)}) copy-start(s32[4,4]{1,0:T(4,128)} %adapter_ref.7) | copy-start | bytes 196
  4.4 48.5 %copy-start.2 = (bf16[96,3072]{1,0:T(8,128)(2,1)S(1)}, bf16[96,3072]{1,0:T(8,128)(2,1)}, u32[]{:S(2)}) copy-start(bf16[96,3072]{1,0:T(8,128)(2,1)} %hidden_rows.1.refs_2_.refs_0_) | copy-start | bytes 1769476
  4.4 2.3 %collective-permute-start.7 = (bf16[96,3072]{1,0:T(8,128)(2,1)}, bf16[96,3072]{1,0:T(8,128)(2,1)S(1)}, u32[]{:S(2)}, u32[]{:S(2)}) collective-permute-start(bf16[96,3072]{1,0:T(8,128)(2,1)} %hidden_rows.1.refs_2_.refs_0_), channel_id=1, source_target_pairs={{0,1},{1,0},{2,3},{3,2},{4,5},{5,4},{6,7},{7,6},{8,9},{9,8},{10,11... | collective-permute-start | bytes 1769480 | tf_op jit(solution)/shard_map/ppermute | solution.py:580
  4.9 12.7 %collective-permute-start.4 = (bf16[96,3072]{1,0:T(8,128)(2,1)}, bf16[96,3072]{1,0:T(8,128)(2,1)S(1)}, u32[]{:S(2)}, u32[]{:S(2)}) collective-permute-start(bf16[96,3072]{1,0:T(8,128)(2,1)} %hidden_rows.1.refs_2_.refs_0_), channel_id=1, source_target_pairs={{1,3},{3,5},{5,7},{2,0},{4,2},{6,4},{9,11},{11,13},{13,15},{10,8},... | collective-permute-start | bytes 1769480 | tf_op jit(solution)/shard_map/ppermute | solution.py:586
  6.8 17.1 %collective-permute-start.8 = (bf16[96,3072]{1,0:T(8,128)(2,1)S(1)}, bf16[96,3072]{1,0:T(8,128)(2,1)S(1)}, u32[]{:S(2)}, u32[]{:S(2)}) collective-permute-start(bf16[96,3072]{1,0:T(8,128)(2,1)S(1)} %collective-permute-done.7.refs_3_.refs_1_), channel_id=1, source_target_pairs={{1,3},{3,5},{5,7},{2,0},{4,2},{6,4},{9,11},{11,13},{13,15},{10,8},... | collective-permute-start | bytes 1769480 | tf_op jit(solution)/shard_map/ppermute | solution.py:586
  17.6 25.6 %collective-permute-start.5 = (bf16[96,3072]{1,0:T(8,128)(2,1)S(1)}, bf16[96,3072]{1,0:T(8,128)(2,1)S(1)}, u32[]{:S(2)}, u32[]{:S(2)}) collective-permute-start(bf16[96,3072]{1,0:T(8,128)(2,1)S(1)} %collective-permute-done.4.refs_4_.refs_2_), channel_id=1, source_target_pairs={{3,5},{5,7},{2,0},{4,2},{11,13},{13,15},{10,8},{12,10},{19,21},{21... | collective-permute-start | bytes 1769480 | tf_op jit(solution)/shard_map/ppermute | solution.py:586
  23.9 19.8 %collective-permute-start.9 = (bf16[96,3072]{1,0:T(8,128)(2,1)S(1)}, bf16[96,3072]{1,0:T(8,128)(2,1)S(1)}, u32[]{:S(2)}, u32[]{:S(2)}) collective-permute-start(bf16[96,3072]{1,0:T(8,128)(2,1)S(1)} %collective-permute-done.8.refs_5_.refs_3_), channel_id=1, source_target_pairs={{3,5},{5,7},{2,0},{4,2},{11,13},{13,15},{10,8},{12,10},{19,21},{21... | collective-permute-start | bytes 1769480 | tf_op jit(solution)/shard_map/ppermute | solution.py:586
  28.4 30.9 %copy-start.10 = (bf16[128,768]{1,0:T(8,128)(2,1)S(1)}, bf16[128,768]{1,0:T(8,128)(2,1)}, u32[]{:S(2)}) copy-start(bf16[128,768]{1,0:T(8,128)(2,1)} %get-tuple-element.25) | copy-start | bytes 589828
  28.4 40.0 %copy-start.9 = (bf16[128,768]{1,0:T(8,128)(2,1)S(1)}, bf16[128,768]{1,0:T(8,128)(2,1)}, u32[]{:S(2)}) copy-start(bf16[128,768]{1,0:T(8,128)(2,1)} %get-tuple-element.26) | copy-start | bytes 589828
  28.4 42.0 %copy-start.8 = (bf16[128,768]{1,0:T(8,128)(2,1)S(1)}, bf16[128,768]{1,0:T(8,128)(2,1)}, u32[]{:S(2)}) copy-start(bf16[128,768]{1,0:T(8,128)(2,1)} %get-tuple-element.27) | copy-start | bytes 589828
  28.4 5.8 %collective-permute-start = (bf16[64,768]{1,0:T(8,128)(2,1)}, bf16[64,768]{1,0:T(8,128)(2,1)S(1)}, u32[]{:S(2)}, u32[]{:S(2)}) collective-permute-start(bf16[64,768]{1,0:T(8,128)(2,1)} %get-tuple-element.21), channel_id=1, source_target_pairs={{0,8},{8,0},{16,24},{24,16},{1,9},{9,1},{17,25},{25,17},{2,10},{10... | collective-permute-start | bytes 294920 | tf_op jit(solution)/shard_map/ppermute | solution.py:598
  30.4 5.1 %collective-permute-start.1 = (bf16[64,768]{1,0:T(8,128)(2,1)}, bf16[64,768]{1,0:T(8,128)(2,1)S(1)}, u32[]{:S(2)}, u32[]{:S(2)}) collective-permute-start(bf16[64,768]{1,0:T(8,128)(2,1)} %get-tuple-element.22), channel_id=1, source_target_pairs={{0,16},{8,24},{16,0},{24,8},{1,17},{9,25},{17,1},{25,9},{2,18},{10... | collective-permute-start | bytes 294920 | tf_op jit(solution)/shard_map/ppermute | solution.py:598
  31.9 5.7 %collective-permute-start.2 = (bf16[64,768]{1,0:T(8,128)(2,1)}, bf16[64,768]{1,0:T(8,128)(2,1)S(1)}, u32[]{:S(2)}, u32[]{:S(2)}) collective-permute-start(bf16[64,768]{1,0:T(8,128)(2,1)} %get-tuple-element.23), channel_id=1, source_target_pairs={{0,24},{8,16},{16,8},{24,0},{1,25},{9,17},{17,9},{25,1},{2,26},{10... | collective-permute-start | bytes 294920 | tf_op jit(solution)/shard_map/ppermute | solution.py:598
  34.2 17.4 %collective-permute-start.11 = (bf16[96,3072]{1,0:T(8,128)(2,1)S(1)}, bf16[96,3072]{1,0:T(8,128)(2,1)S(1)}, u32[]{:S(2)}, u32[]{:S(2)}) collective-permute-start(bf16[96,3072]{1,0:T(8,128)(2,1)S(1)} %collective-permute-done.4.refs_4_.refs_2_), channel_id=1, source_target_pairs={{0,1},{1,0},{2,3},{3,2},{4,5},{5,4},{6,7},{7,6},{8,9},{9,8},{10,11... | collective-permute-start | bytes 1769480 | tf_op jit(solution)/shard_map/ppermute | solution.py:587
  38.6 11.8 %collective-permute-start.3 = (bf16[4,64,768]{2,1,0:T(8,128)(2,1)S(1)}, bf16[4,64,768]{2,1,0:T(8,128)(2,1)S(1)}, u32[]{:S(2)}, u32[]{:S(2)}) collective-permute-start(bf16[4,64,768]{2,1,0:T(8,128)(2,1)S(1)} %pad_maximum_fusion.refs_0_), channel_id=1, source_target_pairs={{0,2},{1,3},{6,4},{7,5},{8,10},{9,11},{14,12},{15,13},{16,18},{17,... | collective-permute-start | bytes 1179656 | tf_op jit(solution)/shard_map/ppermute | solution.py:605
  43.2 9.8 %collective-permute-start.12 = (bf16[96,3072]{1,0:T(8,128)(2,1)S(1)}, bf16[96,3072]{1,0:T(8,128)(2,1)S(1)}, u32[]{:S(2)}, u32[]{:S(2)}) collective-permute-start(bf16[96,3072]{1,0:T(8,128)(2,1)S(1)} %collective-permute-done.8.refs_5_.refs_3_), channel_id=1, source_target_pairs={{0,1},{1,0},{2,3},{3,2},{4,5},{5,4},{6,7},{7,6},{8,9},{9,8},{10,11... | collective-permute-start | bytes 1769480 | tf_op jit(solution)/shard_map/ppermute | solution.py:587
  43.2 14.1 %collective-permute-start.6 = (bf16[96,3072]{1,0:T(8,128)(2,1)S(1)}, bf16[96,3072]{1,0:T(8,128)(2,1)S(1)}, u32[]{:S(2)}, u32[]{:S(2)}) collective-permute-start(bf16[96,3072]{1,0:T(8,128)(2,1)S(1)} %collective-permute-done.5.refs_2_.refs_0_), channel_id=1, source_target_pairs={{0,1},{1,0},{2,3},{3,2},{4,5},{5,4},{6,7},{7,6},{8,9},{9,8},{10,11... | collective-permute-start | bytes 1769480 | tf_op jit(solution)/shard_map/ppermute | solution.py:587
  43.7 13.6 %collective-permute-start.10 = (bf16[96,3072]{1,0:T(8,128)(2,1)S(1)}, bf16[96,3072]{1,0:T(8,128)(2,1)S(1)}, u32[]{:S(2)}, u32[]{:S(2)}) collective-permute-start(bf16[96,3072]{1,0:T(8,128)(2,1)S(1)} %collective-permute-done.9.refs_4_.refs_2_), channel_id=1, source_target_pairs={{0,1},{1,0},{2,3},{3,2},{4,5},{5,4},{6,7},{7,6},{8,9},{9,8},{10,11... | collective-permute-start | bytes 1769480 | tf_op jit(solution)/shard_map/ppermute | solution.py:587
  50.3 11.8 %collective-permute-start.19 = (bf16[96,3072]{1,0:T(8,128)(2,1)S(1)}, bf16[96,3072]{1,0:T(8,128)(2,1)S(1)}, u32[]{:S(2)}, u32[]{:S(2)}) collective-permute-start(bf16[96,3072]{1,0:T(8,128)(2,1)S(1)} %collective-permute-done.5.refs_2_.refs_0_), channel_id=1, source_target_pairs={{5,7},{2,0},{13,15},{10,8},{21,23},{18,16},{29,31},{26,24}} | collective-permute-start | bytes 1769480 | tf_op jit(solution)/shard_map/ppermute | solution.py:586
  51.6 16.8 %collective-permute-start.21 = (bf16[96,3072]{1,0:T(8,128)(2,1)S(1)}, bf16[96,3072]{1,0:T(8,128)(2,1)S(1)}, u32[]{:S(2)}, u32[]{:S(2)}) collective-permute-start(bf16[96,3072]{1,0:T(8,128)(2,1)S(1)} %collective-permute-done.9.refs_4_.refs_2_), channel_id=1, source_target_pairs={{5,7},{2,0},{13,15},{10,8},{21,23},{18,16},{29,31},{26,24}} | collective-permute-start | bytes 1769480 | tf_op jit(solution)/shard_map/ppermute | solution.py:586
  59.2 2.1 %collective-permute-start.13 = (bf16[2,8,8,128]{3,2,1,0:T(8,128)(2,1)S(1)}, bf16[2,8,8,128]{3,2,1,0:T(8,128)(2,1)S(1)}, u32[]{:S(2)}, u32[]{:S(2)}) collective-permute-start(bf16[2,8,8,128]{3,2,1,0:T(8,128)(2,1)S(1)} %rank_parts.3), channel_id=1, source_target_pairs={{0,1},{1,0},{2,3},{3,2},{4,5},{5,4},{6,7},{7,6},{8,9},{9,8},{10,11... | collective-permute-start | bytes 98312 | tf_op jit(solution)/shard_map/ppermute | solution.py:620
  59.3 12.6 %collective-permute-start.16 = (bf16[128,768]{1,0:T(8,128)(2,1)S(1)}, bf16[128,768]{1,0:T(8,128)(2,1)S(1)}, u32[]{:S(2)}, u32[]{:S(2)}) collective-permute-start(bf16[128,768]{1,0:T(8,128)(2,1)S(1)} %copy-done.10), channel_id=1, source_target_pairs={{0,8},{8,0},{16,24},{24,16},{1,9},{9,1},{17,25},{25,17},{2,10},{10... | collective-permute-start | bytes 589832 | tf_op jit(solution)/shard_map/ppermute | solution.py:598
  61.4 9.0 %collective-permute-start.14 = (bf16[2,2,8,8,128]{4,3,2,1,0:T(8,128)(2,1)S(1)}, bf16[2,2,8,8,128]{4,3,2,1,0:T(8,128)(2,1)S(1)}, u32[]{:S(2)}, u32[]{:S(2)}) collective-permute-start(bf16[2,2,8,8,128]{4,3,2,1,0:T(8,128)(2,1)S(1)} %get-tuple-element.39), channel_id=1, source_target_pairs={{2,4},{3,5},{4,2},{5,3},{10,12},{11,13},{12,10},{13,11},{18,20},{1... | collective-permute-start | bytes 196616 | tf_op jit(solution)/shard_map/ppermute | solution.py:621
  62.1 23.6 %collective-permute-start.20 = (bf16[96,3072]{1,0:T(8,128)(2,1)S(1)}, bf16[96,3072]{1,0:T(8,128)(2,1)S(1)}, u32[]{:S(2)}, u32[]{:S(2)}) collective-permute-start(bf16[96,3072]{1,0:T(8,128)(2,1)S(1)} %collective-permute-done.19.refs_0_), channel_id=1, source_target_pairs={{0,1},{1,0},{2,3},{3,2},{4,5},{5,4},{6,7},{7,6},{8,9},{9,8},{10,11... | collective-permute-start | bytes 1769480 | tf_op jit(solution)/shard_map/ppermute | solution.py:587
  68.4 17.2 %collective-permute-start.22 = (bf16[96,3072]{1,0:T(8,128)(2,1)S(1)}, bf16[96,3072]{1,0:T(8,128)(2,1)S(1)}, u32[]{:S(2)}, u32[]{:S(2)}) collective-permute-start(bf16[96,3072]{1,0:T(8,128)(2,1)S(1)} %collective-permute-done.21.refs_2_), channel_id=1, source_target_pairs={{0,1},{1,0},{2,3},{3,2},{4,5},{5,4},{6,7},{7,6},{8,9},{9,8},{10,11... | collective-permute-start | bytes 1769480 | tf_op jit(solution)/shard_map/ppermute | solution.py:587
  68.4 13.8 %collective-permute-start.17 = (bf16[128,768]{1,0:T(8,128)(2,1)S(1)}, bf16[128,768]{1,0:T(8,128)(2,1)S(1)}, u32[]{:S(2)}, u32[]{:S(2)}) collective-permute-start(bf16[128,768]{1,0:T(8,128)(2,1)S(1)} %copy-done.9), channel_id=1, source_target_pairs={{0,16},{8,24},{16,0},{24,8},{1,17},{9,25},{17,1},{25,9},{2,18},{10... | collective-permute-start | bytes 589832 | tf_op jit(solution)/shard_map/ppermute | solution.py:598
  70.4 11.8 %collective-permute-start.18 = (bf16[128,768]{1,0:T(8,128)(2,1)S(1)}, bf16[128,768]{1,0:T(8,128)(2,1)S(1)}, u32[]{:S(2)}, u32[]{:S(2)}) collective-permute-start(bf16[128,768]{1,0:T(8,128)(2,1)S(1)} %copy-done.8), channel_id=1, source_target_pairs={{0,24},{8,16},{16,8},{24,0},{1,25},{9,17},{17,9},{25,1},{2,26},{10... | collective-permute-start | bytes 589832 | tf_op jit(solution)/shard_map/ppermute | solution.py:598
  71.9 10.4 %collective-permute-start.15 = (bf16[2,2,2,8,8,128]{5,4,3,2,1,0:T(8,128)(2,1)S(1)}, bf16[2,2,2,8,8,128]{5,4,3,2,1,0:T(8,128)(2,1)S(1)}, u32[]{:S(2)}, u32[]{:S(2)}) collective-permute-start(bf16[2,2,2,8,8,128]{5,4,3,2,1,0:T(8,128)(2,1)S(1)} %pad_maximum_fusion.1.refs_0_), channel_id=1, source_target_pairs={{2,0},{3,1},{4,6},{5,7},{10,8},{11,9},{12,14},{13,15},{18,16},{19,... | collective-permute-start | bytes 393224 | tf_op jit(solution)/shard_map/ppermute | solution.py:624
  73.2 3.7 %copy-start = (bf16[2,3072,768]{2,1,0:T(8,128)(2,1)S(1)}, bf16[2,3072,768]{2,1,0:T(8,128)(2,1)}, u32[]{:S(2)}) copy-start(bf16[2,3072,768]{2,1,0:T(8,128)(2,1)} %refs_4_.3) | copy-start | bytes 28311556
  76.9 3.7 %copy-start.1 = (bf16[2,3072,768]{2,1,0:T(8,128)(2,1)S(1)}, bf16[2,3072,768]{2,1,0:T(8,128)(2,1)}, u32[]{:S(2)}) copy-start(bf16[2,3072,768]{2,1,0:T(8,128)(2,1)} %refs_4_.3) | copy-start | bytes 28311556
  (2 other events, 3.4 us)

commit v2 on v1

--- a/solution.py
+++ b/solution.py
@@ -22,7 +22,6 @@
 VMEM = functools.partial(pl.BlockSpec, memory_space=pltpu.VMEM)
 HBM = functools.partial(pl.BlockSpec, memory_space=pltpu.HBM)
 NT = (((1,), (1,)), ((), ()))
-TN = (((0,), (0,)), ((), ()))
 
 
 def round_up(value, step):
@@ -255,27 +254,32 @@
 
 def rank_kernel(plan, slots, lengths_ref, store_row_ref, adapter_ref, *refs):
     halves = CORES * len(slots)
-    downs, refs = refs[: plan.half], refs[plan.half :]
     each = refs_per_half(slots)
+    first = slots[0][0] == "own"
+    given = plan.half if first else 2
+    downs, refs = refs[:given], refs[given:]
     blocks, refs = refs[: each * halves], refs[each * halves :]
-    before, (out_ref, stacked) = refs[:-2], refs[-2:]
-    for one in before:
-        out_ref[...] = one[...]
+    if first:
+        out_ref, turned, stacked = refs
+    else:
+        (out_ref,), (turned, before) = refs, downs
+        out_ref[...] = before[...]
     bag, seq_index = lax.axis_index("bag"), lax.axis_index("seq")
     chip = seq_index // CORES
     passed = is_passed(plan, slots[0], seq_index)
     keys = user_keys(plan, bag, store_row_ref, adapter_ref)
     tall = plan.bags * plan.down_rows
-    for index, down_ref in enumerate(downs):
-        for part in range(plan.parts):
-            lanes = slice(part * plan.cols, (part + 1) * plan.cols)
-            stacked[index * tall : (index + 1) * tall, lanes] = down_ref[part]
+    for part in range(plan.parts if first else 0):
+        lanes = slice(part * plan.cols, (part + 1) * plan.cols)
+        for index, down_ref in enumerate(downs):
+            stacked[index * tall : (index + 1) * tall, :] = down_ref[part].astype(jnp.float32)
+        turned[lanes, :] = jnp.transpose(stacked[...]).astype(jnp.bfloat16)
     for at in range(halves):
         place, valid = place_of(plan, slots[at // CORES], at % CORES, seq_index)
         block = blocks[each * at][...]
         if each > 1:
             block = jnp.where(passed, block, blocks[each * at + 1][...])
-        found = lax.dot_general(block, stacked[...], NT, preferred_element_type=jnp.float32)
+        found = jnp.dot(block, turned[...], preferred_element_type=jnp.float32)
         found = jnp.transpose(found)
         if plan.rows < plan.lanes:
             pad = jnp.zeros((found.shape[0], plan.lanes - plan.rows), jnp.float32)
@@ -297,26 +301,29 @@
                 out_ref[spot, place] = total.astype(jnp.bfloat16)
 
 
-def rank_parts(plan, slots, lengths, store_row, user_adapter, downs, blocks, before):
-    before = [] if before is None else [before]
-    each = plan.bags * plan.down_rows
-    rows = plan.rows * len(blocks)
+def rank_parts(plan, slots, lengths, store_row, user_adapter, downs, blocks):
+    first = slots[0][0] == "own"
+    tall = plan.half * plan.bags * plan.down_rows
+    rows = plan.rows * CORES * len(slots)
+    out_shape = [
+        jax.ShapeDtypeStruct((plan.half, plan.seq, plan.down_dev, plan.lanes), jnp.bfloat16)
+    ]
+    if first:
+        out_shape.append(jax.ShapeDtypeStruct((plan.width, tall), jnp.bfloat16))
     return pl.pallas_call(
         functools.partial(rank_kernel, plan, slots),
-        out_shape=jax.ShapeDtypeStruct(
-            (plan.half, plan.seq, plan.down_dev, plan.lanes), jnp.bfloat16
-        ),
-        in_specs=[SMEM()] * 3 + [VMEM()] * (len(downs) + len(blocks) + len(before)),
-        out_specs=VMEM(),
-        scratch_shapes=[pltpu.VMEM((len(downs) * each, plan.width), jnp.bfloat16)],
+        out_shape=out_shape,
+        in_specs=[SMEM()] * 3 + [VMEM()] * (len(downs) + len(blocks)),
+        out_specs=[VMEM()] * len(out_shape),
+        scratch_shapes=[pltpu.VMEM((tall, plan.cols), jnp.float32)] if first else [],
         compiler_params=PARAMS,
         cost_estimate=pl.CostEstimate(
-            flops=4 * rows * plan.width * len(downs) * each,
+            flops=(64 if first else 1) * rows * plan.width * tall,
             bytes_accessed=2 * rows * plan.width,
             transcendentals=0,
         ),
         name="rank_parts",
-    )(lengths, store_row, user_adapter, *downs, *blocks, *before)
+    )(lengths, store_row, user_adapter, *downs, *blocks)
 
 
 def head_normed(values, gain_row):
@@ -336,49 +343,58 @@
 
 
 def early_kernel(plan, groups, lengths_ref, store_row_ref, adapter_ref, gain_ref, *refs):
-    ranks, refs = refs[: plan.half], refs[plan.half :]
+    ranks, refs = refs[: 2 * plan.half + 1], refs[2 * plan.half + 1 :]
     packs, refs = refs[: plan.bags], refs[plan.bags :]
     plains, refs = refs[: 2 * len(groups)], refs[2 * len(groups) :]
-    text_heads, image_heads, text_last, image_last, ranks_ref, spread, ups, adjust = refs
+    text_heads, image_heads, text_last, image_last, ranks_ref, spread, text_side, image_side, ups, adjust = refs
+    sides = (text_side, image_side)
     bag, seq_index = lax.axis_index("bag"), lax.axis_index("seq")
     chip, core = seq_index // CORES, seq_index % CORES
-    upper = (chip >= plan.half).astype(jnp.int32)
-    reach = jnp.where(chip < plan.half, plan.half - 1 - chip, chip - plan.half)
-    for hop in range(plan.half):
-
-        @pl.when(reach == hop)
-        def _():
-            ranks_ref[...] = ranks[hop][...]
+    leads = []
+    for side, middle in enumerate((plan.half - 1, plan.half)):
+        away = jnp.abs(chip - middle)
+        sender = jnp.where(away == 0, core, (chip > middle).astype(jnp.int32))
+        leads.append(sender)
+        for at, source in enumerate(ranks):
+            hop = at if at <= plan.half else at - plan.half
+            here = (away == hop) & ((sender == core) if at <= plan.half else (sender != core))
+
+            @pl.when(here)
+            def _():
+                ranks_ref[side] = source[...]
 
     keys = user_keys(plan, bag, store_row_ref, adapter_ref)
     for place in range(plan.seq):
         key, _ = lane_keys(plan, lengths_ref, keys, place)
-        lanes = slice(place * plan.lanes, (place + 1) * plan.lanes)
         for side in range(2):
             for lead in range(CORES):
                 for index in range(plan.half):
                     rows = ranks_ref[
-                        lax.bitwise_xor(upper, side), lax.bitwise_xor(core, lead), index, place
+                        side, lax.bitwise_xor(leads[side], lead), index, place
                     ].astype(jnp.float32)
                     first = ((side * plan.half + index) * CORES + lead) * plan.down_dev
                     for hop in range(plan.bags):
                         top = hop * plan.rank + first
-                        spread[top : top + plan.down_dev, lanes] = jnp.where(key == hop, rows, 0.0)
+                        spread[place, top : top + plan.down_dev, :] = jnp.where(
+                            key == hop, rows, 0.0
+                        )
+        turned = jnp.transpose(spread[place]).astype(jnp.bfloat16)
+        for stream, size, skip in ((0, plan.text_dev, 0), (1, plan.image_dev, plan.text_dev)):
+            sides[stream][place * size : (place + 1) * size, :] = turned[skip : skip + size, :]
     for stream in range(2):
         for hop in range(plan.bags):
             ups[hop * plan.rank : (hop + 1) * plan.rank, :] = packs[hop][
                 stream * plan.rank : (stream + 1) * plan.rank, :
             ]
-        adjust[...] = lax.dot_general(
-            spread[...].astype(jnp.bfloat16), ups[...], TN, preferred_element_type=jnp.float32
+        size = plan.text_dev if stream == 0 else plan.image_dev
+        adjust[: plan.seq * size, :] = jnp.dot(
+            sides[stream][...], ups[...], preferred_element_type=jnp.float32
         )
-        size = plan.text_dev if stream == 0 else plan.image_dev
-        skip = 0 if stream == 0 else plan.text_dev
         out_ref = text_heads if stream == 0 else image_heads
         last_ref = text_last if stream == 0 else image_last
 
         def rows_of(place):
-            return pl.ds(pl.multiple_of(place * plan.lanes + skip, 32), size)
+            return pl.ds(pl.multiple_of(place * size, size), size)
 
         for group_at, group in enumerate(groups):
             plain = plains[2 * group_at + stream]
@@ -410,13 +426,15 @@
         functools.partial(early_kernel, plan, groups),
         out_shape=tuple(jax.ShapeDtypeStruct((3, n, plan.wide), jnp.bfloat16) for n in total)
         + tuple(jax.ShapeDtypeStruct((n, plan.cols), jnp.float32) for n in last),
-        in_specs=[SMEM()] * 3 + [VMEM()] * (1 + plan.half + plan.bags + len(plains)),
+        in_specs=[SMEM()] * 3 + [VMEM()] * (1 + len(ranks) + plan.bags + len(plains)),
         out_specs=(VMEM(),) * 4,
         scratch_shapes=[
-            pltpu.VMEM(ranks[0].shape, jnp.bfloat16),
-            pltpu.VMEM((plan.bags * plan.rank, plan.seq * plan.lanes), jnp.float32),
+            pltpu.VMEM((2,) + ranks[0].shape, jnp.bfloat16),
+            pltpu.VMEM((plan.seq, plan.bags * plan.rank, plan.lanes), jnp.float32),
+            pltpu.VMEM((total[0], plan.bags * plan.rank), jnp.bfloat16),
+            pltpu.VMEM((total[1], plan.bags * plan.rank), jnp.bfloat16),
             pltpu.VMEM((plan.bags * plan.rank, plan.cols), jnp.bfloat16),
-            pltpu.VMEM((plan.seq * plan.lanes, plan.cols), jnp.float32),
+            pltpu.VMEM((total[0], plan.cols), jnp.float32),
         ],
         compiler_params=pltpu.CompilerParams(vmem_limit_bytes=max(VMEM_GRANT, 2 * scratch)),
         cost_estimate=pl.CostEstimate(
@@ -432,7 +450,7 @@
     text_in, image_in, text_plain, image_plain, text_adjust, image_adjust = refs[:6]
     out_ref, text_heads, image_heads = refs[6:]
     seq_index = lax.axis_index("seq")
-    factor = 1.0 / math.sqrt(HEAD_DIM)
+    factor = math.log2(math.e) / math.sqrt(HEAD_DIM)
     text_heads[...] = text_in[...]
     image_heads[...] = image_in[...]
     for stream in range(2):
@@ -460,56 +478,50 @@
     image_cols = image_seg(lax.broadcasted_iota(jnp.int32, (1, image_total), 1))
     image_rows = image_seg(lax.broadcasted_iota(jnp.int32, (image_total, 1), 0))
     step = TEXT
-
-    def softmax(scores, hits):
-        scores = [jnp.where(hit, one * factor, -1e30) for one, hit in zip(scores, hits)]
+    segs = text_total // step
+    hits = (image_rows == image_cols, image_rows == text_cols)
+    image_bias = [jnp.where(hit, 0.0, -1e30) for hit in hits]
+    text_bias = [jnp.where(image_cols == seg, 0.0, -1e30) for seg in range(segs)]
+    text_bias = jnp.concatenate(
+        [jnp.broadcast_to(one, (step, image_total)) for one in text_bias], axis=0
+    )
+
+    def pair(queries, keys):
+        return lax.dot_general(queries, keys, NT, preferred_element_type=jnp.float32)
+
+    def softmax(scores):
         tops = [jnp.max(one, axis=1, keepdims=True) for one in scores]
         top = functools.reduce(jnp.maximum, tops)
-        weights = [jnp.exp(one - top) for one in scores]
+        weights = [jnp.exp2(one - top) for one in scores]
         total = sum(jnp.sum(one, axis=1, keepdims=True) for one in weights)
         inverse = 1.0 / total
         return [(one * inverse).astype(jnp.bfloat16) for one in weights]
 
-    def pair(queries, keys):
-        return lax.dot_general(queries, keys, NT, preferred_element_type=jnp.float32)
-
     def mix(probs, values):
-        found = [
-            jnp.dot(one, value, preferred_element_type=jnp.float32)
-            for one, value in zip(probs, values)
-        ]
-        return sum(found).astype(jnp.bfloat16)
+        return jnp.dot(probs, values, preferred_element_type=jnp.float32)
 
     for head in range(plan.heads):
         lanes = slice(head * HEAD_DIM, (head + 1) * HEAD_DIM)
-        image_keys, image_values = image_heads[1, :, lanes], image_heads[2, :, lanes]
-        for seg in range(text_total // step):
-            rows = slice(seg * step, (seg + 1) * step)
-            queries = text_heads[0, rows, lanes]
-            near = pair(queries, text_heads[1, rows, lanes]) * factor
-            far = pair(queries, image_keys)
-            far = jnp.where(image_cols == seg, far * factor, -1e30)
-            top = jnp.maximum(
-                jnp.max(near, axis=1, keepdims=True), jnp.max(far, axis=1, keepdims=True)
-            )
-            near, far = jnp.exp(near - top), jnp.exp(far - top)
-            total = jnp.sum(near, axis=1, keepdims=True) + jnp.sum(far, axis=1, keepdims=True)
-            inverse = 1.0 / total
-            probs = [(one * inverse).astype(jnp.bfloat16) for one in (near, far)]
-            place, inner = divmod(seg * step, plan.text_dev)
-            out_ref[place, inner : inner + step, lanes] = mix(
-                probs, (text_heads[2, rows, lanes], image_values)
-            )
-        queries = image_heads[0, :, lanes]
-        probs = softmax(
-            (pair(queries, image_keys), pair(queries, text_heads[1, :, lanes])),
-            (image_rows == image_cols, image_rows == text_cols),
+        text_q, text_k, text_v = (text_heads[which, :, lanes] for which in range(3))
+        image_q, image_k, image_v = (image_heads[which, :, lanes] for which in range(3))
+        spots = [slice(seg * step, (seg + 1) * step) for seg in range(segs)]
+        near = jnp.concatenate([pair(text_q[one], text_k[one]) for one in spots], axis=0)
+        near, far = softmax([near * factor, pair(text_q, image_k) * factor + text_bias])
+        own = jnp.concatenate([mix(near[one], text_v[one]) for one in spots], axis=0)
+        result = (own + mix(far, image_v)).astype(jnp.bfloat16)
+        for place in range(plan.seq):
+            rows = slice(place * plan.text_dev, (place + 1) * plan.text_dev)
+            out_ref[place, : plan.text_dev, lanes] = result[rows]
+        near, far = softmax(
+            [
+                pair(image_q, keys) * factor + bias
+                for keys, bias in zip((image_k, text_k), image_bias)
+            ]
         )
-        result = mix(probs, (image_values, text_heads[2, :, lanes]))
+        result = (mix(near, image_v) + mix(far, text_v)).astype(jnp.bfloat16)
         for place in range(plan.seq):
-            out_ref[place, plan.text_dev :, lanes] = result[
-                place * plan.image_dev : (place + 1) * plan.image_dev, :
-            ]
+            rows = slice(place * plan.image_dev, (place + 1) * plan.image_dev)
+            out_ref[place, plan.text_dev :, lanes] = result[rows]
 
 
 def attention(plan, lengths, norm_gain, arrays):
@@ -614,16 +626,18 @@
     for group in plan.groups:
         plains.append(project(plan, group, blocks_of(group), head_weight))
     scalars = (image_lengths, store_row, user_adapter)
-    ranks = None
-    for group in plan.groups[:2]:
-        ranks = rank_parts(plan, group, *scalars, downs, blocks_of(group), ranks)
-    ranks = jnp.stack([ranks, lax.ppermute(ranks, "seq", swap)])
-    other = lax.ppermute(ranks, "seq", plan.on_cores([(low, high), (high, low)]))
-    ranks = jnp.stack([ranks, other])
-    ranks = [ranks] + [
-        lax.ppermute(ranks, "seq", plan.on_cores([(low, low - hop), (high, high + hop)]))
-        for hop in range(1, plan.half)
-    ]
+    before, turned = rank_parts(plan, plan.groups[0], *scalars, downs, blocks_of(plan.groups[0]))
+    (ranks,) = rank_parts(
+        plan, plan.groups[1], *scalars, [turned, before], blocks_of(plan.groups[1])
+    )
+    ranks = [jnp.stack([ranks, lax.ppermute(ranks, "seq", swap)])]
+    for away in range(1, plan.half + 1):
+        pairs = []
+        for chip in (low, high):
+            pairs += [(2 * chip + 1, 2 * (chip + away) + 1)] * (chip + away < plan.chips)
+            pairs += [(2 * chip, 2 * (chip - away))] * (chip >= away)
+        ranks.append(lax.ppermute(ranks[0], "seq", pairs))
+    ranks += [lax.ppermute(ranks[away], "seq", swap) for away in range(1, plan.half + 1)]
 
     arrays = early_heads(
         plan,

time: 113 us -> 101 us (0.89)
  Pallas kernels: 31.3 us -> 24.9 us
  local copies, waits for them, and re-layouts: 4.44 us -> 0.05 us
  starting transfers between devices: 24.6 us -> 27.1 us
  waiting for transfers between devices: 33.6 us -> 31.6 us
  blocking collectives: 16.3 us -> 15.1 us
    ppermute x6, waiting for transfers between devices: 5.69 us -> 0.02 us  [steps(): lax.ppermute(sent[hop], 'bag', [(b, b ^ hop) for b in range(bags)])]
    unnamed x22 -> x20, local copies, waits for them, and re-layouts: 4.44 us -> 0.05 us
    pallas_call x1, Pallas kernels: 7.5 us -> 3.46 us  [attention(): pl.pallas_call(functools.partial(attend_kernel, plan), out_shape=jax.Shap...]
    ppermute x3 -> x5, waiting for transfers between devices: 0.01 us -> 3.59 us  [the longest x2 2.73 us: steps(): ranks.append(lax.ppermute(ranks[0], 'seq', pairs))]
    ppermute x1, waiting for transfers between devices: 6.52 us -> 8.2 us  [steps(): lax.ppermute(down_own, 'seq', plan.on_cores([(low - hop, low), (high + ho...]
    pallas_call x2, Pallas kernels: 6.2 us -> 4.57 us  [rank_parts(): pl.pallas_call(functools.partial(rank_kernel, plan, slots), out_shape=out...]
    ppermute x6, waiting for transfers between devices: 20.8 us -> 19.2 us  [steps(): passing[half] = lax.ppermute(passing[half], 'seq', up + down)]
    all_to_all x1, blocking collectives: 16.3 us -> 15.1 us  [steps(): lax.all_to_all(outs, 'seq', split_axis=0, concat_axis=0, tiled=True)]
  transfers between devices with their start and end apart: 23 -> 25, of which waited for: 9 -> 9; matrix products, arithmetic and copies ran while one was open for 1% -> 1% of each run, Pallas kernels for 15% -> 15%
where the time goes in v2:
time: 101 us
  waiting for transfers between devices  31.6 us (31%)
  starting transfers between devices  27.1 us (27%)
  Pallas kernels  24.9 us (25%)
  blocking collectives  15.1 us (15%)
    ppermute x6, waiting for transfers between devices, steps(): passing[half] = lax.ppermute(passing[half], 'seq', up + down)  19.2 us
    all_to_all x1, blocking collectives, steps(): lax.all_to_all(outs, 'seq', split_axis=0, concat_axis=0, tiled=True)  15.1 us
    ppermute x6, starting transfers between devices, steps(): lax.ppermute(sent[hop], 'bag', [(b, b ^ hop) for b in range(bags)])  10 us
    ppermute x1, waiting for transfers between devices, steps(): lax.ppermute(down_own, 'seq', plan.on_cores([(low - hop, low), (high + ho...  8.2 us
    ppermute x6, starting transfers between devices, steps(): passing[half] = lax.ppermute(passing[half], 'seq', up + down)  7.69 us
    pallas_call x3, Pallas kernels, project(): pl.pallas_call(functools.partial(project_kernel, plan, slots), out_shape=...  6.5 us
    pallas_call x2, Pallas kernels, rank_parts(): pl.pallas_call(functools.partial(rank_kernel, plan, slots), out_shape=out...  4.57 us
    ppermute x1, starting transfers between devices, steps(): lax.ppermute(down_own, 'seq', plan.on_cores([(low - hop, low), (high + ho...  4.57 us
  transfers between devices with their start and end apart: 25, of which 9 were waited for; matrix products, arithmetic and copies ran while one was open for 1% of the time, Pallas kernels for 15%

profile of v2, /device:TPU:0, one launch (start us, length us, event | category | flops | bytes accessed | tf_op | source)
XLA Modules:
  0.0 100.6 jit_solution(10051623505774648761)
XLA Ops:
  0.7 3.8 %hidden_rows.1.refs_2_.refs_0_ = bf16[96,3072]{1,0:T(8,128)(2,1)} custom-call(s32[1,4]{1,0:T(1,128)} %lengths_ref.9, bf16[64,3072]{1,0:T(8,128)(2,1)} %text_ref.1, bf16[32,3072]{1,0:T(8,128)(2,1)} %image_ref.1, f32[8,2,2,3072]{3,2,1,0:T(2,128)} %mod_ref.1), custom_call_target="tpu_custom_call" | custom-call | tf_op jit(solution)/shard_map/hidden_rows/pallas_call | solution.py:140
  4.9 1.3 %collective-permute-start.5 = (bf16[96,3072]{1,0:T(8,128)(2,1)}, bf16[96,3072]{1,0:T(8,128)(2,1)S(1)}, u32[]{:S(2)}, u32[]{:S(2)}) collective-permute-start(bf16[96,3072]{1,0:T(8,128)(2,1)} %hidden_rows.1.refs_2_.refs_0_), channel_id=1, source_target_pairs={{1,3},{3,5},{5,7},{2,0},{4,2},{6,4},{9,11},{11,13},{13,15},{10,8},... | collective-permute-start | bytes 1769480 | tf_op jit(solution)/shard_map/ppermute | solution.py:598
  6.8 1.3 %collective-permute-start.6 = (bf16[96,3072]{1,0:T(8,128)(2,1)S(1)}, bf16[96,3072]{1,0:T(8,128)(2,1)S(1)}, u32[]{:S(2)}, u32[]{:S(2)}) collective-permute-start(bf16[96,3072]{1,0:T(8,128)(2,1)S(1)} %collective-permute-done.4.refs_3_.refs_1_), channel_id=1, source_target_pairs={{1,3},{3,5},{5,7},{2,0},{4,2},{6,4},{9,11},{11,13},{13,15},{10,8},... | collective-permute-start | bytes 1769480 | tf_op jit(solution)/shard_map/ppermute | solution.py:598
  8.1 3.2 %packed_adapters.1 = (bf16[64,768]{1,0:T(8,128)(2,1)}, bf16[64,768]{1,0:T(8,128)(2,1)}, bf16[64,768]{1,0:T(8,128)(2,1)}, bf16[64,768]{1,0:T(8,128)(2,1)}, bf16[1...) custom-call(s32[128]{0:T(128)} %store_row_ref.7, ...), custom_call_target="tpu_custom_call" | custom-call | tf_op jit(solution)/shard_map/packed_adapters/pallas_call | solution.py:182
  11.3 2.9 %collective-permute-start = (bf16[64,768]{1,0:T(8,128)(2,1)}, bf16[64,768]{1,0:T(8,128)(2,1)S(1)}, u32[]{:S(2)}, u32[]{:S(2)}) collective-permute-start(bf16[64,768]{1,0:T(8,128)(2,1)} %get-tuple-element.23), channel_id=1, source_target_pairs={{0,8},{8,0},{16,24},{24,16},{1,9},{9,1},{17,25},{25,17},{2,10},{10... | collective-permute-start | bytes 294920 | tf_op jit(solution)/shard_map/ppermute | solution.py:610
  14.2 1.5 %collective-permute-start.1 = (bf16[64,768]{1,0:T(8,128)(2,1)}, bf16[64,768]{1,0:T(8,128)(2,1)S(1)}, u32[]{:S(2)}, u32[]{:S(2)}) collective-permute-start(bf16[64,768]{1,0:T(8,128)(2,1)} %get-tuple-element.24), channel_id=1, source_target_pairs={{0,16},{8,24},{16,0},{24,8},{1,17},{9,25},{17,1},{25,9},{2,18},{10... | collective-permute-start | bytes 294920 | tf_op jit(solution)/shard_map/ppermute | solution.py:610
  15.7 1.9 %collective-permute-done.5.refs_4_.refs_2_ = bf16[96,3072]{1,0:T(8,128)(2,1)S(1)} collective-permute-done((bf16[96,3072]{1,0:T(8,128)(2,1)}, bf16[96,3072]{1,0:T(8,128)(2,1)S(1)}, u32[]{:S(2)}, u32[]{:S(2)}) %collective-permute-start.5) | collective-permute-done | bytes 589856 | tf_op jit(solution)/shard_map/ppermute | solution.py:598
  17.6 1.3 %collective-permute-start.9 = (bf16[96,3072]{1,0:T(8,128)(2,1)S(1)}, bf16[96,3072]{1,0:T(8,128)(2,1)S(1)}, u32[]{:S(2)}, u32[]{:S(2)}) collective-permute-start(bf16[96,3072]{1,0:T(8,128)(2,1)S(1)} %collective-permute-done.5.refs_4_.refs_2_), channel_id=1, source_target_pairs={{3,5},{5,7},{2,0},{4,2},{11,13},{13,15},{10,8},{12,10},{19,21},{21... | collective-permute-start | bytes 1769480 | tf_op jit(solution)/shard_map/ppermute | solution.py:598
  18.9 5.0 %collective-permute-done.6.refs_5_.refs_3_ = bf16[96,3072]{1,0:T(8,128)(2,1)S(1)} collective-permute-done((bf16[96,3072]{1,0:T(8,128)(2,1)S(1)}, bf16[96,3072]{1,0:T(8,128)(2,1)S(1)}, u32[]{:S(2)}, u32[]{:S(2)}) %collective-permute-start.6) | collective-permute-done | bytes 589856 | tf_op jit(solution)/shard_map/ppermute | solution.py:598
  23.9 1.3 %collective-permute-start.11 = (bf16[96,3072]{1,0:T(8,128)(2,1)S(1)}, bf16[96,3072]{1,0:T(8,128)(2,1)S(1)}, u32[]{:S(2)}, u32[]{:S(2)}) collective-permute-start(bf16[96,3072]{1,0:T(8,128)(2,1)S(1)} %collective-permute-done.6.refs_5_.refs_3_), channel_id=1, source_target_pairs={{3,5},{5,7},{2,0},{4,2},{11,13},{13,15},{10,8},{12,10},{19,21},{21... | collective-permute-start | bytes 1769480 | tf_op jit(solution)/shard_map/ppermute | solution.py:598
  25.2 0.9 pad_maximum_fusion.refs_0_
  26.2 4.6 %collective-permute-start.3 = (bf16[4,64,768]{2,1,0:T(8,128)(2,1)S(1)}, bf16[4,64,768]{2,1,0:T(8,128)(2,1)S(1)}, u32[]{:S(2)}, u32[]{:S(2)}) collective-permute-start(bf16[4,64,768]{2,1,0:T(8,128)(2,1)S(1)} %pad_maximum_fusion.refs_0_), channel_id=1, source_target_pairs={{0,2},{1,3},{6,4},{7,5},{8,10},{9,11},{14,12},{15,13},{16,18},{17,... | collective-permute-start | bytes 1179656 | tf_op jit(solution)/shard_map/ppermute | solution.py:617
  31.9 8.2 %collective-permute-done.3.refs_1_ = bf16[4,64,768]{2,1,0:T(8,128)(2,1)S(1)} collective-permute-done((bf16[4,64,768]{2,1,0:T(8,128)(2,1)S(1)}, bf16[4,64,768]{2,1,0:T(8,128)(2,1)S(1)}, u32[]{:S(2)}, u32[]{:S(2)}) %collective-permute-start.3) | collective-permute-done | bytes 393248 | tf_op jit(solution)/shard_map/ppermute | solution.py:617
  40.1 1.3 %collective-permute-start.21 = (bf16[96,3072]{1,0:T(8,128)(2,1)S(1)}, bf16[96,3072]{1,0:T(8,128)(2,1)S(1)}, u32[]{:S(2)}, u32[]{:S(2)}) collective-permute-start(bf16[96,3072]{1,0:T(8,128)(2,1)S(1)} %collective-permute-done.9.refs_2_.refs_0_), channel_id=1, source_target_pairs={{5,7},{2,0},{13,15},{10,8},{21,23},{18,16},{29,31},{26,24}} | collective-permute-start | bytes 1769480 | tf_op jit(solution)/shard_map/ppermute | solution.py:598
  41.4 1.3 %collective-permute-start.23 = (bf16[96,3072]{1,0:T(8,128)(2,1)S(1)}, bf16[96,3072]{1,0:T(8,128)(2,1)S(1)}, u32[]{:S(2)}, u32[]{:S(2)}) collective-permute-start(bf16[96,3072]{1,0:T(8,128)(2,1)S(1)} %collective-permute-done.11.refs_4_.refs_2_), channel_id=1, source_target_pairs={{5,7},{2,0},{13,15},{10,8},{21,23},{18,16},{29,31},{26,24}} | collective-permute-start | bytes 1769480 | tf_op jit(solution)/shard_map/ppermute | solution.py:598
  42.7 1.6 %collective-permute-start.18 = (bf16[128,768]{1,0:T(8,128)(2,1)}, bf16[128,768]{1,0:T(8,128)(2,1)S(1)}, u32[]{:S(2)}, u32[]{:S(2)}) collective-permute-start(bf16[128,768]{1,0:T(8,128)(2,1)} %get-tuple-element.29), channel_id=1, source_target_pairs={{0,8},{8,0},{16,24},{24,16},{1,9},{9,1},{17,25},{25,17},{2,10},{10... | collective-permute-start | bytes 589832 | tf_op jit(solution)/shard_map/ppermute | solution.py:610
  44.3 1.6 %collective-permute-start.19 = (bf16[128,768]{1,0:T(8,128)(2,1)}, bf16[128,768]{1,0:T(8,128)(2,1)S(1)}, u32[]{:S(2)}, u32[]{:S(2)}) collective-permute-start(bf16[128,768]{1,0:T(8,128)(2,1)} %get-tuple-element.30), channel_id=1, source_target_pairs={{0,16},{8,24},{16,0},{24,8},{1,17},{9,25},{17,1},{25,9},{2,18},{10... | collective-permute-start | bytes 589832 | tf_op jit(solution)/shard_map/ppermute | solution.py:610
  45.9 6.0 %collective-permute-done.21.refs_0_ = bf16[96,3072]{1,0:T(8,128)(2,1)S(1)} collective-permute-done((bf16[96,3072]{1,0:T(8,128)(2,1)S(1)}, bf16[96,3072]{1,0:T(8,128)(2,1)S(1)}, u32[]{:S(2)}, u32[]{:S(2)}) %collective-permute-start.21) | collective-permute-done | bytes 589856 | tf_op jit(solution)/shard_map/ppermute | solution.py:598
  51.8 6.3 %collective-permute-done.23.refs_2_ = bf16[96,3072]{1,0:T(8,128)(2,1)S(1)} collective-permute-done((bf16[96,3072]{1,0:T(8,128)(2,1)S(1)}, bf16[96,3072]{1,0:T(8,128)(2,1)S(1)}, u32[]{:S(2)}, u32[]{:S(2)}) %collective-permute-start.23) | collective-permute-done | bytes 589856 | tf_op jit(solution)/shard_map/ppermute | solution.py:598
  58.2 3.2 %rank_parts.2 = (bf16[2,8,8,128]{3,2,1,0:T(8,128)(2,1)S(1)}, bf16[3072,128]{1,0:T(8,128)(2,1)S(1)}) custom-call(s32[1,4]{1,0:T(1,128)S(1)} %copy-done.4, s32[128]{0:T(128)S(1)} %copy-done.5, s32[4,4]{1,0:T(4,128)S(1)} %copy-done.2, bf16[4,64,768]{2,1,0:T(8,128)(2,1)S(1)} %pad_maximum_fusion.refs_0_, bf16[4,64,768]{2,1,0:T(8,128)(2,1)S(1)} %collective-permute-done.3.refs_1_, ...), custom_call_target="tpu_custom_call" | custom-call | flops 14495514624 | bytes 3538944 | tf_op jit(solution)/shard_map/rank_parts/pallas_call | solution.py:313
  61.4 1.4 %rank_parts.3 = bf16[2,8,8,128]{3,2,1,0:T(8,128)(2,1)S(1)} custom-call(s32[1,4]{1,0:T(1,128)S(1)} %copy-done.4, s32[128]{0:T(128)S(1)} %copy-done.5, s32[4,4]{1,0:T(4,128)S(1)} %copy-done.2, bf16[3072,128]{1,0:T(8,128)(2,1)S(1)} %get-tuple-element.26.refs_0_, bf16[2,8,8,128]{3,2,1,0:T(8,128)(2,1)S(1)} %get-tuple-element.27.refs_1_, ...), custom_call_target="tpu_custom_call" | custom-call | flops 75497472 | bytes 1179648 | tf_op jit(solution)/shard_map/rank_parts/pallas_call | solution.py:313
  63.3 0.9 collective-permute-done.13
  64.2 2.4 %collective-permute-start.20 = (bf16[128,768]{1,0:T(8,128)(2,1)S(1)}, bf16[128,768]{1,0:T(8,128)(2,1)S(1)}, u32[]{:S(2)}, u32[]{:S(2)}) collective-permute-start(bf16[128,768]{1,0:T(8,128)(2,1)S(1)} %copy-done.6), channel_id=1, source_target_pairs={{0,24},{8,16},{16,8},{24,0},{1,25},{9,17},{17,9},{25,1},{2,26},{10... | collective-permute-start | bytes 589832 | tf_op jit(solution)/shard_map/ppermute | solution.py:610
  66.7 1.3 %collective-permute-start.14 = (bf16[2,2,8,8,128]{4,3,2,1,0:T(8,128)(2,1)S(1)}, bf16[2,2,8,8,128]{4,3,2,1,0:T(8,128)(2,1)S(1)}, u32[]{:S(2)}, u32[]{:S(2)}) collective-permute-start(bf16[2,2,8,8,128]{4,3,2,1,0:T(8,128)(2,1)S(1)} %pad_maximum_fusion.1.refs_0_), channel_id=1, source_target_pairs={{3,5},{2,0},{5,7},{4,2},{11,13},{10,8},{13,15},{12,10},{19,21},{18... | collective-permute-start | bytes 196616 | tf_op jit(solution)/shard_map/ppermute | solution.py:639
  68.0 1.3 %collective-permute-start.15 = (bf16[2,2,8,8,128]{4,3,2,1,0:T(8,128)(2,1)S(1)}, bf16[2,2,8,8,128]{4,3,2,1,0:T(8,128)(2,1)S(1)}, u32[]{:S(2)}, u32[]{:S(2)}) collective-permute-start(bf16[2,2,8,8,128]{4,3,2,1,0:T(8,128)(2,1)S(1)} %pad_maximum_fusion.1.refs_0_), channel_id=1, source_target_pairs={{3,7},{4,0},{11,15},{12,8},{19,23},{20,16},{27,31},{28,24}} | collective-permute-start | bytes 196616 | tf_op jit(solution)/shard_map/ppermute | solution.py:639
  69.3 3.0 %shard_map.113 = (f32[384,768]{1,0:T(8,128)S(1)}, f32[192,768]{1,0:T(8,128)S(1)}) custom-call(bf16[96,3072]{1,0:T(8,128)(2,1)S(1)} %copy-done, bf16[96,3072]{1,0:T(8,128)(2,1)S(1)} %collective-permute-done.4.refs_3_.refs_1_, bf16[96,3072]{1,0:T(8,128)(2,1)S(1)} %collective-permute-done.5.refs_4_.refs_2_, ...), custom_call_target="tpu_custom_call" | custom-call | flops 2717908992 | bytes 3538944 | tf_op jit(solution)/shard_map/pallas_call | solution.py:228
  72.8 2.2 %collective-permute-done.15.refs_2_ = bf16[2,2,8,8,128]{4,3,2,1,0:T(8,128)(2,1)S(1)} collective-permute-done((bf16[2,2,8,8,128]{4,3,2,1,0:T(8,128)(2,1)S(1)}, bf16[2,2,8,8,128]{4,3,2,1,0:T(8,128)(2,1)S(1)}, u32[]{:S(2)}, u32[]{:S(2)}) %collective-permute-start.15) | collective-permute-done | bytes 65568 | tf_op jit(solution)/shard_map/ppermute | solution.py:639
  75.0 1.7 %shard_map.114 = (f32[128,768]{1,0:T(8,128)S(1)}, f32[64,768]{1,0:T(8,128)S(1)}) custom-call(bf16[96,3072]{1,0:T(8,128)(2,1)S(1)} %collective-permute-done.9.refs_2_.refs_0_, bf16[96,3072]{1,0:T(8,128)(2,1)S(1)} %collective-permute-done.10.refs_3_.refs_1_, bf16[96,3072]{1,0:T(8,128)(2,1)S(1)} %collective-permute-done.11.refs_4_.refs_2_, ...), custom_call_target="tpu_custom_call" | custom-call | flops 905969664 | bytes 1179648 | tf_op jit(solution)/shard_map/pallas_call | solution.py:228
  76.8 2.6 %early_heads.1 = (bf16[3,512,256]{2,1,0:T(8,128)(2,1)S(1)}, bf16[3,256,256]{2,1,0:T(8,128)(2,1)S(1)}, f32[128,768]{1,0:T(8,128)S(1)}, f32[64,768]{1,0:T(8,128)S(1)}) custom-call(s32[1,4]{1,0:T(1,128)S(1)} %copy-done.4, s32[128]{0:T(128)S(1)} %copy-done.5, s32[4,4]{1,0:T(4,128)S(1)} %copy-done.2, f32[2,2,128]{2,1,0:T(2,128)S(1)} %copy-done.3, ...), custom_call_target="tpu_custom_call" | custom-call | flops 805306368 | bytes 4718592 | tf_op jit(solution)/shard_map/early_heads/pallas_call | solution.py:425
  79.4 1.9 %shard_map.115 = (f32[128,768]{1,0:T(8,128)S(1)}, f32[64,768]{1,0:T(8,128)S(1)}) custom-call(bf16[96,3072]{1,0:T(8,128)(2,1)S(1)} %collective-permute-done.21.refs_0_, bf16[96,3072]{1,0:T(8,128)(2,1)S(1)} %collective-permute-done.22.refs_1_, bf16[96,3072]{1,0:T(8,128)(2,1)S(1)} %collective-permute-done.23.refs_2_, ...), custom_call_target="tpu_custom_call" | custom-call | flops 905969664 | bytes 1179648 | tf_op jit(solution)/shard_map/pallas_call | solution.py:228
  81.3 3.5 %attention.1 = bf16[8,96,256]{2,1,0:T(8,128)(2,1)S(1)} custom-call(s32[1,4]{1,0:T(1,128)S(1)} %copy-done.4, f32[2,2,128]{2,1,0:T(2,128)S(1)} %copy-done.3, bf16[3,512,256]{2,1,0:T(8,128)(2,1)S(1)} %get-tuple-element.36.refs_0_, bf16[3,256,256]{2,1,0:T(8,128)(2,1)S(1)} %get-tuple-element.37.refs_1_, f32[128,768]{1,0:T(8,128)S(1)} %get-tuple-element.38.refs_2_, ...), custom_call_target="tpu_custom_call" | custom-call | tf_op jit(solution)/shard_map/attention/pallas_call | solution.py:529
  84.8 15.1 %all_to_all.5.pieces = bf16[8,96,256]{2,1,0:T(8,128)(2,1)S(1)} all-to-all(bf16[8,96,256]{2,1,0:T(8,128)(2,1)S(1)} %attention.1), channel_id=1, replica_groups=mesh['bag'=4,'seq'=8] {'seq'}, dimensions={0} | all-to-all | bytes 786432 | tf_op jit(solution)/shard_map/all_to_all | solution.py:654
  (52 shorter events, 4.2 us)
Async XLA Ops:
  0.6 57.5 %copy-start.4 = (s32[1,4]{1,0:T(1,128)S(1)}, s32[1,4]{1,0:T(1,128)}, u32[]{:S(2)}) copy-start(s32[1,4]{1,0:T(1,128)} %lengths_ref.9) | copy-start | bytes 52
  0.6 57.5 %copy-start.5 = (s32[128]{0:T(128)S(1)}, s32[128]{0:T(128)}, u32[]{:S(2)}) copy-start(s32[128]{0:T(128)} %store_row_ref.7) | copy-start | bytes 1540
  0.7 57.5 %copy-start.2 = (s32[4,4]{1,0:T(4,128)S(1)}, s32[4,4]{1,0:T(4,128)}, u32[]{:S(2)}) copy-start(s32[4,4]{1,0:T(4,128)} %adapter_ref.7) | copy-start | bytes 196
  4.4 53.7 %copy-start = (bf16[96,3072]{1,0:T(8,128)(2,1)S(1)}, bf16[96,3072]{1,0:T(8,128)(2,1)}, u32[]{:S(2)}) copy-start(bf16[96,3072]{1,0:T(8,128)(2,1)} %hidden_rows.1.refs_2_.refs_0_) | copy-start | bytes 1769476
  4.4 2.3 %collective-permute-start.4 = (bf16[96,3072]{1,0:T(8,128)(2,1)}, bf16[96,3072]{1,0:T(8,128)(2,1)S(1)}, u32[]{:S(2)}, u32[]{:S(2)}) collective-permute-start(bf16[96,3072]{1,0:T(8,128)(2,1)} %hidden_rows.1.refs_2_.refs_0_), channel_id=1, source_target_pairs={{0,1},{1,0},{2,3},{3,2},{4,5},{5,4},{6,7},{7,6},{8,9},{9,8},{10,11... | collective-permute-start | bytes 1769480 | tf_op jit(solution)/shard_map/ppermute | solution.py:592
  4.9 12.7 %collective-permute-start.5 = (bf16[96,3072]{1,0:T(8,128)(2,1)}, bf16[96,3072]{1,0:T(8,128)(2,1)S(1)}, u32[]{:S(2)}, u32[]{:S(2)}) collective-permute-start(bf16[96,3072]{1,0:T(8,128)(2,1)} %hidden_rows.1.refs_2_.refs_0_), channel_id=1, source_target_pairs={{1,3},{3,5},{5,7},{2,0},{4,2},{6,4},{9,11},{11,13},{13,15},{10,8},... | collective-permute-start | bytes 1769480 | tf_op jit(solution)/shard_map/ppermute | solution.py:598
  6.8 17.1 %collective-permute-start.6 = (bf16[96,3072]{1,0:T(8,128)(2,1)S(1)}, bf16[96,3072]{1,0:T(8,128)(2,1)S(1)}, u32[]{:S(2)}, u32[]{:S(2)}) collective-permute-start(bf16[96,3072]{1,0:T(8,128)(2,1)S(1)} %collective-permute-done.4.refs_3_.refs_1_), channel_id=1, source_target_pairs={{1,3},{3,5},{5,7},{2,0},{4,2},{6,4},{9,11},{11,13},{13,15},{10,8},... | collective-permute-start | bytes 1769480 | tf_op jit(solution)/shard_map/ppermute | solution.py:598
  11.3 13.9 %collective-permute-start = (bf16[64,768]{1,0:T(8,128)(2,1)}, bf16[64,768]{1,0:T(8,128)(2,1)S(1)}, u32[]{:S(2)}, u32[]{:S(2)}) collective-permute-start(bf16[64,768]{1,0:T(8,128)(2,1)} %get-tuple-element.23), channel_id=1, source_target_pairs={{0,8},{8,0},{16,24},{24,16},{1,9},{9,1},{17,25},{25,17},{2,10},{10... | collective-permute-start | bytes 294920 | tf_op jit(solution)/shard_map/ppermute | solution.py:610
  14.2 11.0 %collective-permute-start.1 = (bf16[64,768]{1,0:T(8,128)(2,1)}, bf16[64,768]{1,0:T(8,128)(2,1)S(1)}, u32[]{:S(2)}, u32[]{:S(2)}) collective-permute-start(bf16[64,768]{1,0:T(8,128)(2,1)} %get-tuple-element.24), channel_id=1, source_target_pairs={{0,16},{8,24},{16,0},{24,8},{1,17},{9,25},{17,1},{25,9},{2,18},{10... | collective-permute-start | bytes 294920 | tf_op jit(solution)/shard_map/ppermute | solution.py:610
  15.7 9.5 %collective-permute-start.2 = (bf16[64,768]{1,0:T(8,128)(2,1)}, bf16[64,768]{1,0:T(8,128)(2,1)S(1)}, u32[]{:S(2)}, u32[]{:S(2)}) collective-permute-start(bf16[64,768]{1,0:T(8,128)(2,1)} %get-tuple-element.25), channel_id=1, source_target_pairs={{0,24},{8,16},{16,8},{24,0},{1,25},{9,17},{17,9},{25,1},{2,26},{10... | collective-permute-start | bytes 294920 | tf_op jit(solution)/shard_map/ppermute | solution.py:610
  17.6 13.9 %collective-permute-start.9 = (bf16[96,3072]{1,0:T(8,128)(2,1)S(1)}, bf16[96,3072]{1,0:T(8,128)(2,1)S(1)}, u32[]{:S(2)}, u32[]{:S(2)}) collective-permute-start(bf16[96,3072]{1,0:T(8,128)(2,1)S(1)} %collective-permute-done.5.refs_4_.refs_2_), channel_id=1, source_target_pairs={{3,5},{5,7},{2,0},{4,2},{11,13},{13,15},{10,8},{12,10},{19,21},{21... | collective-permute-start | bytes 1769480 | tf_op jit(solution)/shard_map/ppermute | solution.py:598
  23.9 17.5 %collective-permute-start.11 = (bf16[96,3072]{1,0:T(8,128)(2,1)S(1)}, bf16[96,3072]{1,0:T(8,128)(2,1)S(1)}, u32[]{:S(2)}, u32[]{:S(2)}) collective-permute-start(bf16[96,3072]{1,0:T(8,128)(2,1)S(1)} %collective-permute-done.6.refs_5_.refs_3_), channel_id=1, source_target_pairs={{3,5},{5,7},{2,0},{4,2},{11,13},{13,15},{10,8},{12,10},{19,21},{21... | collective-permute-start | bytes 1769480 | tf_op jit(solution)/shard_map/ppermute | solution.py:598
  26.2 13.9 %collective-permute-start.3 = (bf16[4,64,768]{2,1,0:T(8,128)(2,1)S(1)}, bf16[4,64,768]{2,1,0:T(8,128)(2,1)S(1)}, u32[]{:S(2)}, u32[]{:S(2)}) collective-permute-start(bf16[4,64,768]{2,1,0:T(8,128)(2,1)S(1)} %pad_maximum_fusion.refs_0_), channel_id=1, source_target_pairs={{0,2},{1,3},{6,4},{7,5},{8,10},{9,11},{14,12},{15,13},{16,18},{17,... | collective-permute-start | bytes 1179656 | tf_op jit(solution)/shard_map/ppermute | solution.py:617
  30.7 11.9 %collective-permute-start.7 = (bf16[96,3072]{1,0:T(8,128)(2,1)S(1)}, bf16[96,3072]{1,0:T(8,128)(2,1)S(1)}, u32[]{:S(2)}, u32[]{:S(2)}) collective-permute-start(bf16[96,3072]{1,0:T(8,128)(2,1)S(1)} %collective-permute-done.5.refs_4_.refs_2_), channel_id=1, source_target_pairs={{0,1},{1,0},{2,3},{3,2},{4,5},{5,4},{6,7},{7,6},{8,9},{9,8},{10,11... | collective-permute-start | bytes 1769480 | tf_op jit(solution)/shard_map/ppermute | solution.py:599
  31.4 12.9 %collective-permute-start.8 = (bf16[96,3072]{1,0:T(8,128)(2,1)S(1)}, bf16[96,3072]{1,0:T(8,128)(2,1)S(1)}, u32[]{:S(2)}, u32[]{:S(2)}) collective-permute-start(bf16[96,3072]{1,0:T(8,128)(2,1)S(1)} %collective-permute-done.6.refs_5_.refs_3_), channel_id=1, source_target_pairs={{0,1},{1,0},{2,3},{3,2},{4,5},{5,4},{6,7},{7,6},{8,9},{9,8},{10,11... | collective-permute-start | bytes 1769480 | tf_op jit(solution)/shard_map/ppermute | solution.py:599
  31.4 14.4 %collective-permute-start.10 = (bf16[96,3072]{1,0:T(8,128)(2,1)S(1)}, bf16[96,3072]{1,0:T(8,128)(2,1)S(1)}, u32[]{:S(2)}, u32[]{:S(2)}) collective-permute-start(bf16[96,3072]{1,0:T(8,128)(2,1)S(1)} %collective-permute-done.9.refs_2_.refs_0_), channel_id=1, source_target_pairs={{0,1},{1,0},{2,3},{3,2},{4,5},{5,4},{6,7},{7,6},{8,9},{9,8},{10,11... | collective-permute-start | bytes 1769480 | tf_op jit(solution)/shard_map/ppermute | solution.py:599
  40.1 11.8 %collective-permute-start.21 = (bf16[96,3072]{1,0:T(8,128)(2,1)S(1)}, bf16[96,3072]{1,0:T(8,128)(2,1)S(1)}, u32[]{:S(2)}, u32[]{:S(2)}) collective-permute-start(bf16[96,3072]{1,0:T(8,128)(2,1)S(1)} %collective-permute-done.9.refs_2_.refs_0_), channel_id=1, source_target_pairs={{5,7},{2,0},{13,15},{10,8},{21,23},{18,16},{29,31},{26,24}} | collective-permute-start | bytes 1769480 | tf_op jit(solution)/shard_map/ppermute | solution.py:598
  41.4 16.8 %collective-permute-start.23 = (bf16[96,3072]{1,0:T(8,128)(2,1)S(1)}, bf16[96,3072]{1,0:T(8,128)(2,1)S(1)}, u32[]{:S(2)}, u32[]{:S(2)}) collective-permute-start(bf16[96,3072]{1,0:T(8,128)(2,1)S(1)} %collective-permute-done.11.refs_4_.refs_2_), channel_id=1, source_target_pairs={{5,7},{2,0},{13,15},{10,8},{21,23},{18,16},{29,31},{26,24}} | collective-permute-start | bytes 1769480 | tf_op jit(solution)/shard_map/ppermute | solution.py:598
  42.7 24.0 %collective-permute-start.18 = (bf16[128,768]{1,0:T(8,128)(2,1)}, bf16[128,768]{1,0:T(8,128)(2,1)S(1)}, u32[]{:S(2)}, u32[]{:S(2)}) collective-permute-start(bf16[128,768]{1,0:T(8,128)(2,1)} %get-tuple-element.29), channel_id=1, source_target_pairs={{0,8},{8,0},{16,24},{24,16},{1,9},{9,1},{17,25},{25,17},{2,10},{10... | collective-permute-start | bytes 589832 | tf_op jit(solution)/shard_map/ppermute | solution.py:610
  44.2 25.0 %slice-start = ((s8[9437184]{0:T(1024)(128)(4,1)}), s8[4194304]{0:T(1024)(128)(4,1)S(1)}, s32[]{:S(2)}) async-start(s8[9437184]{0:T(1024)(128)(4,1)} %bitcast.6), calls=%async_computation.1 | async-start | bytes 8388608
  44.2 25.0 %slice-start.1 = ((s8[9437184]{0:T(1024)(128)(4,1)}), s8[4194304]{0:T(1024)(128)(4,1)S(1)}, s32[]{:S(2)}) async-start(s8[9437184]{0:T(1024)(128)(4,1)} %bitcast.6), calls=%async_computation.2 | async-start | bytes 8388608
  44.3 25.0 %slice-start.2 = ((s8[9437184]{0:T(1024)(128)(4,1)}), s8[1048576]{0:T(1024)(128)(4,1)S(1)}, s32[]{:S(2)}) async-start(s8[9437184]{0:T(1024)(128)(4,1)} %bitcast.6), calls=%async_computation.3 | async-start | bytes 2097152
  44.3 23.7 %collective-permute-start.19 = (bf16[128,768]{1,0:T(8,128)(2,1)}, bf16[128,768]{1,0:T(8,128)(2,1)S(1)}, u32[]{:S(2)}, u32[]{:S(2)}) collective-permute-start(bf16[128,768]{1,0:T(8,128)(2,1)} %get-tuple-element.30), channel_id=1, source_target_pairs={{0,16},{8,24},{16,0},{24,8},{1,17},{9,25},{17,1},{25,9},{2,18},{10... | collective-permute-start | bytes 589832 | tf_op jit(solution)/shard_map/ppermute | solution.py:610
  45.9 15.5 %collective-permute-start.12 = (bf16[96,3072]{1,0:T(8,128)(2,1)S(1)}, bf16[96,3072]{1,0:T(8,128)(2,1)S(1)}, u32[]{:S(2)}, u32[]{:S(2)}) collective-permute-start(bf16[96,3072]{1,0:T(8,128)(2,1)S(1)} %collective-permute-done.11.refs_4_.refs_2_), channel_id=1, source_target_pairs={{0,1},{1,0},{2,3},{3,2},{4,5},{5,4},{6,7},{7,6},{8,9},{9,8},{10,11... | collective-permute-start | bytes 1769480 | tf_op jit(solution)/shard_map/ppermute | solution.py:599
  51.8 27.6 %collective-permute-start.22 = (bf16[96,3072]{1,0:T(8,128)(2,1)S(1)}, bf16[96,3072]{1,0:T(8,128)(2,1)S(1)}, u32[]{:S(2)}, u32[]{:S(2)}) collective-permute-start(bf16[96,3072]{1,0:T(8,128)(2,1)S(1)} %collective-permute-done.21.refs_0_), channel_id=1, source_target_pairs={{0,1},{1,0},{2,3},{3,2},{4,5},{5,4},{6,7},{7,6},{8,9},{9,8},{10,11... | collective-permute-start | bytes 1769480 | tf_op jit(solution)/shard_map/ppermute | solution.py:599
  58.2 21.3 %collective-permute-start.24 = (bf16[96,3072]{1,0:T(8,128)(2,1)S(1)}, bf16[96,3072]{1,0:T(8,128)(2,1)S(1)}, u32[]{:S(2)}, u32[]{:S(2)}) collective-permute-start(bf16[96,3072]{1,0:T(8,128)(2,1)S(1)} %collective-permute-done.23.refs_2_), channel_id=1, source_target_pairs={{0,1},{1,0},{2,3},{3,2},{4,5},{5,4},{6,7},{7,6},{8,9},{9,8},{10,11... | collective-permute-start | bytes 1769480 | tf_op jit(solution)/shard_map/ppermute | solution.py:599
  62.8 1.4 %collective-permute-start.13 = (bf16[2,8,8,128]{3,2,1,0:T(8,128)(2,1)S(1)}, bf16[2,8,8,128]{3,2,1,0:T(8,128)(2,1)S(1)}, u32[]{:S(2)}, u32[]{:S(2)}) collective-permute-start(bf16[2,8,8,128]{3,2,1,0:T(8,128)(2,1)S(1)} %rank_parts.3), channel_id=1, source_target_pairs={{0,1},{1,0},{2,3},{3,2},{4,5},{5,4},{6,7},{7,6},{8,9},{9,8},{10,11... | collective-permute-start | bytes 98312 | tf_op jit(solution)/shard_map/ppermute | solution.py:633
  64.2 12.5 %collective-permute-start.20 = (bf16[128,768]{1,0:T(8,128)(2,1)S(1)}, bf16[128,768]{1,0:T(8,128)(2,1)S(1)}, u32[]{:S(2)}, u32[]{:S(2)}) collective-permute-start(bf16[128,768]{1,0:T(8,128)(2,1)S(1)} %copy-done.6), channel_id=1, source_target_pairs={{0,24},{8,16},{16,8},{24,0},{1,25},{9,17},{17,9},{25,1},{2,26},{10... | collective-permute-start | bytes 589832 | tf_op jit(solution)/shard_map/ppermute | solution.py:610
  66.7 6.2 %collective-permute-start.14 = (bf16[2,2,8,8,128]{4,3,2,1,0:T(8,128)(2,1)S(1)}, bf16[2,2,8,8,128]{4,3,2,1,0:T(8,128)(2,1)S(1)}, u32[]{:S(2)}, u32[]{:S(2)}) collective-permute-start(bf16[2,2,8,8,128]{4,3,2,1,0:T(8,128)(2,1)S(1)} %pad_maximum_fusion.1.refs_0_), channel_id=1, source_target_pairs={{3,5},{2,0},{5,7},{4,2},{11,13},{10,8},{13,15},{12,10},{19,21},{18... | collective-permute-start | bytes 196616 | tf_op jit(solution)/shard_map/ppermute | solution.py:639
  68.0 7.1 %collective-permute-start.15 = (bf16[2,2,8,8,128]{4,3,2,1,0:T(8,128)(2,1)S(1)}, bf16[2,2,8,8,128]{4,3,2,1,0:T(8,128)(2,1)S(1)}, u32[]{:S(2)}, u32[]{:S(2)}) collective-permute-start(bf16[2,2,8,8,128]{4,3,2,1,0:T(8,128)(2,1)S(1)} %pad_maximum_fusion.1.refs_0_), channel_id=1, source_target_pairs={{3,7},{4,0},{11,15},{12,8},{19,23},{20,16},{27,31},{28,24}} | collective-permute-start | bytes 196616 | tf_op jit(solution)/shard_map/ppermute | solution.py:639
  72.8 3.9 %collective-permute-start.16 = (bf16[2,2,8,8,128]{4,3,2,1,0:T(8,128)(2,1)S(1)}, bf16[2,2,8,8,128]{4,3,2,1,0:T(8,128)(2,1)S(1)}, u32[]{:S(2)}, u32[]{:S(2)}) collective-permute-start(bf16[2,2,8,8,128]{4,3,2,1,0:T(8,128)(2,1)S(1)} %collective-permute-done.14.refs_1_), channel_id=1, source_target_pairs={{0,1},{1,0},{2,3},{3,2},{4,5},{5,4},{6,7},{7,6},{8,9},{9,8},{10,11... | collective-permute-start | bytes 196616 | tf_op jit(solution)/shard_map/ppermute | solution.py:640
  75.0 1.7 %collective-permute-start.17 = (bf16[2,2,8,8,128]{4,3,2,1,0:T(8,128)(2,1)S(1)}, bf16[2,2,8,8,128]{4,3,2,1,0:T(8,128)(2,1)S(1)}, u32[]{:S(2)}, u32[]{:S(2)}) collective-permute-start(bf16[2,2,8,8,128]{4,3,2,1,0:T(8,128)(2,1)S(1)} %collective-permute-done.15.refs_2_), channel_id=1, source_target_pairs={{0,1},{1,0},{2,3},{3,2},{4,5},{5,4},{6,7},{7,6},{8,9},{9,8},{10,11... | collective-permute-start | bytes 196616 | tf_op jit(solution)/shard_map/ppermute | solution.py:640
  (3 other events, 28.9 us)

commit v3 on v2

--- a/solution.py
+++ b/solution.py
@@ -15,6 +15,7 @@
 ROW_STEP = 16
 
 
+WIDE_GRANT = 59 << 20
 VMEM_GRANT = 26 << 20
 PARAMS = pltpu.CompilerParams(vmem_limit_bytes=VMEM_GRANT)
 
@@ -22,6 +23,10 @@
 VMEM = functools.partial(pl.BlockSpec, memory_space=pltpu.VMEM)
 HBM = functools.partial(pl.BlockSpec, memory_space=pltpu.HBM)
 NT = (((1,), (1,)), ((), ()))
+
+
+def chip_core(seq_index):
+    return lax.shift_right_logical(seq_index, CORES // 2), lax.bitwise_and(seq_index, CORES - 1)
 
 
 def round_up(value, step):
@@ -55,7 +60,7 @@
 
 
 def place_of(plan, slot, half, seq_index):
-    chip, core = seq_index // CORES, seq_index % CORES
+    chip, core = chip_core(seq_index)
     kind, hop = slot
     if kind == "own":
         source, lead = chip, core
@@ -76,8 +81,18 @@
 
 
 def is_passed(plan, slot, seq_index):
-    chip, core = seq_index // CORES, seq_index % CORES
+    chip, core = chip_core(seq_index)
     return jnp.where(core == 1, chip >= slot[1], chip + slot[1] < plan.chips)
+
+
+def user_keys(plan, store_row_ref, adapter_ref):
+    bag, keys = lax.axis_index("bag"), []
+    for user in range(plan.users):
+        row, owner = store_row_ref[adapter_ref[bag, user]], jnp.int32(0)
+        for other in range(1, plan.bags):
+            owner = owner + (row >= other * plan.store).astype(jnp.int32)
+        keys.append(lax.bitwise_xor(owner, bag))
+    return keys
 
 
 def image_seg_of(position, lengths_ref, users):
@@ -88,13 +103,6 @@
             end = end + lengths_ref[0, user]
             seg = seg + (position >= end).astype(jnp.int32)
     return seg
-
-
-def user_keys(plan, bag, store_row_ref, adapter_ref):
-    return [
-        lax.bitwise_xor(store_row_ref[adapter_ref[bag, user]] // plan.store, bag)
-        for user in range(plan.users)
-    ]
 
 
 def hidden_kernel(plan, lengths_ref, text_ref, image_ref, mod_ref, out_ref):
@@ -123,7 +131,7 @@
         out_ref[target, :] = ((1.0 + scale) * base + shift).astype(jnp.bfloat16)
         return 0
 
-    lax.fori_loop(0, plan.image_dev // ROW_STEP, image_step, 0)
+    lax.fori_loop(0, plan.image_dev // ROW_STEP, image_step, 0, unroll=True)
 
     def text_step(step, _):
         rows = pl.ds(pl.multiple_of(step * ROW_STEP, ROW_STEP), ROW_STEP)
@@ -133,7 +141,7 @@
         out_ref[rows, :] = ((1.0 + scale) * normed(text_ref[rows, :]) + shift).astype(jnp.bfloat16)
         return 0
 
-    lax.fori_loop(0, plan.text_dev // ROW_STEP, text_step, 0)
+    lax.fori_loop(0, plan.text_dev // ROW_STEP, text_step, 0, unroll=True)
 
 
 def hidden_rows(plan, lengths, text_rows, image_rows, modulation):
@@ -142,6 +150,7 @@
         out_shape=jax.ShapeDtypeStruct((plan.rows, plan.width), jnp.bfloat16),
         in_specs=[SMEM(), VMEM(), VMEM(), VMEM()],
         out_specs=VMEM(),
+        compiler_params=pltpu.CompilerParams(vmem_limit_bytes=WIDE_GRANT),
         name="hidden_rows",
     )(lengths, text_rows, image_rows, modulation)
 
@@ -156,7 +165,8 @@
         place = jnp.int32(0)
         for user in range(plan.users):
             row = store_row_ref[adapter_ref[target, user]]
-            place = jnp.where(row // plan.store == bag, row % plan.store, place)
+            row = row - bag * plan.store
+            place = jnp.where((row >= 0) & (row < plan.store), row, place)
         one = pltpu.make_async_copy(down_hbm.at[place], down.at[hop], down_sem.at[hop])
         two = pltpu.make_async_copy(up_hbm.at[place], up.at[hop], up_sem.at[hop])
         one.start()
@@ -186,7 +196,7 @@
             for rows in sizes
             for _ in range(plan.bags)
         ],
-        in_specs=[SMEM(), SMEM(), HBM(), HBM()],
+        in_specs=[SMEM()] * 2 + [HBM(), HBM()],
         out_specs=[VMEM()] * (2 * plan.bags),
         scratch_shapes=[
             pltpu.VMEM((plan.bags,) + store_down.shape[1:], jnp.bfloat16),
@@ -194,6 +204,7 @@
             pltpu.SemaphoreType.DMA((plan.bags,)),
             pltpu.SemaphoreType.DMA((plan.bags,)),
         ],
+        compiler_params=pltpu.CompilerParams(vmem_limit_bytes=52 << 20),
         name="packed_adapters",
     )(store_row, user_adapter, store_down, store_up)
 
@@ -218,8 +229,15 @@
                 for at in range(CORES):
                     take(at, blocks[2 * at + choice])
 
-    text_out[...] = jnp.dot(texts[...], weight_ref[0], preferred_element_type=jnp.float32)
-    image_out[...] = jnp.dot(images[...], weight_ref[1], preferred_element_type=jnp.float32)
+    def multiply():
+        text_out[...] = jnp.dot(texts[...], weight_ref[0], preferred_element_type=jnp.float32)
+        image_out[...] = jnp.dot(images[...], weight_ref[1], preferred_element_type=jnp.float32)
+
+    if each == 1:
+        multiply()
+    else:
+        _, valid = place_of(plan, slots[0], 0, lax.axis_index("seq"))
+        pl.when(valid)(multiply)
 
 
 def project(plan, slots, blocks, head_weight):
@@ -264,10 +282,10 @@
     else:
         (out_ref,), (turned, before) = refs, downs
         out_ref[...] = before[...]
-    bag, seq_index = lax.axis_index("bag"), lax.axis_index("seq")
-    chip = seq_index // CORES
+    seq_index = lax.axis_index("seq")
+    chip, _ = chip_core(seq_index)
     passed = is_passed(plan, slots[0], seq_index)
-    keys = user_keys(plan, bag, store_row_ref, adapter_ref)
+    keys = user_keys(plan, store_row_ref, adapter_ref)
     tall = plan.bags * plan.down_rows
     for part in range(plan.parts if first else 0):
         lanes = slice(part * plan.cols, (part + 1) * plan.cols)
@@ -301,7 +319,7 @@
                 out_ref[spot, place] = total.astype(jnp.bfloat16)
 
 
-def rank_parts(plan, slots, lengths, store_row, user_adapter, downs, blocks):
+def rank_parts(plan, slots, scalars, downs, blocks):
     first = slots[0][0] == "own"
     tall = plan.half * plan.bags * plan.down_rows
     rows = plan.rows * CORES * len(slots)
@@ -323,7 +341,7 @@
             transcendentals=0,
         ),
         name="rank_parts",
-    )(lengths, store_row, user_adapter, *downs, *blocks)
+    )(*scalars, *downs, *blocks)
 
 
 def head_normed(values, gain_row):
@@ -346,10 +364,10 @@
     ranks, refs = refs[: 2 * plan.half + 1], refs[2 * plan.half + 1 :]
     packs, refs = refs[: plan.bags], refs[plan.bags :]
     plains, refs = refs[: 2 * len(groups)], refs[2 * len(groups) :]
-    text_heads, image_heads, text_last, image_last, ranks_ref, spread, text_side, image_side, ups, adjust = refs
-    sides = (text_side, image_side)
-    bag, seq_index = lax.axis_index("bag"), lax.axis_index("seq")
-    chip, core = seq_index // CORES, seq_index % CORES
+    text_heads, image_heads, text_last, image_last, ranks_ref, spread, text_side, image_side, ups = refs[:9]
+    sides, adjusts = (text_side, image_side), refs[9:]
+    seq_index = lax.axis_index("seq")
+    chip, core = chip_core(seq_index)
     leads = []
     for side, middle in enumerate((plan.half - 1, plan.half)):
         away = jnp.abs(chip - middle)
@@ -363,7 +381,7 @@
             def _():
                 ranks_ref[side] = source[...]
 
-    keys = user_keys(plan, bag, store_row_ref, adapter_ref)
+    keys = user_keys(plan, store_row_ref, adapter_ref)
     for place in range(plan.seq):
         key, _ = lane_keys(plan, lengths_ref, keys, place)
         for side in range(2):
@@ -386,39 +404,48 @@
             ups[hop * plan.rank : (hop + 1) * plan.rank, :] = packs[hop][
                 stream * plan.rank : (stream + 1) * plan.rank, :
             ]
-        size = plan.text_dev if stream == 0 else plan.image_dev
-        adjust[: plan.seq * size, :] = jnp.dot(
+        adjusts[stream][...] = jnp.dot(
             sides[stream][...], ups[...], preferred_element_type=jnp.float32
         )
-        out_ref = text_heads if stream == 0 else image_heads
-        last_ref = text_last if stream == 0 else image_last
-
-        def rows_of(place):
-            return pl.ds(pl.multiple_of(place * size, size), size)
-
-        for group_at, group in enumerate(groups):
-            plain = plains[2 * group_at + stream]
-            for at in range(CORES * len(group)):
-                place, valid = place_of(plan, group[at // CORES], at % CORES, seq_index)
-
-                @pl.when(valid)
-                def _():
-                    write_heads(
-                        plan,
-                        lambda lanes: plain[at * size : (at + 1) * size, lanes]
-                        + adjust[rows_of(place), lanes],
-                        gain_ref,
-                        stream,
-                        out_ref,
-                        pl.ds(pl.multiple_of(place * size, size), size),
-                    )
-
-        for half in range(CORES):
-            place, _ = place_of(plan, plan.groups[-1][0], half, seq_index)
-            last_ref[half * size : (half + 1) * size, :] = adjust[rows_of(place), :]
-
-
-def early_heads(plan, groups, lengths, store_row, user_adapter, norm_gain, ranks, packs, plains):
+
+    sizes = (plan.text_dev, plan.image_dev)
+    outs = (text_heads, image_heads)
+
+    def rows_of(place, size):
+        return pl.ds(pl.multiple_of(place * size, size), size)
+
+    for group_at, group in enumerate(groups):
+        for slot_at, slot in enumerate(group):
+            _, valid = place_of(plan, slot, 0, seq_index)
+
+            @pl.when(valid)
+            def _():
+                for half in range(CORES):
+                    place, _ = place_of(plan, slot, half, seq_index)
+                    at = slot_at * CORES + half
+                    for stream, size in enumerate(sizes):
+                        plain = plains[2 * group_at + stream]
+                        spot = rows_of(place, size)
+                        write_heads(
+                            plan,
+                            lambda lanes: plain[at * size : (at + 1) * size, lanes]
+                            + adjusts[stream][spot, lanes],
+                            gain_ref,
+                            stream,
+                            outs[stream],
+                            spot,
+                        )
+
+    for half in range(CORES):
+        place, _ = place_of(plan, plan.groups[-1][0], half, seq_index)
+        for stream, size in enumerate(sizes):
+            last_ref = (text_last, image_last)[stream]
+            last_ref[half * size : (half + 1) * size, :] = adjusts[stream][
+                rows_of(place, size), :
+            ]
+
+
+def early_heads(plan, groups, scalars, norm_gain, ranks, packs, plains):
     total = (plan.seq * plan.text_dev, plan.seq * plan.image_dev)
     last = (CORES * plan.text_dev, CORES * plan.image_dev)
     scratch = 4 * plan.seq * plan.lanes * (plan.bags * plan.rank + plan.cols)
@@ -435,6 +462,7 @@
             pltpu.VMEM((total[1], plan.bags * plan.rank), jnp.bfloat16),
             pltpu.VMEM((plan.bags * plan.rank, plan.cols), jnp.bfloat16),
             pltpu.VMEM((total[0], plan.cols), jnp.float32),
+            pltpu.VMEM((total[1], plan.cols), jnp.float32),
         ],
         compiler_params=pltpu.CompilerParams(vmem_limit_bytes=max(VMEM_GRANT, 2 * scratch)),
         cost_estimate=pl.CostEstimate(
@@ -443,7 +471,7 @@
             transcendentals=0,
         ),
         name="early_heads",
-    )(lengths, store_row, user_adapter, norm_gain, *ranks, *packs, *plains)
+    )(*scalars, norm_gain, *ranks, *packs, *plains)
 
 
 def attend_kernel(plan, lengths_ref, gain_ref, *refs):
@@ -453,22 +481,24 @@
     factor = math.log2(math.e) / math.sqrt(HEAD_DIM)
     text_heads[...] = text_in[...]
     image_heads[...] = image_in[...]
-    for stream in range(2):
-        plain = text_plain if stream == 0 else image_plain
-        adjust = text_adjust if stream == 0 else image_adjust
-        size = plan.text_dev if stream == 0 else plan.image_dev
+    last = plan.groups[-1][0]
+    _, valid = place_of(plan, last, 0, seq_index)
+
+    @pl.when(valid)
+    def _():
         for half in range(CORES):
-            place, valid = place_of(plan, plan.groups[-1][0], half, seq_index)
-            rows = slice(half * size, (half + 1) * size)
-
-            @pl.when(valid)
-            def _():
+            place, _ = place_of(plan, last, half, seq_index)
+            for stream, plain, adjust, out, size in (
+                (0, text_plain, text_adjust, text_heads, plan.text_dev),
+                (1, image_plain, image_adjust, image_heads, plan.image_dev),
+            ):
+                rows = slice(half * size, (half + 1) * size)
                 write_heads(
                     plan,
                     lambda lanes: plain[rows, lanes] + adjust[rows, lanes],
                     gain_ref,
                     stream,
-                    text_heads if stream == 0 else image_heads,
+                    out,
                     pl.ds(pl.multiple_of(place * size, size), size),
                 )
 
@@ -626,9 +656,11 @@
     for group in plan.groups:
         plains.append(project(plan, group, blocks_of(group), head_weight))
     scalars = (image_lengths, store_row, user_adapter)
-    before, turned = rank_parts(plan, plan.groups[0], *scalars, downs, blocks_of(plan.groups[0]))
+    before, turned = rank_parts(
+        plan, plan.groups[0], scalars, downs, blocks_of(plan.groups[0])
+    )
     (ranks,) = rank_parts(
-        plan, plan.groups[1], *scalars, [turned, before], blocks_of(plan.groups[1])
+        plan, plan.groups[1], scalars, [turned, before], blocks_of(plan.groups[1])
     )
     ranks = [jnp.stack([ranks, lax.ppermute(ranks, "seq", swap)])]
     for away in range(1, plan.half + 1):
@@ -642,8 +674,7 @@
     arrays = early_heads(
         plan,
         plan.groups[:-1],
-        *scalars,
-        norm_gain,
+        scalars, norm_gain,
         ranks,
         arrived["up"],
         [one for pair in plains[:-1] for one in pair],

time: 101 us -> 98.3 us (0.973)
  Pallas kernels: 24.9 us -> 22.1 us
  local copies, waits for them, and re-layouts: 0.05 us -> 1.36 us
    unnamed x20 -> x16, local copies, waits for them, and re-layouts: 0.05 us -> 1.36 us
    pallas_call x1, Pallas kernels: 3.18 us -> 2.02 us  [packed_adapters(): pl.pallas_call(functools.partial(pack_kernel, plan), out_shape=[jax.Shape...]
  transfers between devices with their start and end apart: 25 -> 25, of which waited for: 9 -> 9; matrix products, arithmetic and copies ran while one was open for 1% -> 0% of each run, Pallas kernels for 15% -> 13%
where the time goes in v3:
time: 98.3 us; the launch traced here: 97.9 us
  waiting for transfers between devices  31.4 us (32%)
  starting transfers between devices  27.1 us (28%)
  Pallas kernels  22.1 us (22%)
  blocking collectives  14.9 us (15%)
  local copies, waits for them, and re-layouts  1.36 us (1%)
    ppermute x6, waiting for transfers between devices, steps(): passing[half] = lax.ppermute(passing[half], 'seq', up + down)  19 us
    all_to_all x1, blocking collectives, steps(): lax.all_to_all(outs, 'seq', split_axis=0, concat_axis=0, tiled=True)  14.9 us
    ppermute x6, starting transfers between devices, steps(): lax.ppermute(sent[hop], 'bag', [(b, b ^ hop) for b in range(bags)])  10 us
    ppermute x1, waiting for transfers between devices, steps(): lax.ppermute(down_own, 'seq', plan.on_cores([(low - hop, low), (high + ho...  8.2 us
    ppermute x6, starting transfers between devices, steps(): passing[half] = lax.ppermute(passing[half], 'seq', up + down)  7.69 us
    pallas_call x3, Pallas kernels, project(): pl.pallas_call(functools.partial(project_kernel, plan, slots), out_shape=...  6.43 us
    pallas_call x2, Pallas kernels, rank_parts(): pl.pallas_call(functools.partial(rank_kernel, plan, slots), out_shape=out...  4.62 us
    ppermute x1, starting transfers between devices, steps(): lax.ppermute(down_own, 'seq', plan.on_cores([(low - hop, low), (high + ho...  4.57 us
  transfers between devices with their start and end apart: 25, of which 9 were waited for; matrix products, arithmetic and copies ran while one was open for 0% of the time, Pallas kernels for 13%

profile of v3, /device:TPU:0, one launch (start us, length us, event | category | flops | bytes accessed | tf_op | source)
XLA Modules:
  0.0 97.9 jit_solution(2350373981963524587)
XLA Ops:
  0.6 3.0 %hidden_rows.1.refs_2_.refs_0_ = bf16[96,3072]{1,0:T(8,128)(2,1)} custom-call(s32[1,4]{1,0:T(1,128)} %lengths_ref.9, bf16[64,3072]{1,0:T(8,128)(2,1)} %text_ref.1, bf16[32,3072]{1,0:T(8,128)(2,1)} %image_ref.1, f32[8,2,2,3072]{3,2,1,0:T(2,128)} %mod_ref.1), custom_call_target="tpu_custom_call" | custom-call | tf_op jit(solution)/shard_map/hidden_rows/pallas_call | solution.py:148
  4.1 1.3 %collective-permute-start.5 = (bf16[96,3072]{1,0:T(8,128)(2,1)}, bf16[96,3072]{1,0:T(8,128)(2,1)S(1)}, u32[]{:S(2)}, u32[]{:S(2)}) collective-permute-start(bf16[96,3072]{1,0:T(8,128)(2,1)} %hidden_rows.1.refs_2_.refs_0_), channel_id=1, source_target_pairs={{1,3},{3,5},{5,7},{2,0},{4,2},{6,4},{9,11},{11,13},{13,15},{10,8},... | collective-permute-start | bytes 1769480 | tf_op jit(solution)/shard_map/ppermute | solution.py:628
  6.0 1.3 %collective-permute-start.6 = (bf16[96,3072]{1,0:T(8,128)(2,1)S(1)}, bf16[96,3072]{1,0:T(8,128)(2,1)S(1)}, u32[]{:S(2)}, u32[]{:S(2)}) collective-permute-start(bf16[96,3072]{1,0:T(8,128)(2,1)S(1)} %collective-permute-done.4.refs_3_.refs_1_), channel_id=1, source_target_pairs={{1,3},{3,5},{5,7},{2,0},{4,2},{6,4},{9,11},{11,13},{13,15},{10,8},... | collective-permute-start | bytes 1769480 | tf_op jit(solution)/shard_map/ppermute | solution.py:628
  8.6 2.0 %packed_adapters.1 = (bf16[64,768]{1,0:T(8,128)(2,1)S(1)}, bf16[64,768]{1,0:T(8,128)(2,1)S(1)}, bf16[64,768]{1,0:T(8,128)(2,1)S(1)}, bf16[64,768]{1,0:T(8,128)(2...) custom-call(s32[128]{0:T(128)S(1)} %copy-done.4, ...), custom_call_target="tpu_custom_call" | custom-call | tf_op jit(solution)/shard_map/packed_adapters/pallas_call | solution.py:192
  10.6 2.9 %collective-permute-start = (bf16[64,768]{1,0:T(8,128)(2,1)S(1)}, bf16[64,768]{1,0:T(8,128)(2,1)S(1)}, u32[]{:S(2)}, u32[]{:S(2)}) collective-permute-start(bf16[64,768]{1,0:T(8,128)(2,1)S(1)} %get-tuple-element.23), channel_id=1, source_target_pairs={{0,8},{8,0},{16,24},{24,16},{1,9},{9,1},{17,25},{25,17},{2,10},{10... | collective-permute-start | bytes 294920 | tf_op jit(solution)/shard_map/ppermute | solution.py:640
  13.5 1.5 %collective-permute-start.1 = (bf16[64,768]{1,0:T(8,128)(2,1)S(1)}, bf16[64,768]{1,0:T(8,128)(2,1)S(1)}, u32[]{:S(2)}, u32[]{:S(2)}) collective-permute-start(bf16[64,768]{1,0:T(8,128)(2,1)S(1)} %get-tuple-element.24), channel_id=1, source_target_pairs={{0,16},{8,24},{16,0},{24,8},{1,17},{9,25},{17,1},{25,9},{2,18},{10... | collective-permute-start | bytes 294920 | tf_op jit(solution)/shard_map/ppermute | solution.py:640
  15.1 1.7 %collective-permute-done.5.refs_4_.refs_2_ = bf16[96,3072]{1,0:T(8,128)(2,1)S(1)} collective-permute-done((bf16[96,3072]{1,0:T(8,128)(2,1)}, bf16[96,3072]{1,0:T(8,128)(2,1)S(1)}, u32[]{:S(2)}, u32[]{:S(2)}) %collective-permute-start.5) | collective-permute-done | bytes 589856 | tf_op jit(solution)/shard_map/ppermute | solution.py:628
  16.8 1.3 %collective-permute-start.9 = (bf16[96,3072]{1,0:T(8,128)(2,1)S(1)}, bf16[96,3072]{1,0:T(8,128)(2,1)S(1)}, u32[]{:S(2)}, u32[]{:S(2)}) collective-permute-start(bf16[96,3072]{1,0:T(8,128)(2,1)S(1)} %collective-permute-done.5.refs_4_.refs_2_), channel_id=1, source_target_pairs={{3,5},{5,7},{2,0},{4,2},{11,13},{13,15},{10,8},{12,10},{19,21},{21... | collective-permute-start | bytes 1769480 | tf_op jit(solution)/shard_map/ppermute | solution.py:628
  18.1 5.0 %collective-permute-done.6.refs_5_.refs_3_ = bf16[96,3072]{1,0:T(8,128)(2,1)S(1)} collective-permute-done((bf16[96,3072]{1,0:T(8,128)(2,1)S(1)}, bf16[96,3072]{1,0:T(8,128)(2,1)S(1)}, u32[]{:S(2)}, u32[]{:S(2)}) %collective-permute-start.6) | collective-permute-done | bytes 589856 | tf_op jit(solution)/shard_map/ppermute | solution.py:628
  23.1 1.3 %collective-permute-start.11 = (bf16[96,3072]{1,0:T(8,128)(2,1)S(1)}, bf16[96,3072]{1,0:T(8,128)(2,1)S(1)}, u32[]{:S(2)}, u32[]{:S(2)}) collective-permute-start(bf16[96,3072]{1,0:T(8,128)(2,1)S(1)} %collective-permute-done.6.refs_5_.refs_3_), channel_id=1, source_target_pairs={{3,5},{5,7},{2,0},{4,2},{11,13},{13,15},{10,8},{12,10},{19,21},{21... | collective-permute-start | bytes 1769480 | tf_op jit(solution)/shard_map/ppermute | solution.py:628
  24.4 4.6 %collective-permute-start.3 = (bf16[4,64,768]{2,1,0:T(8,128)(2,1)S(1)}, bf16[4,64,768]{2,1,0:T(8,128)(2,1)S(1)}, u32[]{:S(2)}, u32[]{:S(2)}) collective-permute-start(bf16[4,64,768]{2,1,0:T(8,128)(2,1)S(1)} %pad_maximum_fusion.refs_0_), channel_id=1, source_target_pairs={{0,2},{1,3},{6,4},{7,5},{8,10},{9,11},{14,12},{15,13},{16,18},{17,... | collective-permute-start | bytes 1179656 | tf_op jit(solution)/shard_map/ppermute | solution.py:647
  30.2 8.2 %collective-permute-done.3.refs_1_ = bf16[4,64,768]{2,1,0:T(8,128)(2,1)S(1)} collective-permute-done((bf16[4,64,768]{2,1,0:T(8,128)(2,1)S(1)}, bf16[4,64,768]{2,1,0:T(8,128)(2,1)S(1)}, u32[]{:S(2)}, u32[]{:S(2)}) %collective-permute-start.3) | collective-permute-done | bytes 393248 | tf_op jit(solution)/shard_map/ppermute | solution.py:647
  38.4 1.3 %collective-permute-start.21 = (bf16[96,3072]{1,0:T(8,128)(2,1)S(1)}, bf16[96,3072]{1,0:T(8,128)(2,1)S(1)}, u32[]{:S(2)}, u32[]{:S(2)}) collective-permute-start(bf16[96,3072]{1,0:T(8,128)(2,1)S(1)} %collective-permute-done.9.refs_2_.refs_0_), channel_id=1, source_target_pairs={{5,7},{2,0},{13,15},{10,8},{21,23},{18,16},{29,31},{26,24}} | collective-permute-start | bytes 1769480 | tf_op jit(solution)/shard_map/ppermute | solution.py:628
  39.7 1.3 %collective-permute-start.23 = (bf16[96,3072]{1,0:T(8,128)(2,1)S(1)}, bf16[96,3072]{1,0:T(8,128)(2,1)S(1)}, u32[]{:S(2)}, u32[]{:S(2)}) collective-permute-start(bf16[96,3072]{1,0:T(8,128)(2,1)S(1)} %collective-permute-done.11.refs_4_.refs_2_), channel_id=1, source_target_pairs={{5,7},{2,0},{13,15},{10,8},{21,23},{18,16},{29,31},{26,24}} | collective-permute-start | bytes 1769480 | tf_op jit(solution)/shard_map/ppermute | solution.py:628
  41.0 1.6 %collective-permute-start.18 = (bf16[128,768]{1,0:T(8,128)(2,1)S(1)}, bf16[128,768]{1,0:T(8,128)(2,1)S(1)}, u32[]{:S(2)}, u32[]{:S(2)}) collective-permute-start(bf16[128,768]{1,0:T(8,128)(2,1)S(1)} %get-tuple-element.29), channel_id=1, source_target_pairs={{0,8},{8,0},{16,24},{24,16},{1,9},{9,1},{17,25},{25,17},{2,10},{10... | collective-permute-start | bytes 589832 | tf_op jit(solution)/shard_map/ppermute | solution.py:640
  42.5 1.6 %collective-permute-start.19 = (bf16[128,768]{1,0:T(8,128)(2,1)S(1)}, bf16[128,768]{1,0:T(8,128)(2,1)S(1)}, u32[]{:S(2)}, u32[]{:S(2)}) collective-permute-start(bf16[128,768]{1,0:T(8,128)(2,1)S(1)} %get-tuple-element.30), channel_id=1, source_target_pairs={{0,16},{8,24},{16,0},{24,8},{1,17},{9,25},{17,1},{25,9},{2,18},{10... | collective-permute-start | bytes 589832 | tf_op jit(solution)/shard_map/ppermute | solution.py:640
  44.1 6.0 %collective-permute-done.21.refs_0_ = bf16[96,3072]{1,0:T(8,128)(2,1)S(1)} collective-permute-done((bf16[96,3072]{1,0:T(8,128)(2,1)S(1)}, bf16[96,3072]{1,0:T(8,128)(2,1)S(1)}, u32[]{:S(2)}, u32[]{:S(2)}) %collective-permute-start.21) | collective-permute-done | bytes 589856 | tf_op jit(solution)/shard_map/ppermute | solution.py:628
  50.1 6.3 %collective-permute-done.23.refs_2_ = bf16[96,3072]{1,0:T(8,128)(2,1)S(1)} collective-permute-done((bf16[96,3072]{1,0:T(8,128)(2,1)S(1)}, bf16[96,3072]{1,0:T(8,128)(2,1)S(1)}, u32[]{:S(2)}, u32[]{:S(2)}) %collective-permute-start.23) | collective-permute-done | bytes 589856 | tf_op jit(solution)/shard_map/ppermute | solution.py:628
  56.5 3.3 %rank_parts.2 = (bf16[2,8,8,128]{3,2,1,0:T(8,128)(2,1)S(1)}, bf16[3072,128]{1,0:T(8,128)(2,1)S(1)}) custom-call(s32[1,4]{1,0:T(1,128)S(1)} %copy-done.3, s32[128]{0:T(128)S(1)} %copy-done.4, s32[4,4]{1,0:T(4,128)S(1)} %copy-done.1, bf16[4,64,768]{2,1,0:T(8,128)(2,1)S(1)} %pad_maximum_fusion.refs_0_, bf16[4,64,768]{2,1,0:T(8,128)(2,1)S(1)} %collective-permute-done.3.refs_1_, ...), custom_call_target="tpu_custom_call" | custom-call | flops 14495514624 | bytes 3538944 | tf_op jit(solution)/shard_map/rank_parts/pallas_call | solution.py:331
  59.7 1.4 %rank_parts.3 = bf16[2,8,8,128]{3,2,1,0:T(8,128)(2,1)S(1)} custom-call(s32[1,4]{1,0:T(1,128)S(1)} %copy-done.3, s32[128]{0:T(128)S(1)} %copy-done.4, s32[4,4]{1,0:T(4,128)S(1)} %copy-done.1, bf16[3072,128]{1,0:T(8,128)(2,1)S(1)} %get-tuple-element.26.refs_0_, bf16[2,8,8,128]{3,2,1,0:T(8,128)(2,1)S(1)} %get-tuple-element.27.refs_1_, ...), custom_call_target="tpu_custom_call" | custom-call | flops 75497472 | bytes 1179648 | tf_op jit(solution)/shard_map/rank_parts/pallas_call | solution.py:331
  61.6 0.9 collective-permute-done.13
  62.5 2.5 %collective-permute-start.20 = (bf16[128,768]{1,0:T(8,128)(2,1)S(1)}, bf16[128,768]{1,0:T(8,128)(2,1)S(1)}, u32[]{:S(2)}, u32[]{:S(2)}) collective-permute-start(bf16[128,768]{1,0:T(8,128)(2,1)S(1)} %get-tuple-element.31), channel_id=1, source_target_pairs={{0,24},{8,16},{16,8},{24,0},{1,25},{9,17},{17,9},{25,1},{2,26},{10... | collective-permute-start | bytes 589832 | tf_op jit(solution)/shard_map/ppermute | solution.py:640
  65.0 1.3 %collective-permute-start.14 = (bf16[2,2,8,8,128]{4,3,2,1,0:T(8,128)(2,1)S(1)}, bf16[2,2,8,8,128]{4,3,2,1,0:T(8,128)(2,1)S(1)}, u32[]{:S(2)}, u32[]{:S(2)}) collective-permute-start(bf16[2,2,8,8,128]{4,3,2,1,0:T(8,128)(2,1)S(1)} %pad_maximum_fusion.1.refs_0_), channel_id=1, source_target_pairs={{3,5},{2,0},{5,7},{4,2},{11,13},{10,8},{13,15},{12,10},{19,21},{18... | collective-permute-start | bytes 196616 | tf_op jit(solution)/shard_map/ppermute | solution.py:671
  66.3 1.3 %collective-permute-start.15 = (bf16[2,2,8,8,128]{4,3,2,1,0:T(8,128)(2,1)S(1)}, bf16[2,2,8,8,128]{4,3,2,1,0:T(8,128)(2,1)S(1)}, u32[]{:S(2)}, u32[]{:S(2)}) collective-permute-start(bf16[2,2,8,8,128]{4,3,2,1,0:T(8,128)(2,1)S(1)} %pad_maximum_fusion.1.refs_0_), channel_id=1, source_target_pairs={{3,7},{4,0},{11,15},{12,8},{19,23},{20,16},{27,31},{28,24}} | collective-permute-start | bytes 196616 | tf_op jit(solution)/shard_map/ppermute | solution.py:671
  67.6 3.0 %shard_map.113 = (f32[384,768]{1,0:T(8,128)S(1)}, f32[192,768]{1,0:T(8,128)S(1)}) custom-call(bf16[96,3072]{1,0:T(8,128)(2,1)S(1)} %copy-done, bf16[96,3072]{1,0:T(8,128)(2,1)S(1)} %collective-permute-done.4.refs_3_.refs_1_, bf16[96,3072]{1,0:T(8,128)(2,1)S(1)} %collective-permute-done.5.refs_4_.refs_2_, ...), custom_call_target="tpu_custom_call" | custom-call | flops 2717908992 | bytes 3538944 | tf_op jit(solution)/shard_map/pallas_call | solution.py:246
  71.1 2.2 %collective-permute-done.15.refs_2_ = bf16[2,2,8,8,128]{4,3,2,1,0:T(8,128)(2,1)S(1)} collective-permute-done((bf16[2,2,8,8,128]{4,3,2,1,0:T(8,128)(2,1)S(1)}, bf16[2,2,8,8,128]{4,3,2,1,0:T(8,128)(2,1)S(1)}, u32[]{:S(2)}, u32[]{:S(2)}) %collective-permute-start.15) | collective-permute-done | bytes 65568 | tf_op jit(solution)/shard_map/ppermute | solution.py:671
  73.3 1.6 %shard_map.114 = (f32[128,768]{1,0:T(8,128)S(1)}, f32[64,768]{1,0:T(8,128)S(1)}) custom-call(bf16[96,3072]{1,0:T(8,128)(2,1)S(1)} %collective-permute-done.9.refs_2_.refs_0_, bf16[96,3072]{1,0:T(8,128)(2,1)S(1)} %collective-permute-done.10.refs_3_.refs_1_, bf16[96,3072]{1,0:T(8,128)(2,1)S(1)} %collective-permute-done.11.refs_4_.refs_2_, ...), custom_call_target="tpu_custom_call" | custom-call | flops 905969664 | bytes 1179648 | tf_op jit(solution)/shard_map/pallas_call | solution.py:246
  75.0 1.9 %early_heads.1 = (bf16[3,512,256]{2,1,0:T(8,128)(2,1)S(1)}, bf16[3,256,256]{2,1,0:T(8,128)(2,1)S(1)}, f32[128,768]{1,0:T(8,128)S(1)}, f32[64,768]{1,0:T(8,128)S(1)}) custom-call(s32[1,4]{1,0:T(1,128)S(1)} %copy-done.3, s32[128]{0:T(128)S(1)} %copy-done.4, s32[4,4]{1,0:T(4,128)S(1)} %copy-done.1, f32[2,2,128]{2,1,0:T(2,128)S(1)} %copy-done.2, ...), custom_call_target="tpu_custom_call" | custom-call | flops 805306368 | bytes 4718592 | tf_op jit(solution)/shard_map/early_heads/pallas_call | solution.py:452
  77.0 1.8 %shard_map.115 = (f32[128,768]{1,0:T(8,128)S(1)}, f32[64,768]{1,0:T(8,128)S(1)}) custom-call(bf16[96,3072]{1,0:T(8,128)(2,1)S(1)} %collective-permute-done.21.refs_0_, bf16[96,3072]{1,0:T(8,128)(2,1)S(1)} %collective-permute-done.22.refs_1_, bf16[96,3072]{1,0:T(8,128)(2,1)S(1)} %collective-permute-done.23.refs_2_, ...), custom_call_target="tpu_custom_call" | custom-call | flops 905969664 | bytes 1179648 | tf_op jit(solution)/shard_map/pallas_call | solution.py:246
  78.8 3.4 %attention.1 = bf16[8,96,256]{2,1,0:T(8,128)(2,1)S(1)} custom-call(s32[1,4]{1,0:T(1,128)S(1)} %copy-done.3, f32[2,2,128]{2,1,0:T(2,128)S(1)} %copy-done.2, bf16[3,512,256]{2,1,0:T(8,128)(2,1)S(1)} %get-tuple-element.36.refs_0_, bf16[3,256,256]{2,1,0:T(8,128)(2,1)S(1)} %get-tuple-element.37.refs_1_, f32[128,768]{1,0:T(8,128)S(1)} %get-tuple-element.38.refs_2_, ...), custom_call_target="tpu_custom_call" | custom-call | tf_op jit(solution)/shard_map/attention/pallas_call | solution.py:559
  82.2 14.9 %all_to_all.5.pieces = bf16[8,96,256]{2,1,0:T(8,128)(2,1)S(1)} all-to-all(bf16[8,96,256]{2,1,0:T(8,128)(2,1)S(1)} %attention.1), channel_id=1, replica_groups=mesh['bag'=4,'seq'=8] {'seq'}, dimensions={0} | all-to-all | bytes 786432 | tf_op jit(solution)/shard_map/all_to_all | solution.py:685
  97.1 0.8 placed.1
  (48 shorter events, 4.8 us)
Async XLA Ops:
  0.6 55.8 %copy-start.3 = (s32[1,4]{1,0:T(1,128)S(1)}, s32[1,4]{1,0:T(1,128)}, u32[]{:S(2)}) copy-start(s32[1,4]{1,0:T(1,128)} %lengths_ref.9) | copy-start | bytes 52
  3.6 52.8 %copy-start = (bf16[96,3072]{1,0:T(8,128)(2,1)S(1)}, bf16[96,3072]{1,0:T(8,128)(2,1)}, u32[]{:S(2)}) copy-start(bf16[96,3072]{1,0:T(8,128)(2,1)} %hidden_rows.1.refs_2_.refs_0_) | copy-start | bytes 1769476
  3.6 2.3 %collective-permute-start.4 = (bf16[96,3072]{1,0:T(8,128)(2,1)}, bf16[96,3072]{1,0:T(8,128)(2,1)S(1)}, u32[]{:S(2)}, u32[]{:S(2)}) collective-permute-start(bf16[96,3072]{1,0:T(8,128)(2,1)} %hidden_rows.1.refs_2_.refs_0_), channel_id=1, source_target_pairs={{0,1},{1,0},{2,3},{3,2},{4,5},{5,4},{6,7},{7,6},{8,9},{9,8},{10,11... | collective-permute-start | bytes 1769480 | tf_op jit(solution)/shard_map/ppermute | solution.py:622
  4.1 12.7 %collective-permute-start.5 = (bf16[96,3072]{1,0:T(8,128)(2,1)}, bf16[96,3072]{1,0:T(8,128)(2,1)S(1)}, u32[]{:S(2)}, u32[]{:S(2)}) collective-permute-start(bf16[96,3072]{1,0:T(8,128)(2,1)} %hidden_rows.1.refs_2_.refs_0_), channel_id=1, source_target_pairs={{1,3},{3,5},{5,7},{2,0},{4,2},{6,4},{9,11},{11,13},{13,15},{10,8},... | collective-permute-start | bytes 1769480 | tf_op jit(solution)/shard_map/ppermute | solution.py:628
  6.0 17.1 %collective-permute-start.6 = (bf16[96,3072]{1,0:T(8,128)(2,1)S(1)}, bf16[96,3072]{1,0:T(8,128)(2,1)S(1)}, u32[]{:S(2)}, u32[]{:S(2)}) collective-permute-start(bf16[96,3072]{1,0:T(8,128)(2,1)S(1)} %collective-permute-done.4.refs_3_.refs_1_), channel_id=1, source_target_pairs={{1,3},{3,5},{5,7},{2,0},{4,2},{6,4},{9,11},{11,13},{13,15},{10,8},... | collective-permute-start | bytes 1769480 | tf_op jit(solution)/shard_map/ppermute | solution.py:628
  7.2 0.7 copy-start.1
  10.6 13.8 %collective-permute-start = (bf16[64,768]{1,0:T(8,128)(2,1)S(1)}, bf16[64,768]{1,0:T(8,128)(2,1)S(1)}, u32[]{:S(2)}, u32[]{:S(2)}) collective-permute-start(bf16[64,768]{1,0:T(8,128)(2,1)S(1)} %get-tuple-element.23), channel_id=1, source_target_pairs={{0,8},{8,0},{16,24},{24,16},{1,9},{9,1},{17,25},{25,17},{2,10},{10... | collective-permute-start | bytes 294920 | tf_op jit(solution)/shard_map/ppermute | solution.py:640
  13.5 10.9 %collective-permute-start.1 = (bf16[64,768]{1,0:T(8,128)(2,1)S(1)}, bf16[64,768]{1,0:T(8,128)(2,1)S(1)}, u32[]{:S(2)}, u32[]{:S(2)}) collective-permute-start(bf16[64,768]{1,0:T(8,128)(2,1)S(1)} %get-tuple-element.24), channel_id=1, source_target_pairs={{0,16},{8,24},{16,0},{24,8},{1,17},{9,25},{17,1},{25,9},{2,18},{10... | collective-permute-start | bytes 294920 | tf_op jit(solution)/shard_map/ppermute | solution.py:640
  15.0 9.4 %collective-permute-start.2 = (bf16[64,768]{1,0:T(8,128)(2,1)S(1)}, bf16[64,768]{1,0:T(8,128)(2,1)S(1)}, u32[]{:S(2)}, u32[]{:S(2)}) collective-permute-start(bf16[64,768]{1,0:T(8,128)(2,1)S(1)} %get-tuple-element.25), channel_id=1, source_target_pairs={{0,24},{8,16},{16,8},{24,0},{1,25},{9,17},{17,9},{25,1},{2,26},{10... | collective-permute-start | bytes 294920 | tf_op jit(solution)/shard_map/ppermute | solution.py:640
  16.8 13.0 %collective-permute-start.9 = (bf16[96,3072]{1,0:T(8,128)(2,1)S(1)}, bf16[96,3072]{1,0:T(8,128)(2,1)S(1)}, u32[]{:S(2)}, u32[]{:S(2)}) collective-permute-start(bf16[96,3072]{1,0:T(8,128)(2,1)S(1)} %collective-permute-done.5.refs_4_.refs_2_), channel_id=1, source_target_pairs={{3,5},{5,7},{2,0},{4,2},{11,13},{13,15},{10,8},{12,10},{19,21},{21... | collective-permute-start | bytes 1769480 | tf_op jit(solution)/shard_map/ppermute | solution.py:628
  23.1 16.6 %collective-permute-start.11 = (bf16[96,3072]{1,0:T(8,128)(2,1)S(1)}, bf16[96,3072]{1,0:T(8,128)(2,1)S(1)}, u32[]{:S(2)}, u32[]{:S(2)}) collective-permute-start(bf16[96,3072]{1,0:T(8,128)(2,1)S(1)} %collective-permute-done.6.refs_5_.refs_3_), channel_id=1, source_target_pairs={{3,5},{5,7},{2,0},{4,2},{11,13},{13,15},{10,8},{12,10},{19,21},{21... | collective-permute-start | bytes 1769480 | tf_op jit(solution)/shard_map/ppermute | solution.py:628
  24.4 13.9 %collective-permute-start.3 = (bf16[4,64,768]{2,1,0:T(8,128)(2,1)S(1)}, bf16[4,64,768]{2,1,0:T(8,128)(2,1)S(1)}, u32[]{:S(2)}, u32[]{:S(2)}) collective-permute-start(bf16[4,64,768]{2,1,0:T(8,128)(2,1)S(1)} %pad_maximum_fusion.refs_0_), channel_id=1, source_target_pairs={{0,2},{1,3},{6,4},{7,5},{8,10},{9,11},{14,12},{15,13},{16,18},{17,... | collective-permute-start | bytes 1179656 | tf_op jit(solution)/shard_map/ppermute | solution.py:647
  29.0 11.9 %collective-permute-start.7 = (bf16[96,3072]{1,0:T(8,128)(2,1)S(1)}, bf16[96,3072]{1,0:T(8,128)(2,1)S(1)}, u32[]{:S(2)}, u32[]{:S(2)}) collective-permute-start(bf16[96,3072]{1,0:T(8,128)(2,1)S(1)} %collective-permute-done.5.refs_4_.refs_2_), channel_id=1, source_target_pairs={{0,1},{1,0},{2,3},{3,2},{4,5},{5,4},{6,7},{7,6},{8,9},{9,8},{10,11... | collective-permute-start | bytes 1769480 | tf_op jit(solution)/shard_map/ppermute | solution.py:629
  29.6 12.9 %collective-permute-start.8 = (bf16[96,3072]{1,0:T(8,128)(2,1)S(1)}, bf16[96,3072]{1,0:T(8,128)(2,1)S(1)}, u32[]{:S(2)}, u32[]{:S(2)}) collective-permute-start(bf16[96,3072]{1,0:T(8,128)(2,1)S(1)} %collective-permute-done.6.refs_5_.refs_3_), channel_id=1, source_target_pairs={{0,1},{1,0},{2,3},{3,2},{4,5},{5,4},{6,7},{7,6},{8,9},{9,8},{10,11... | collective-permute-start | bytes 1769480 | tf_op jit(solution)/shard_map/ppermute | solution.py:629
  29.7 14.4 %collective-permute-start.10 = (bf16[96,3072]{1,0:T(8,128)(2,1)S(1)}, bf16[96,3072]{1,0:T(8,128)(2,1)S(1)}, u32[]{:S(2)}, u32[]{:S(2)}) collective-permute-start(bf16[96,3072]{1,0:T(8,128)(2,1)S(1)} %collective-permute-done.9.refs_2_.refs_0_), channel_id=1, source_target_pairs={{0,1},{1,0},{2,3},{3,2},{4,5},{5,4},{6,7},{7,6},{8,9},{9,8},{10,11... | collective-permute-start | bytes 1769480 | tf_op jit(solution)/shard_map/ppermute | solution.py:629
  38.4 11.8 %collective-permute-start.21 = (bf16[96,3072]{1,0:T(8,128)(2,1)S(1)}, bf16[96,3072]{1,0:T(8,128)(2,1)S(1)}, u32[]{:S(2)}, u32[]{:S(2)}) collective-permute-start(bf16[96,3072]{1,0:T(8,128)(2,1)S(1)} %collective-permute-done.9.refs_2_.refs_0_), channel_id=1, source_target_pairs={{5,7},{2,0},{13,15},{10,8},{21,23},{18,16},{29,31},{26,24}} | collective-permute-start | bytes 1769480 | tf_op jit(solution)/shard_map/ppermute | solution.py:628
  39.7 16.8 %collective-permute-start.23 = (bf16[96,3072]{1,0:T(8,128)(2,1)S(1)}, bf16[96,3072]{1,0:T(8,128)(2,1)S(1)}, u32[]{:S(2)}, u32[]{:S(2)}) collective-permute-start(bf16[96,3072]{1,0:T(8,128)(2,1)S(1)} %collective-permute-done.11.refs_4_.refs_2_), channel_id=1, source_target_pairs={{5,7},{2,0},{13,15},{10,8},{21,23},{18,16},{29,31},{26,24}} | collective-permute-start | bytes 1769480 | tf_op jit(solution)/shard_map/ppermute | solution.py:628
  41.0 24.0 %collective-permute-start.18 = (bf16[128,768]{1,0:T(8,128)(2,1)S(1)}, bf16[128,768]{1,0:T(8,128)(2,1)S(1)}, u32[]{:S(2)}, u32[]{:S(2)}) collective-permute-start(bf16[128,768]{1,0:T(8,128)(2,1)S(1)} %get-tuple-element.29), channel_id=1, source_target_pairs={{0,8},{8,0},{16,24},{24,16},{1,9},{9,1},{17,25},{25,17},{2,10},{10... | collective-permute-start | bytes 589832 | tf_op jit(solution)/shard_map/ppermute | solution.py:640
  42.5 25.1 %slice-start = ((s8[9437184]{0:T(1024)(128)(4,1)}), s8[4194304]{0:T(1024)(128)(4,1)S(1)}, s32[]{:S(2)}) async-start(s8[9437184]{0:T(1024)(128)(4,1)} %bitcast.6), calls=%async_computation.1 | async-start | bytes 8388608
  42.5 25.1 %slice-start.1 = ((s8[9437184]{0:T(1024)(128)(4,1)}), s8[4194304]{0:T(1024)(128)(4,1)S(1)}, s32[]{:S(2)}) async-start(s8[9437184]{0:T(1024)(128)(4,1)} %bitcast.6), calls=%async_computation.2 | async-start | bytes 8388608
  42.5 25.1 %slice-start.2 = ((s8[9437184]{0:T(1024)(128)(4,1)}), s8[1048576]{0:T(1024)(128)(4,1)S(1)}, s32[]{:S(2)}) async-start(s8[9437184]{0:T(1024)(128)(4,1)} %bitcast.6), calls=%async_computation.3 | async-start | bytes 2097152
  42.5 23.7 %collective-permute-start.19 = (bf16[128,768]{1,0:T(8,128)(2,1)S(1)}, bf16[128,768]{1,0:T(8,128)(2,1)S(1)}, u32[]{:S(2)}, u32[]{:S(2)}) collective-permute-start(bf16[128,768]{1,0:T(8,128)(2,1)S(1)} %get-tuple-element.30), channel_id=1, source_target_pairs={{0,16},{8,24},{16,0},{24,8},{1,17},{9,25},{17,1},{25,9},{2,18},{10... | collective-permute-start | bytes 589832 | tf_op jit(solution)/shard_map/ppermute | solution.py:640
  44.1 15.6 %collective-permute-start.12 = (bf16[96,3072]{1,0:T(8,128)(2,1)S(1)}, bf16[96,3072]{1,0:T(8,128)(2,1)S(1)}, u32[]{:S(2)}, u32[]{:S(2)}) collective-permute-start(bf16[96,3072]{1,0:T(8,128)(2,1)S(1)} %collective-permute-done.11.refs_4_.refs_2_), channel_id=1, source_target_pairs={{0,1},{1,0},{2,3},{3,2},{4,5},{5,4},{6,7},{7,6},{8,9},{9,8},{10,11... | collective-permute-start | bytes 1769480 | tf_op jit(solution)/shard_map/ppermute | solution.py:629
  50.1 26.8 %collective-permute-start.22 = (bf16[96,3072]{1,0:T(8,128)(2,1)S(1)}, bf16[96,3072]{1,0:T(8,128)(2,1)S(1)}, u32[]{:S(2)}, u32[]{:S(2)}) collective-permute-start(bf16[96,3072]{1,0:T(8,128)(2,1)S(1)} %collective-permute-done.21.refs_0_), channel_id=1, source_target_pairs={{0,1},{1,0},{2,3},{3,2},{4,5},{5,4},{6,7},{7,6},{8,9},{9,8},{10,11... | collective-permute-start | bytes 1769480 | tf_op jit(solution)/shard_map/ppermute | solution.py:629
  56.4 20.5 %collective-permute-start.24 = (bf16[96,3072]{1,0:T(8,128)(2,1)S(1)}, bf16[96,3072]{1,0:T(8,128)(2,1)S(1)}, u32[]{:S(2)}, u32[]{:S(2)}) collective-permute-start(bf16[96,3072]{1,0:T(8,128)(2,1)S(1)} %collective-permute-done.23.refs_2_), channel_id=1, source_target_pairs={{0,1},{1,0},{2,3},{3,2},{4,5},{5,4},{6,7},{7,6},{8,9},{9,8},{10,11... | collective-permute-start | bytes 1769480 | tf_op jit(solution)/shard_map/ppermute | solution.py:629
  61.1 1.4 %collective-permute-start.13 = (bf16[2,8,8,128]{3,2,1,0:T(8,128)(2,1)S(1)}, bf16[2,8,8,128]{3,2,1,0:T(8,128)(2,1)S(1)}, u32[]{:S(2)}, u32[]{:S(2)}) collective-permute-start(bf16[2,8,8,128]{3,2,1,0:T(8,128)(2,1)S(1)} %rank_parts.3), channel_id=1, source_target_pairs={{0,1},{1,0},{2,3},{3,2},{4,5},{5,4},{6,7},{7,6},{8,9},{9,8},{10,11... | collective-permute-start | bytes 98312 | tf_op jit(solution)/shard_map/ppermute | solution.py:665
  62.5 12.5 %collective-permute-start.20 = (bf16[128,768]{1,0:T(8,128)(2,1)S(1)}, bf16[128,768]{1,0:T(8,128)(2,1)S(1)}, u32[]{:S(2)}, u32[]{:S(2)}) collective-permute-start(bf16[128,768]{1,0:T(8,128)(2,1)S(1)} %get-tuple-element.31), channel_id=1, source_target_pairs={{0,24},{8,16},{16,8},{24,0},{1,25},{9,17},{17,9},{25,1},{2,26},{10... | collective-permute-start | bytes 589832 | tf_op jit(solution)/shard_map/ppermute | solution.py:640
  65.0 6.2 %collective-permute-start.14 = (bf16[2,2,8,8,128]{4,3,2,1,0:T(8,128)(2,1)S(1)}, bf16[2,2,8,8,128]{4,3,2,1,0:T(8,128)(2,1)S(1)}, u32[]{:S(2)}, u32[]{:S(2)}) collective-permute-start(bf16[2,2,8,8,128]{4,3,2,1,0:T(8,128)(2,1)S(1)} %pad_maximum_fusion.1.refs_0_), channel_id=1, source_target_pairs={{3,5},{2,0},{5,7},{4,2},{11,13},{10,8},{13,15},{12,10},{19,21},{18... | collective-permute-start | bytes 196616 | tf_op jit(solution)/shard_map/ppermute | solution.py:671
  66.3 7.1 %collective-permute-start.15 = (bf16[2,2,8,8,128]{4,3,2,1,0:T(8,128)(2,1)S(1)}, bf16[2,2,8,8,128]{4,3,2,1,0:T(8,128)(2,1)S(1)}, u32[]{:S(2)}, u32[]{:S(2)}) collective-permute-start(bf16[2,2,8,8,128]{4,3,2,1,0:T(8,128)(2,1)S(1)} %pad_maximum_fusion.1.refs_0_), channel_id=1, source_target_pairs={{3,7},{4,0},{11,15},{12,8},{19,23},{20,16},{27,31},{28,24}} | collective-permute-start | bytes 196616 | tf_op jit(solution)/shard_map/ppermute | solution.py:671
  70.6 4.4 %copy-start.2 = (f32[2,2,128]{2,1,0:T(2,128)S(1)}, f32[2,2,128]{2,1,0:T(2,128)}, u32[]{:S(2)}) copy-start(f32[2,2,128]{2,1,0:T(2,128)} %gain_ref.3) | copy-start | bytes 6148
  71.1 3.9 %collective-permute-start.16 = (bf16[2,2,8,8,128]{4,3,2,1,0:T(8,128)(2,1)S(1)}, bf16[2,2,8,8,128]{4,3,2,1,0:T(8,128)(2,1)S(1)}, u32[]{:S(2)}, u32[]{:S(2)}) collective-permute-start(bf16[2,2,8,8,128]{4,3,2,1,0:T(8,128)(2,1)S(1)} %collective-permute-done.14.refs_1_), channel_id=1, source_target_pairs={{0,1},{1,0},{2,3},{3,2},{4,5},{5,4},{6,7},{7,6},{8,9},{9,8},{10,11... | collective-permute-start | bytes 196616 | tf_op jit(solution)/shard_map/ppermute | solution.py:672
  73.3 1.7 %collective-permute-start.17 = (bf16[2,2,8,8,128]{4,3,2,1,0:T(8,128)(2,1)S(1)}, bf16[2,2,8,8,128]{4,3,2,1,0:T(8,128)(2,1)S(1)}, u32[]{:S(2)}, u32[]{:S(2)}) collective-permute-start(bf16[2,2,8,8,128]{4,3,2,1,0:T(8,128)(2,1)S(1)} %collective-permute-done.15.refs_2_), channel_id=1, source_target_pairs={{0,1},{1,0},{2,3},{3,2},{4,5},{5,4},{6,7},{7,6},{8,9},{9,8},{10,11... | collective-permute-start | bytes 196616 | tf_op jit(solution)/shard_map/ppermute | solution.py:672
  (1 other events, 0.7 us)
